TPU v7x, 32 devices: a whole 2x2x4 slice. The times are simulated.
32 devices in a mesh: stn: 2 (over x), vox: 16 (over z, y, core).
Axes of the slice: x: 2, y: 2, z: 4, core: 2. Of those that a mesh axis runs over, the one named last changes fastest.
Arguments:
- voltages: bfloat16 [56, 2, 65536], P('stn', None, 'vox'), may hold values from -6 to 6
- sample_delays: int32 [56, 65536], P(None, 'vox'), may hold values from 0 to 239
- timing_offsets: int32 [56], replicated, may hold values from 0 to 15
- reference_station: int32 [1], replicated, may hold values from 0 to 55
Outputs:
- image_out: float32 [64, 65536], P('stn', 'vox')
All inputs are finite; a program needn't handle non-finite values.
Results may differ from a plain program's by a relative error of at most 0.004.
Values may be sent and summed in bfloat16 or wider, within the bound.
No kernel may reach another device: no remote copies, remote signals or barrier semaphores. Data moves between devices by JAX's collectives and lax.ppermute only.
A program may use at most 64 MiB of HBM per device.

v0:
```python
import math

import jax
import jax.numpy as jnp
from jax import lax
from jax.sharding import PartitionSpec as P

STATIONS = 56
WIN = 1024
LAGS = 256


def spread(value, axis, source):
    kept = jnp.where(lax.axis_index(axis) == source, value, 0).astype(value.dtype)
    return lax.psum(kept, axis)


def padded(block, sides, width):
    for axis, dim in sides:
        count = lax.axis_size(axis)
        forward = [(i, i + 1) for i in range(count - 1)]
        backward = [(target, source) for source, target in forward]
        low = lax.ppermute(
            lax.slice_in_dim(block, block.shape[dim] - width, None, axis=dim), axis, forward
        )
        high = lax.ppermute(lax.slice_in_dim(block, 0, width, axis=dim), axis, backward)
        block = jnp.concatenate([low, block, high], axis=dim)
    return block


def taper_weights(length):
    position = (jnp.arange(length, dtype=jnp.float32) + 0.5) / length
    return 0.5 - 0.5 * jnp.cos(2.0 * math.pi * position)


def shards(voltages, sample_delays, timing_offsets, reference_station):
    stations_here, polarizations, samples_here = voltages.shape
    slices_here = samples_here // WIN
    voxels_here = sample_delays.shape[1]
    station_ref = reference_station[0]
    stn_index = lax.axis_index("stn")
    taper_curve = taper_weights(WIN)
    norm_inv = 1.0 / jnp.sqrt(jnp.sum(taper_curve * taper_curve))
    owner_index = station_ref // stations_here
    ref_local = lax.dynamic_index_in_dim(voltages, station_ref % stations_here, 0, keepdims=False)
    ref_signal = spread(ref_local, "stn", owner_index)
    extended = padded(ref_signal, (("vox", 1),), LAGS // 2)
    extended = jnp.pad(extended, ((0, 0), (0, WIN)))
    leading = extended[:, :samples_here].reshape(polarizations, slices_here, WIN)
    trailing = extended[:, WIN : samples_here + WIN].reshape(polarizations, slices_here, WIN)[
        :, :, : LAGS - 1
    ]
    segments = jnp.concatenate([leading, trailing], axis=2).reshape(
        1, polarizations * slices_here, WIN + LAGS - 1
    )
    windowed = (
        voltages.reshape(stations_here, polarizations, slices_here, WIN) * taper_curve
    ).astype(jnp.bfloat16)
    kernels = jnp.transpose(windowed, (1, 2, 0, 3)).reshape(
        polarizations * slices_here * stations_here, 1, WIN
    )
    lagged_sums = lax.conv_general_dilated(
        segments,
        kernels,
        (1,),
        "VALID",
        feature_group_count=polarizations * slices_here,
        preferred_element_type=jnp.float32,
    )
    lagged_sums = jnp.sum(
        lagged_sums.reshape(polarizations, slices_here, stations_here, LAGS), axis=0
    )
    station_ids = stn_index * stations_here + jnp.arange(stations_here, dtype=jnp.int32)
    keep_mask = (station_ids != station_ref).astype(jnp.float32)
    local_corr = (
        jnp.transpose(lagged_sums, (1, 0, 2)) * keep_mask[:, None, None] * norm_inv
    ).astype(jnp.bfloat16)
    corr_all = lax.all_gather(local_corr, "vox", axis=1, tiled=True)
    lag_index = sample_delays + timing_offsets[:, None]
    total_slices = corr_all.shape[1]
    out_scale = 1.0 / math.sqrt(2.0 * STATIONS)
    my_lags = lax.dynamic_slice_in_dim(lag_index, stn_index * stations_here, stations_here, 0)
    corr_block = lax.slice_in_dim(
        corr_all, 0, lax.axis_size("stn") * (total_slices // lax.axis_size("stn")), axis=1
    )
    lag_grid = lax.broadcasted_iota(jnp.int32, (LAGS, voxels_here), 0)

    def add_station(running, inputs_pair):
        corr_rows, lags_one = inputs_pair
        selector = (lag_grid == lags_one[None, :]).astype(jnp.bfloat16)
        return (running + jnp.dot(corr_rows, selector, preferred_element_type=jnp.float32), None)

    running, unused = lax.scan(
        add_station,
        jnp.zeros(
            (lax.axis_size("stn") * (total_slices // lax.axis_size("stn")), voxels_here),
            jnp.float32,
        ),
        (corr_block, my_lags),
    )
    image_out = lax.psum_scatter(running, "stn", scatter_dimension=0, tiled=True)
    return image_out * out_scale


def solution(mesh):
    return jax.shard_map(
        shards,
        mesh=mesh,
        in_specs=(P("stn", None, "vox"), P(None, "vox"), P(), P()),
        out_specs=P("stn", "vox"),
        check_vma=False,
    )
```

profile of v0, /device:TPU:0, one launch (start us, length us, event | category | flops | bytes accessed | tf_op | source)
XLA Modules:
  0.0 126.3 jit_solution(5938789996437528588)
XLA Ops:
  8.0 9.7 %psum.7 = bf16[2,4096]{1,0:T(2,128)(2,1)S(1)} all-reduce(bf16[2,4096]{1,0:T(2,128)(2,1)S(1)} %fusion.14), channel_id=1, replica_groups=mesh['stn'=2,'vox'=16] {'stn'}, use_global_device_ids=true, to_apply=%region_0.0 | all-reduce | flops 8192 | bytes 32768 | tf_op jit(solution)/shard_map/psum | solution.py:15
  17.6 1.3 %collective-permute-start = (bf16[2,128]{1,0:T(2,128)(2,1)S(1)}, bf16[2,128]{1,0:T(2,128)(2,1)S(1)}, u32[]{:S(2)}, u32[]{:S(2)}) collective-permute-start(bf16[2,128]{1,0:T(2,128)(2,1)S(1)} %get-tuple-element.64), channel_id=1, source_target_pairs={{0,1},{1,2},{2,3},{3,4},{4,5},{5,6},{6,7},{7,8},{8,9},{9,10},{10,1... | collective-permute-start | bytes 1544 | tf_op jit(solution)/shard_map/ppermute | solution.py:23
  18.9 1.3 %collective-permute-start.1 = (bf16[2,128]{1,0:T(2,128)(2,1)S(1)}, bf16[2,128]{1,0:T(2,128)(2,1)S(1)}, u32[]{:S(2)}, u32[]{:S(2)}) collective-permute-start(bf16[2,128]{1,0:T(2,128)(2,1)S(1)} %get-tuple-element.65), channel_id=1, source_target_pairs={{1,0},{2,1},{3,2},{4,3},{5,4},{6,5},{7,6},{8,7},{9,8},{10,9},{11,1... | collective-permute-start | bytes 1544 | tf_op jit(solution)/shard_map/ppermute | solution.py:26
  20.2 1.4 %reshape.40 = f32[28,2,4,1024]{3,2,1,0:T(4,128)S(1)} reshape(bf16[28,2,4096]{2,1,0:T(2,128)(2,1)} %param.6) | data formatting | bytes 1376256 | tf_op jit(solution)/shard_map/convert_element_type | solution.py:57
  25.6 16.9 %fusion.7 = f32[1,224,256]{1,0,2:T(1,128)S(1)} fusion(bf16[1,8,1279]{1,0,2:T(2,128)(2,1)S(1)} %copy.13, s32[224]{0:T(256)S(1)} %copy-done.3, bf16[224,1024]{0,1:T(8,128)(2,1)S(1)} %copy.12), kind=kOutput, calls=%fused_computation.10 | convolution fusion | flops 943194112 | bytes 709488 | tf_op jit(solution)/shard_map/conv_general_dilated | solution.py:62
  42.8 27.5 %all_gather.3 = bf16[28,64,256]{2,0,1:T(8,128)(2,1)S(1)} all-gather(bf16[28,4,256]{2,0,1:T(8,128)(2,1)S(1)} %fusion.13), channel_id=1, replica_groups=mesh['stn'=2,'vox'=16] {'vox'}, dimensions={1}, use_global_device_ids=true | all-gather | bytes 974848 | tf_op jit(solution)/shard_map/all_gather | solution.py:78
  70.9 28.9 %while.11 = (s32[]{:T(128)}, f32[64,4096]{1,0:T(8,128)S(1)}, bf16[28,64,256]{2,1,0:T(8,128)(2,1)S(1)}, s32[28,4096]{1,0:T(8,128)S(1)}, s32[]{:T(128)}, /*index=5*/s32[]{:T(128)}) while((s32[]{:T(128)}, f32[64,4096]{1,0:T(8,128)S(1)}, bf16[28,64,256]{2,1,0:T(8,128)(2,1)S(1)}, s32[28,4096]{1,0:T(8,128)S(1)}, s32[]{:T(128)}, ...), condition=%wide.region_4.5_spmd.clone, body=%wide.region_3.4_spmd.clone.sunk | while | flops 135790592 | bytes 2179159 | solution.py:93
  70.9 1.0 convolution_add_fusion.2
  72.0 1.0 convolution_add_fusion.2
  73.0 1.0 convolution_add_fusion.2
  74.0 1.0 convolution_add_fusion.2
  75.1 1.0 convolution_add_fusion.2
  76.1 1.0 convolution_add_fusion.2
  77.1 1.0 convolution_add_fusion.2
  78.1 1.0 convolution_add_fusion.2
  79.2 1.0 convolution_add_fusion.2
  80.2 1.0 convolution_add_fusion.2
  81.2 1.0 convolution_add_fusion.2
  82.3 1.0 convolution_add_fusion.2
  83.3 1.0 convolution_add_fusion.2
  84.3 1.0 convolution_add_fusion.2
  85.4 1.0 convolution_add_fusion.2
  87.4 1.0 convolution_add_fusion.2
  88.5 1.0 convolution_add_fusion.2
  89.5 1.0 convolution_add_fusion.2
  91.6 1.0 convolution_add_fusion.2
  93.6 1.0 convolution_add_fusion.2
  95.7 1.0 convolution_add_fusion.2
  97.7 1.0 convolution_add_fusion.2
  99.8 1.0 copy-done
  100.8 16.8 %reduce-scatter.2.cloned.1.call-done = f32[32,4096]{1,0:T(8,128)} async-done(((f32[64,4096]{1,0:T(8,128)}), f32[32,4096]{1,0:T(8,128)}) %reduce-scatter.2.cloned.1.call-update) | async-done | bytes 524304 | tf_op jit(solution)/shard_map/reduce_scatter | solution.py:101
  117.6 1.9 %broadcast_multiply_fusion = f32[32,4096]{1,0:T(8,128)} fusion(f32[32,4096]{1,0:T(8,128)} %reduce-scatter.2.cloned.1.call-done), kind=kLoop, calls=%fused_computation.17 | loop fusion | flops 131072 | bytes 1048576 | tf_op jit(solution)/shard_map/mul | solution.py:102
  (68 shorter events, 11.2 us)
Async XLA Ops:
  6.5 111.1 %reduce-scatter.2.cloned.1.call-start = ((), (), s32[]{:S(2)}) async-start(), calls=%async_computation.1 | async-start | bytes 1572864 | tf_op jit(solution)/shard_map/reduce_scatter | solution.py:101
  17.6 6.9 %collective-permute-start = (bf16[2,128]{1,0:T(2,128)(2,1)S(1)}, bf16[2,128]{1,0:T(2,128)(2,1)S(1)}, u32[]{:S(2)}, u32[]{:S(2)}) collective-permute-start(bf16[2,128]{1,0:T(2,128)(2,1)S(1)} %get-tuple-element.64), channel_id=1, source_target_pairs={{0,1},{1,2},{2,3},{3,4},{4,5},{5,6},{6,7},{7,8},{8,9},{9,10},{10,1... | collective-permute-start | bytes 1544 | tf_op jit(solution)/shard_map/ppermute | solution.py:23
  18.9 5.6 %collective-permute-start.1 = (bf16[2,128]{1,0:T(2,128)(2,1)S(1)}, bf16[2,128]{1,0:T(2,128)(2,1)S(1)}, u32[]{:S(2)}, u32[]{:S(2)}) collective-permute-start(bf16[2,128]{1,0:T(2,128)(2,1)S(1)} %get-tuple-element.65), channel_id=1, source_target_pairs={{1,0},{2,1},{3,2},{4,3},{5,4},{6,5},{7,6},{8,7},{9,8},{10,9},{11,1... | collective-permute-start | bytes 1544 | tf_op jit(solution)/shard_map/ppermute | solution.py:26
  21.7 0.7 copy-start.2
  21.7 1.2 copy-start.1
  23.1 2.5 %copy-start.3 = (s32[224]{0:T(256)S(1)}, s32[224]{0:T(256)}, u32[]{:S(2)}) copy-start(s32[224]{0:T(256)} %constant.54.clone.1) | copy-start | bytes 2692
  99.8 1.0 copy-start
Sparse Core Ops, SparseCore 0:
  100.9 16.6 reduce-scatter.1
where the time goes:
time: 127 us; the launch traced here: 126 us
  matrix products  44.3 us (35%)
  blocking collectives  37.2 us (29%)
  waiting for transfers between devices  16.8 us (13%)
  between operations  14.9 us (12%)
  local copies, waits for them, and re-layouts  5.49 us (4%)
  other arithmetic  4.06 us (3%)
  starting transfers between devices  2.58 us (2%)
    all_gather x1, blocking collectives, shards(): corr_all = lax.all_gather(local_corr, 'vox', axis=1, tiled=True)  27.5 us
    dot_general x28, matrix products, add_station(): jnp.dot(corr_rows, selector, preferred_element_type=jnp.float32)  27.4 us
    conv_general_dilated x1, matrix products, shards(): lax.conv_general_dilated(segments, kernels, (1,), 'VALID', feature_group_...  16.9 us
    reduce_scatter x1, waiting for transfers between devices, shards(): lax.psum_scatter(running, 'stn', scatter_dimension=0, tiled=True)  16.8 us
    psum x1, blocking collectives, spread(): return lax.psum(kept, axis)  9.65 us
  transfers between devices with their start and end apart: 3, of which 1 were waited for; matrix products, arithmetic and copies ran while one was open for 2% of the time, Pallas kernels for 0%

commit v1 on v0

v1 whole, which is shorter than its diff:
```python
import functools
import math

import jax
import jax.numpy as jnp
import numpy as np
from jax import lax
from jax.experimental import pallas as pl
from jax.experimental.pallas import tpu as pltpu
from jax.sharding import PartitionSpec as P

STATIONS = 56
WIN = 1024
LAGS = 256
HALF = LAGS // 2
LANES = 128
F8 = jnp.float8_e4m3fn
VMEM = pl.BlockSpec(memory_space=pltpu.VMEM)
SMEM = pl.BlockSpec(memory_space=pltpu.SMEM)


def taper_weights():
    position = (np.arange(WIN, dtype=np.float32) + np.float32(0.5)) / np.float32(WIN)
    return (0.5 - 0.5 * np.cos(2.0 * np.pi * position.astype(np.float64))).astype(np.float32)


def norm_inverse():
    taper = taper_weights()
    return float(np.float32(1.0) / np.sqrt(np.sum(taper * taper, dtype=np.float32)))


def lane_gather(table, index):
    return lax.gather(
        table,
        index[..., None],
        lax.GatherDimensionNumbers(
            offset_dims=(),
            collapsed_slice_dims=(1,),
            start_index_map=(1,),
            operand_batching_dims=(0,),
            start_indices_batching_dims=(0,),
        ),
        slice_sizes=(1, 1),
        mode=lax.GatherScatterMode.PROMISE_IN_BOUNDS,
    )


def corr_kernel(norm, ref_ref, win_ref, ext_ref, out_ref, rev_ref, shift_ref, rows_ref):
    pols, stations, samples = win_ref.shape
    slices = samples // WIN
    blocks = ext_ref.shape[1] // LANES
    pitch = rows_ref.shape[1] // slices
    mirror = LANES - 1 - lax.broadcasted_iota(jnp.int32, (8, LANES), 1)
    for m in range(blocks):
        piece = ext_ref[:, LANES * m : LANES * (m + 1)].astype(jnp.float32)
        piece = jnp.concatenate([piece] * (8 // pols), axis=0)
        at = LANES * (blocks - 1 - m)
        rev_ref[:, at : at + LANES] = lane_gather(piece, mirror)
    for p in range(pols):
        for m in range(blocks - 1):
            pair = jnp.broadcast_to(
                rev_ref[p : p + 1, LANES * m : LANES * (m + 2)], (LANES, 2 * LANES)
            )
            rolled = pltpu.roll(pair, 0, 1, stride=1, stride_axis=0)
            shift_ref[p, :, LANES * (m + 1) : LANES * (m + 2)] = rolled[:, LANES:].astype(
                jnp.bfloat16
            )
    station = lax.broadcasted_iota(jnp.int32, (stations, LAGS), 0)
    mine = ref_ref[0] - lax.axis_index("stn") * stations
    factor = jnp.where(station == mine, 0.0, norm)
    for k in range(slices):
        total = jnp.zeros((stations, LAGS), jnp.float32)
        for p in range(pols):
            for a in range(WIN // LAGS):
                first = WIN * k + LAGS * a
                at = samples - first
                hankel = jnp.concatenate(
                    [shift_ref[p, :, at : at + LAGS], shift_ref[p, :, at - LANES : at + LANES]],
                    axis=0,
                )
                total = total + jnp.dot(
                    win_ref[p, :, first : first + LAGS],
                    hankel,
                    preferred_element_type=jnp.float32,
                )
        total = total * factor
        for h in range(LAGS // LANES):
            rows_ref[h, pitch * k : pitch * k + stations, :] = total[
                :, LANES * h : LANES * (h + 1)
            ]
    for s in range(stations):
        for h in range(LAGS // LANES):
            at = LAGS * s + LANES * h
            out_ref[:, at : at + LANES] = rows_ref[h, pl.ds(s, slices, stride=pitch), :].astype(
                jnp.bfloat16
            )


def correlate(windowed, extended, reference_station):
    pols, stations, samples = windowed.shape
    slices = samples // WIN
    pitch = -(-stations // 8) * 8
    return pl.pallas_call(
        functools.partial(corr_kernel, norm_inverse()),
        out_shape=jax.ShapeDtypeStruct((slices, stations * LAGS), jnp.bfloat16),
        in_specs=[SMEM, VMEM, VMEM],
        out_specs=VMEM,
        scratch_shapes=[
            pltpu.VMEM((8, samples + LAGS), jnp.float32),
            pltpu.VMEM((pols, LANES, samples + LAGS), jnp.bfloat16),
            pltpu.VMEM((LAGS // LANES, pitch * slices, LANES), jnp.float32),
        ],
        cost_estimate=pl.CostEstimate(
            flops=2 * pols * stations * samples * LAGS,
            bytes_accessed=2 * pols * stations * samples,
            transcendentals=0,
        ),
        compiler_params=pltpu.CompilerParams(vmem_limit_bytes=24 << 20),
    )(reference_station, windowed, extended)


def image_kernel(
    swap, offset_ref, corr_ref, delay_ref, *refs
):
    *out_refs, rows_ref, pieces_ref, scale_ref, sums_ref = refs
    groups, slices_each, columns = corr_ref.shape
    total = groups * slices_each
    stations = columns // LAGS
    voxels = delay_ref.shape[1]
    stn = lax.axis_index("stn")
    half = total // 2
    first = stn * (half // slices_each) if swap else 0
    for j in range(groups):
        source = lax.rem(first + j, groups)
        rows_ref[slices_each * j : slices_each * (j + 1), :] = corr_ref[source].astype(jnp.float32)
    chunk = 32
    for r in range(0, total, chunk):
        block = rows_ref[r : r + chunk, :]
        top = jnp.maximum(jnp.max(jnp.abs(block), axis=1, keepdims=True), 1e-36)
        power = jnp.floor(jnp.log2(256.0 / top))
        up = jnp.exp2(power).astype(jnp.bfloat16).astype(jnp.float32)
        down = jnp.exp2(-power).astype(jnp.bfloat16).astype(jnp.float32)
        block = block * up
        coarse = block.astype(F8)
        pieces_ref[r : r + chunk, :] = coarse
        pieces_ref[total + r : total + r + chunk, :] = (
            (block - coarse.astype(jnp.float32)) * 16.0
        ).astype(F8)
        scale_ref[r : r + chunk, :] = jnp.broadcast_to(
            down * (1.0 / math.sqrt(2.0 * STATIONS)), (chunk, LANES)
        )
    level = (lax.broadcasted_iota(jnp.int32, (LAGS, voxels), 0) - HALF).astype(jnp.int8)
    one = jnp.ones((LAGS, voxels), F8)
    zero = jnp.zeros((LAGS, voxels), F8)
    sums = jnp.zeros((2 * total, voxels), jnp.float32)
    for s0 in range(0, stations, 2):
        hots = []
        for s in range(s0, min(s0 + 2, stations)):
            row = stn * stations + s
            where_to = (HALF - 1 - offset_ref[row]) - delay_ref[pl.ds(row, 1), :]
            where_to = jnp.broadcast_to(where_to, (32, voxels)).astype(jnp.int8)[0:1]
            hots.append(jnp.where(level == where_to, one, zero))
        hot = jnp.concatenate(hots, axis=0) if len(hots) > 1 else hots[0]
        sums = sums + jnp.dot(
            pieces_ref[:, LAGS * s0 : LAGS * s0 + hot.shape[0]],
            hot,
            preferred_element_type=jnp.float32,
        )
    sums_ref[...] = sums
    for r in range(0, total, 8):
        value = sums_ref[r : r + 8, :] + sums_ref[total + r : total + r + 8, :] * (1.0 / 16.0)
        value = value * scale_ref[r : r + 8, 0:1]
        if swap and r >= half:
            rows_ref_out = out_refs[1]
            if r % 16 == 0:
                upper = value
            else:
                rows_ref_out[r - half - 8 : r - half + 8, :] = jnp.concatenate(
                    [upper, value], axis=0
                ).astype(jnp.bfloat16)
        else:
            out_refs[0][r : r + 8, :] = value


def image(corr, sample_delays, timing_offsets, swap):
    groups, slices_each, columns = corr.shape
    total = groups * slices_each
    voxels = sample_delays.shape[1]
    if swap:
        out_shape = [
            jax.ShapeDtypeStruct((total // 2, voxels), jnp.float32),
            jax.ShapeDtypeStruct((total // 2, voxels), jnp.bfloat16),
        ]
    else:
        out_shape = [jax.ShapeDtypeStruct((total, voxels), jnp.float32)]
    return pl.pallas_call(
        functools.partial(image_kernel, swap),
        out_shape=out_shape,
        in_specs=[SMEM, VMEM, VMEM],
        out_specs=[VMEM] * len(out_shape),
        scratch_shapes=[
            pltpu.VMEM((total, columns), jnp.float32),
            pltpu.VMEM((2 * total, columns), F8),
            pltpu.VMEM((total, LANES), jnp.float32),
            pltpu.VMEM((2 * total, voxels), jnp.float32),
        ],
        cost_estimate=pl.CostEstimate(
            flops=4 * total * columns * voxels,
            bytes_accessed=4 * total * voxels,
            transcendentals=0,
        ),
        compiler_params=pltpu.CompilerParams(vmem_limit_bytes=56 << 20),
    )(timing_offsets, corr, sample_delays)


def neighbours(block, width):
    count = lax.axis_size("vox")
    forward = [(i, i + 1) for i in range(count - 1)]
    backward = [(target, source) for source, target in forward]
    low = lax.ppermute(block[:, block.shape[1] - width :], "vox", forward)
    high = lax.ppermute(block[:, :width], "vox", backward)
    return jnp.concatenate([low, block, high], axis=1)


def shards(voltages, sample_delays, timing_offsets, reference_station):
    stations_here, pols, samples_here = voltages.shape
    slices_here = samples_here // WIN
    stn_size = lax.axis_size("stn")
    station_ref = reference_station[0]
    owner = station_ref // stations_here
    swap = stn_size == 2

    candidate = lax.dynamic_index_in_dim(voltages, station_ref % stations_here, 0, keepdims=False)
    if swap:
        extended = neighbours(candidate, HALF)
        other = lax.ppermute(extended, "stn", [(0, 1), (1, 0)])
        extended = jnp.where(lax.axis_index("stn") == owner, extended, other)
    else:
        kept = jnp.where(lax.axis_index("stn") == owner, candidate, 0).astype(candidate.dtype)
        extended = neighbours(lax.psum(kept, "stn"), HALF)

    windowed = (
        voltages.reshape(stations_here, pols, slices_here, WIN).astype(jnp.float32)
        * taper_weights()
    ).astype(jnp.bfloat16)
    windowed = jnp.transpose(windowed.reshape(stations_here, pols, samples_here), (1, 0, 2))

    corr = correlate(windowed, extended, reference_station)
    gathered = lax.all_gather(corr, "vox", axis=0, tiled=False)
    if swap:
        kept, sent = image(gathered, sample_delays, timing_offsets, True)
        received = lax.ppermute(sent, "stn", [(0, 1), (1, 0)])
        return kept + received.astype(jnp.float32)
    (partial,) = image(gathered, sample_delays, timing_offsets, False)
    return lax.psum_scatter(partial, "stn", scatter_dimension=0, tiled=True)


def solution(mesh):
    return jax.shard_map(
        shards,
        mesh=mesh,
        in_specs=(P("stn", None, "vox"), P(None, "vox"), P(), P()),
        out_specs=P("stn", "vox"),
        check_vma=False,
    )
```

time: 127 us -> 59.4 us (0.47)
  matrix products: 44.3 us -> 0 us
  between operations: 14.9 us -> 0.79 us
  blocking collectives: 37.2 us -> 26.5 us
  Pallas kernels: 0 us -> 9.11 us
  waiting for transfers between devices: 16.8 us -> 12 us
  local copies, waits for them, and re-layouts: 5.49 us -> 0.75 us
  starting transfers between devices: 2.58 us -> 6.7 us
    dot_general x28 -> x0, matrix products: 27.4 us -> none  [add_station(): jnp.dot(corr_rows, selector, preferred_element_type=jnp.float32)]
    conv_general_dilated x1 -> x0, matrix products: 16.9 us -> none  [shards(): lax.conv_general_dilated(segments, kernels, (1,), 'VALID', feature_group_...]
    reduce_scatter x1 -> x0, waiting for transfers between devices: 16.8 us -> none  [shards(): lax.psum_scatter(running, 'stn', scatter_dimension=0, tiled=True)]
    ppermute x2 -> x4, waiting for transfers between devices: 0.01 us -> 12 us  [the longest x1 7.28 us: shards(): received = lax.ppermute(sent, 'stn', [(0, 1), (1, 0)])]
    psum x1 -> x0, blocking collectives: 9.65 us -> none  [spread(): return lax.psum(kept, axis)]
    pallas_call x0 -> x2, Pallas kernels: none -> 9.11 us  [the longest x1 7.12 us: image(): pl.pallas_call(functools.partial(image_kernel, swap), out_shape=out_shape...]
    ppermute x2 -> x4, starting transfers between devices: 2.58 us -> 6.7 us  [the longest x1 2.36 us: neighbours(): low = lax.ppermute(block[:, block.shape[1] - width:], 'vox', forward)]
    unnamed x9 -> x4, local copies, waits for them, and re-layouts: 2.04 us -> 0.01 us
  transfers between devices with their start and end apart: 3 -> 4, of which waited for: 1 -> 3; matrix products, arithmetic and copies ran while one was open for 2% -> 2% of each run, Pallas kernels for 0% -> 0%
where the time goes in v1:
time: 59.4 us; the launch traced here: 59.1 us
  blocking collectives  26.5 us (45%)
  waiting for transfers between devices  12 us (20%)
  Pallas kernels  9.11 us (15%)
  starting transfers between devices  6.7 us (11%)
  other arithmetic  3.22 us (5%)
  between operations  0.79 us (1%)
  local copies, waits for them, and re-layouts  0.75 us (1%)
    all_gather x1, blocking collectives, shards(): gathered = lax.all_gather(corr, 'vox', axis=0, tiled=False)  26.5 us
    ppermute x1, waiting for transfers between devices, shards(): received = lax.ppermute(sent, 'stn', [(0, 1), (1, 0)])  7.28 us
    pallas_call x1, Pallas kernels, image(): pl.pallas_call(functools.partial(image_kernel, swap), out_shape=out_shape...  7.12 us
    ppermute x1, waiting for transfers between devices, neighbours(): high = lax.ppermute(block[:, :width], 'vox', backward)  3.81 us
    ppermute x1, starting transfers between devices, neighbours(): low = lax.ppermute(block[:, block.shape[1] - width:], 'vox', forward)  2.36 us
    pallas_call x1, Pallas kernels, correlate(): pl.pallas_call(functools.partial(corr_kernel, norm_inverse()), out_shape=...  1.99 us
    add x1, other arithmetic, shards(): return kept + received.astype(jnp.float32)  1.89 us
    ppermute x1, starting transfers between devices, shards(): other = lax.ppermute(extended, 'stn', [(0, 1), (1, 0)])  1.56 us
  transfers between devices with their start and end apart: 4, of which 3 were waited for; matrix products, arithmetic and copies ran while one was open for 2% of the time, Pallas kernels for 0%

profile of v1, /device:TPU:0, one launch (start us, length us, event | category | flops | bytes accessed | tf_op | source)
XLA Modules:
  0.0 59.1 jit_solution(12987802832117557411)
XLA Ops:
  0.7 0.7 %dynamic-slice_bitcast_fusion = bf16[2,4096]{1,0:T(2,128)(2,1)S(1)} fusion(bf16[28,2,4096]{2,1,0:T(2,128)(2,1)} %param.5, s32[]{:T(128)S(6)} %select_n.26), kind=kLoop, calls=%fused_computation.6 | loop fusion | bytes 32772 | tf_op jit(solution)/shard_map/jit(dynamic_index_in_dim)/squeeze | solution.py:233
  1.4 0.0 copy-start
  1.4 2.4 %collective-permute-start = (bf16[2,128]{1,0:T(2,128)(2,1)S(1)}, bf16[2,128]{1,0:T(2,128)(2,1)S(1)}, u32[]{:S(2)}, u32[]{:S(2)}) collective-permute-start(bf16[2,128]{1,0:T(2,128)(2,1)S(1)} %get-tuple-element.9), channel_id=1, source_target_pairs={{0,1},{1,2},{2,3},{3,4},{4,5},{5,6},{6,7},{7,8},{8,9},{9,10},{10,1... | collective-permute-start | bytes 1544 | tf_op jit(solution)/shard_map/ppermute | solution.py:220
  3.8 1.3 %collective-permute-start.1 = (bf16[2,128]{1,0:T(2,128)(2,1)S(1)}, bf16[2,128]{1,0:T(2,128)(2,1)S(1)}, u32[]{:S(2)}, u32[]{:S(2)}) collective-permute-start(bf16[2,128]{1,0:T(2,128)(2,1)S(1)} %get-tuple-element.10), channel_id=1, source_target_pairs={{1,0},{2,1},{3,2},{4,3},{5,4},{6,5},{7,6},{8,7},{9,8},{10,9},{11,1... | collective-permute-start | bytes 1544 | tf_op jit(solution)/shard_map/ppermute | solution.py:221
  5.1 0.0 copy-done
  5.1 0.0 collective-permute-done
  5.1 3.8 %collective-permute-done.1 = bf16[2,128]{1,0:T(2,128)(2,1)S(1)} collective-permute-done((bf16[2,128]{1,0:T(2,128)(2,1)S(1)}, bf16[2,128]{1,0:T(2,128)(2,1)S(1)}, u32[]{:S(2)}, u32[]{:S(2)}) %collective-permute-start.1) | collective-permute-done | bytes 544 | tf_op jit(solution)/shard_map/ppermute | solution.py:221
  9.0 1.6 %collective-permute-start.2 = (bf16[2,4352]{1,0:T(2,128)(2,1)S(1)}, bf16[2,4352]{1,0:T(2,128)(2,1)S(1)}, u32[]{:S(2)}, u32[]{:S(2)}) collective-permute-start(bf16[2,4352]{1,0:T(2,128)(2,1)S(1)} %pad_maximum_fusion), channel_id=1, source_target_pairs={{0,16},{16,0},{1,17},{17,1},{2,18},{18,2},{3,19},{19,3},{4,20},{20... | collective-permute-start | bytes 52232 | tf_op jit(solution)/shard_map/ppermute | solution.py:236
  10.5 1.3 %fusion.win_ref = bf16[2,28,4096]{2,1,0:T(8,128)(2,1)S(1)} fusion(bf16[28,2,4096]{2,1,0:T(2,128)(2,1)} %param.5, f32[4096]{0:T(1024)S(1)} %bitcast.14), kind=kLoop, calls=%fused_computation.1 | loop fusion | flops 688128 | bytes 933888 | tf_op jit(solution)/shard_map/transpose | solution.py:246
  11.8 0.9 %collective-permute-done.2 = bf16[2,4352]{1,0:T(2,128)(2,1)S(1)} collective-permute-done((bf16[2,4352]{1,0:T(2,128)(2,1)S(1)}, bf16[2,4352]{1,0:T(2,128)(2,1)S(1)}, u32[]{:S(2)}, u32[]{:S(2)}) %collective-permute-start.2) | collective-permute-done | bytes 17440 | tf_op jit(solution)/shard_map/ppermute | solution.py:236
  12.8 2.0 %shard_map.55 = bf16[4,7168]{1,0:T(4,128)(2,1)S(1)} custom-call(s32[1]{0:T(128)S(6)} %copy.12.ref_ref, bf16[2,28,4096]{2,1,0:T(8,128)(2,1)S(1)} %fusion.win_ref, bf16[2,4352]{1,0:T(2,128)(2,1)S(1)} %broadcast_select_fusion.ext_ref), custom_call_target="tpu_custom_call" | custom-call | flops 117440512 | bytes 458752 | tf_op jit(solution)/shard_map/pallas_call | solution.py:103
  14.8 26.5 %all-gather.1.corr_ref = bf16[16,4,7168]{2,1,0:T(4,128)(2,1)} all-gather(bf16[1,4,7168]{2,1,0:T(4,128)(2,1)S(1)} %bitcast.13), channel_id=2, replica_groups=mesh['stn'=2,'vox'=16] {'vox'}, dimensions={0}, use_global_device_ids=true | all-gather | bytes 974848 | tf_op jit(solution)/shard_map/all_gather | solution.py:249
  41.3 7.1 %shard_map.56 = (f32[32,4096]{1,0:T(8,128)}, bf16[32,4096]{1,0:T(8,128)(2,1)}) custom-call(s32[56]{0:T(128)} %offset_ref.1, bf16[16,4,7168]{2,1,0:T(4,128)(2,1)} %all-gather.1.corr_ref, s32[56,4096]{1,0:T(8,128)} %delay_ref.1), custom_call_target="tpu_custom_call" | custom-call | flops 7516192768 | bytes 1048576 | tf_op jit(solution)/shard_map/pallas_call | solution.py:196
  48.4 1.5 %collective-permute-start.3 = (bf16[32,4096]{1,0:T(8,128)(2,1)}, bf16[32,4096]{1,0:T(8,128)(2,1)S(1)}, u32[]{:S(2)}, u32[]{:S(2)}) collective-permute-start(bf16[32,4096]{1,0:T(8,128)(2,1)} %get-tuple-element.8), channel_id=1, source_target_pairs={{0,16},{16,0},{1,17},{17,1},{2,18},{18,2},{3,19},{19,3},{4,20},{20... | collective-permute-start | bytes 786440 | tf_op jit(solution)/shard_map/ppermute | solution.py:252
  49.9 7.3 %collective-permute-done.3 = bf16[32,4096]{1,0:T(8,128)(2,1)S(1)} collective-permute-done((bf16[32,4096]{1,0:T(8,128)(2,1)}, bf16[32,4096]{1,0:T(8,128)(2,1)S(1)}, u32[]{:S(2)}, u32[]{:S(2)}) %collective-permute-start.3) | collective-permute-done | bytes 262176 | tf_op jit(solution)/shard_map/ppermute | solution.py:252
  57.2 1.9 %convert_add_fusion = f32[32,4096]{1,0:T(8,128)} fusion(f32[32,4096]{1,0:T(8,128)} %get-tuple-element.7, bf16[32,4096]{1,0:T(8,128)(2,1)S(1)} %collective-permute-done.3), kind=kLoop, calls=%fused_computation.2 | loop fusion | flops 262144 | bytes 1310720 | tf_op jit(solution)/shard_map/add | solution.py:253
  (5 shorter events, 0.1 us)
Async XLA Ops:
  1.4 3.7 %copy-start = (f32[1024]{0:T(1024)S(1)}, f32[1024]{0:T(1024)}, u32[]{:S(2)}) copy-start(f32[1024]{0:T(1024)} %constant.34.clone) | copy-start | bytes 12292
  1.4 3.7 %collective-permute-start = (bf16[2,128]{1,0:T(2,128)(2,1)S(1)}, bf16[2,128]{1,0:T(2,128)(2,1)S(1)}, u32[]{:S(2)}, u32[]{:S(2)}) collective-permute-start(bf16[2,128]{1,0:T(2,128)(2,1)S(1)} %get-tuple-element.9), channel_id=1, source_target_pairs={{0,1},{1,2},{2,3},{3,4},{4,5},{5,6},{6,7},{7,8},{8,9},{9,10},{10,1... | collective-permute-start | bytes 1544 | tf_op jit(solution)/shard_map/ppermute | solution.py:220
  3.8 5.2 %collective-permute-start.1 = (bf16[2,128]{1,0:T(2,128)(2,1)S(1)}, bf16[2,128]{1,0:T(2,128)(2,1)S(1)}, u32[]{:S(2)}, u32[]{:S(2)}) collective-permute-start(bf16[2,128]{1,0:T(2,128)(2,1)S(1)} %get-tuple-element.10), channel_id=1, source_target_pairs={{1,0},{2,1},{3,2},{4,3},{5,4},{6,5},{7,6},{8,7},{9,8},{10,9},{11,1... | collective-permute-start | bytes 1544 | tf_op jit(solution)/shard_map/ppermute | solution.py:221
  9.0 3.8 %collective-permute-start.2 = (bf16[2,4352]{1,0:T(2,128)(2,1)S(1)}, bf16[2,4352]{1,0:T(2,128)(2,1)S(1)}, u32[]{:S(2)}, u32[]{:S(2)}) collective-permute-start(bf16[2,4352]{1,0:T(2,128)(2,1)S(1)} %pad_maximum_fusion), channel_id=1, source_target_pairs={{0,16},{16,0},{1,17},{17,1},{2,18},{18,2},{3,19},{19,3},{4,20},{20... | collective-permute-start | bytes 52232 | tf_op jit(solution)/shard_map/ppermute | solution.py:236
  48.4 8.8 %collective-permute-start.3 = (bf16[32,4096]{1,0:T(8,128)(2,1)}, bf16[32,4096]{1,0:T(8,128)(2,1)S(1)}, u32[]{:S(2)}, u32[]{:S(2)}) collective-permute-start(bf16[32,4096]{1,0:T(8,128)(2,1)} %get-tuple-element.8), channel_id=1, source_target_pairs={{0,16},{16,0},{1,17},{17,1},{2,18},{18,2},{3,19},{19,3},{4,20},{20... | collective-permute-start | bytes 786440 | tf_op jit(solution)/shard_map/ppermute | solution.py:252

commit v2 on v1

v2 whole, which is shorter than its diff:
```python
import functools
import math

import jax
import jax.numpy as jnp
import numpy as np
from jax import lax
from jax.experimental import pallas as pl
from jax.experimental.pallas import tpu as pltpu
from jax.sharding import PartitionSpec as P

STATIONS = 56
WIN = 1024
LAGS = 256
HALF = LAGS // 2
LANES = 128
F8 = jnp.float8_e4m3fn
VMEM = pl.BlockSpec(memory_space=pltpu.VMEM)
SMEM = pl.BlockSpec(memory_space=pltpu.SMEM)


def taper_weights():
    position = (np.arange(WIN, dtype=np.float32) + np.float32(0.5)) / np.float32(WIN)
    return (0.5 - 0.5 * np.cos(2.0 * np.pi * position.astype(np.float64))).astype(np.float32)


def norm_inverse():
    taper = taper_weights()
    return float(np.float32(1.0) / np.sqrt(np.sum(taper * taper, dtype=np.float32)))


def lane_gather(table, index):
    return lax.gather(
        table,
        index[..., None],
        lax.GatherDimensionNumbers(
            offset_dims=(),
            collapsed_slice_dims=(1,),
            start_index_map=(1,),
            operand_batching_dims=(0,),
            start_indices_batching_dims=(0,),
        ),
        slice_sizes=(1, 1),
        mode=lax.GatherScatterMode.PROMISE_IN_BOUNDS,
    )


def corr_kernel(norm, ref_ref, win_ref, ext_ref, out_ref, rev_ref, shift_ref, rows_ref):
    pols, stations, samples = win_ref.shape
    slices = samples // WIN
    blocks = ext_ref.shape[1] // LANES
    pitch = rows_ref.shape[1] // slices
    mirror = LANES - 1 - lax.broadcasted_iota(jnp.int32, (8, LANES), 1)
    for m in range(blocks):
        piece = ext_ref[:, LANES * m : LANES * (m + 1)].astype(jnp.float32)
        piece = jnp.concatenate([piece] * (8 // pols), axis=0)
        at = LANES * (blocks - 1 - m)
        rev_ref[:, at : at + LANES] = lane_gather(piece, mirror)
    for p in range(pols):
        for m in range(blocks - 1):
            pair = jnp.broadcast_to(
                rev_ref[p : p + 1, LANES * m : LANES * (m + 2)], (LANES, 2 * LANES)
            )
            rolled = pltpu.roll(pair, 0, 1, stride=1, stride_axis=0)
            shift_ref[p, :, LANES * (m + 1) : LANES * (m + 2)] = rolled[:, LANES:].astype(
                jnp.bfloat16
            )
    station = lax.broadcasted_iota(jnp.int32, (stations, LAGS), 0)
    column = lax.broadcasted_iota(jnp.int32, (stations, LAGS), 1)
    mine = ref_ref[0] - lax.axis_index("stn") * stations
    factor = jnp.where((station == mine) | (column == 0), 0.0, norm)
    for k in range(slices):
        total = jnp.zeros((stations, LAGS), jnp.float32)
        for p in range(pols):
            for a in range(WIN // LAGS):
                first = WIN * k + LAGS * a
                at = samples - first
                hankel = jnp.concatenate(
                    [shift_ref[p, :, at : at + LAGS], shift_ref[p, :, at - LANES : at + LANES]],
                    axis=0,
                )
                total = total + jnp.dot(
                    win_ref[p, :, first : first + LAGS],
                    hankel,
                    preferred_element_type=jnp.float32,
                )
        total = total * factor
        top = jnp.max(jnp.max(jnp.abs(total), axis=1, keepdims=True), axis=0, keepdims=True)
        power = jnp.floor(jnp.log2(224.0 / jnp.maximum(top, 1e-35)))
        scale = jnp.exp2(power).astype(jnp.bfloat16).astype(jnp.float32)
        total = jnp.where(column == 0, power, total * scale)
        for h in range(LAGS // LANES):
            rows_ref[h, pitch * k : pitch * k + stations, :] = total[
                :, LANES * h : LANES * (h + 1)
            ]
    for s in range(stations):
        for h in range(LAGS // LANES):
            at = LAGS * s + LANES * h
            out_ref[:, at : at + LANES] = rows_ref[h, pl.ds(s, slices, stride=pitch), :].astype(
                jnp.bfloat16
            )


def correlate(windowed, extended, reference_station):
    pols, stations, samples = windowed.shape
    slices = samples // WIN
    pitch = -(-stations // 8) * 8
    return pl.pallas_call(
        functools.partial(corr_kernel, norm_inverse()),
        out_shape=jax.ShapeDtypeStruct((slices, stations * LAGS), jnp.bfloat16),
        in_specs=[SMEM, VMEM, VMEM],
        out_specs=VMEM,
        scratch_shapes=[
            pltpu.VMEM((8, samples + LAGS), jnp.float32),
            pltpu.VMEM((pols, LANES, samples + LAGS), jnp.bfloat16),
            pltpu.VMEM((LAGS // LANES, pitch * slices, LANES), jnp.float32),
        ],
        cost_estimate=pl.CostEstimate(
            flops=2 * pols * stations * samples * LAGS,
            bytes_accessed=2 * pols * stations * samples,
            transcendentals=0,
        ),
        compiler_params=pltpu.CompilerParams(vmem_limit_bytes=24 << 20),
    )(reference_station, windowed, extended)


def split_kernel(*refs):
    *block_refs, pieces_ref, scale_ref = refs
    stages = []
    for ref in block_refs:
        block = ref[...].astype(jnp.float32)
        coarse = block.astype(F8).astype(jnp.float32)
        stages.append(jnp.concatenate([coarse, (block - coarse) * 16.0], axis=0))
    pieces_ref[...] = jnp.concatenate(stages, axis=0).astype(F8)
    for d, ref in enumerate(block_refs):
        rows = ref.shape[0]
        power = ref[:, 0:LANES].astype(jnp.float32)[:, 0:1]
        down = jnp.exp2(-power).astype(jnp.bfloat16).astype(jnp.float32)
        down = jnp.broadcast_to(down * (1.0 / math.sqrt(2.0 * STATIONS)), (rows, LANES))
        scale_ref[2 * rows * d : 2 * rows * (d + 1), :] = jnp.concatenate(
            [down, down * (1.0 / 16.0)], axis=0
        )


def split(blocks):
    slices, columns = blocks[0].shape
    rows = 2 * slices * len(blocks)
    return pl.pallas_call(
        split_kernel,
        out_shape=[
            jax.ShapeDtypeStruct((rows, columns), F8),
            jax.ShapeDtypeStruct((rows, LANES), jnp.float32),
        ],
        in_specs=[VMEM] * len(blocks),
        out_specs=[VMEM] * 2,
        cost_estimate=pl.CostEstimate(
            flops=8 * rows * columns, bytes_accessed=2 * rows * columns, transcendentals=0
        ),
        compiler_params=pltpu.CompilerParams(vmem_limit_bytes=16 << 20),
    )(*blocks)


def target_kernel(offset_ref, delay_ref, out_ref):
    stations, rows, voxels = out_ref.shape
    for s in range(stations):
        row = lax.axis_index("stn") * stations + s
        target = (HALF - 1 - offset_ref[row]) - delay_ref[pl.ds(row, 1), :]
        out_ref[s] = jnp.broadcast_to(target, (rows, voxels)).astype(jnp.int8)


def targets(sample_delays, timing_offsets, stations):
    voxels = sample_delays.shape[1]
    return pl.pallas_call(
        target_kernel,
        out_shape=jax.ShapeDtypeStruct((stations, 32, voxels), jnp.int8),
        in_specs=[SMEM, VMEM],
        out_specs=VMEM,
        cost_estimate=pl.CostEstimate(
            flops=32 * stations * voxels, bytes_accessed=36 * stations * voxels, transcendentals=0
        ),
        compiler_params=pltpu.CompilerParams(vmem_limit_bytes=24 << 20),
    )(timing_offsets, sample_delays)


def image_kernel(swap, parts, target_ref, *refs):
    piece_refs, scale_refs = refs[:parts], refs[parts : 2 * parts]
    *out_refs, sums_ref = refs[2 * parts :]
    rows = piece_refs[0].shape[0]
    stations, tile, voxels = target_ref.shape
    level = (lax.broadcasted_iota(jnp.int32, (LAGS, voxels), 0) - HALF).astype(jnp.int8)
    one = jnp.ones((LAGS, voxels), F8)
    zero = jnp.zeros((LAGS, voxels), F8)
    sums = jnp.zeros((parts * rows, voxels), jnp.float32)
    for s0 in range(0, stations, 2):
        hots = []
        for s in range(s0, min(s0 + 2, stations)):
            target = jnp.concatenate([target_ref[s]] * (LAGS // tile), axis=0)
            hots.append(jnp.where(level == target, one, zero))
        hot = jnp.concatenate(hots, axis=0) if len(hots) > 1 else hots[0]
        at = LAGS * s0
        pieces = jnp.concatenate([ref[:, at : at + hot.shape[0]] for ref in piece_refs], axis=0)
        sums = sums + jnp.dot(pieces, hot, preferred_element_type=jnp.float32)
    for g in range(parts):
        for r in range(0, rows, 8):
            at = rows * g + r
            sums_ref[at : at + 8, :] = sums[at : at + 8, :] * scale_refs[g][r : r + 8, 0:1]
    mine = lax.axis_index("vox")
    groups = parts * rows // 8
    if swap:
        mine = mine ^ (lax.axis_index("stn") * (groups // 2))
    first = lax.broadcasted_iota(jnp.int32, (8, voxels), 0) < 4
    lower = None
    for j in range(0, groups, 2):
        here = sums_ref[pl.ds(pl.multiple_of(8 * (mine ^ j), 8), 8), :]
        there = sums_ref[pl.ds(pl.multiple_of(8 * (mine ^ (j + 1)), 8), 8), :]
        value = jnp.where(
            first,
            here + pltpu.roll(here, 4, 0),
            there + pltpu.roll(there, 4, 0),
        )
        if not swap or j < groups // 2:
            out_refs[0][4 * j : 4 * j + 8, :] = value
        elif lower is None:
            lower = value
        else:
            at = 4 * (j - groups // 2) - 8
            out_refs[1][at : at + 16, :] = jnp.concatenate([lower, value], axis=0).astype(
                jnp.bfloat16
            )
            lower = None


def image(pieces, scales, target, swap, part, count):
    rows, columns = pieces[0].shape
    total = len(pieces) * rows // 2
    stations, tile, voxels = target.shape
    voxels = voxels // count
    if swap:
        out_shape = [
            jax.ShapeDtypeStruct((total // 2, voxels), jnp.float32),
            jax.ShapeDtypeStruct((total // 2, voxels), jnp.bfloat16),
        ]
    else:
        out_shape = [jax.ShapeDtypeStruct((total, voxels), jnp.float32)]
    return pl.pallas_call(
        functools.partial(image_kernel, swap, len(pieces)),
        grid=(1,),
        out_shape=out_shape,
        in_specs=[pl.BlockSpec((stations, tile, voxels), lambda i: (0, 0, part))]
        + [VMEM] * (2 * len(pieces)),
        out_specs=[VMEM] * len(out_shape),
        scratch_shapes=[pltpu.VMEM((2 * total, voxels), jnp.float32)],
        cost_estimate=pl.CostEstimate(
            flops=4 * total * columns * voxels,
            bytes_accessed=4 * total * voxels,
            transcendentals=0,
        ),
        compiler_params=pltpu.CompilerParams(vmem_limit_bytes=48 << 20),
    )(target, *pieces, *scales)


def add_kernel(*refs):
    *in_refs, out_ref = refs
    at = 0
    for kept_ref, came_ref in zip(in_refs[::2], in_refs[1::2], strict=True):
        width = kept_ref.shape[1]
        out_ref[:, at : at + width] = kept_ref[...] + came_ref[...].astype(jnp.float32)
        at += width


def flip(block, axis, mask):
    count = lax.axis_size(axis)
    return lax.ppermute(block, axis, [(i, i ^ mask) for i in range(count)])


def extend_paired(candidate, owner):
    count = lax.axis_size("vox")
    odd = lax.axis_index("vox") % 2 == 1
    first, last = candidate[:, :HALF], candidate[:, candidate.shape[1] - HALF :]
    steps = [(b, b + 1) for b in range(1, count - 1, 2)] + [(b + 1, b) for b in range(1, count - 1, 2)]
    outer = jnp.where(odd, last, first)
    here = lax.ppermute(outer, "vox", steps)
    cross = [
        (x * count + source, (1 - x) * count + target) for x in range(2) for source, target in steps
    ]
    there = lax.ppermute(outer, ("stn", "vox"), cross)
    inner = flip(jnp.where(odd, first, last), "vox", 1)
    wide = jnp.concatenate([candidate, inner], axis=1)
    other = flip(wide, "stn", 1)
    mine = lax.axis_index("stn") == owner
    wide = jnp.where(mine, wide, other)
    outer = jnp.where(mine, here, there)
    body, inner = wide[:, : candidate.shape[1]], wide[:, candidate.shape[1] :]
    return jnp.concatenate(
        [jnp.where(odd, inner, outer), body, jnp.where(odd, outer, inner)], axis=1
    )


def extend(candidate, owner):
    kept = jnp.where(lax.axis_index("stn") == owner, candidate, 0).astype(candidate.dtype)
    block = lax.psum(kept, "stn")
    count = lax.axis_size("vox")
    forward = [(i, i + 1) for i in range(count - 1)]
    backward = [(target, source) for source, target in forward]
    low = lax.ppermute(block[:, block.shape[1] - HALF :], "vox", forward)
    high = lax.ppermute(block[:, :HALF], "vox", backward)
    return jnp.concatenate([low, block, high], axis=1)


def gather_paired(block):
    blocks = {0: block}
    for d in (12, 8, 4):
        blocks[d] = flip(block, "vox", d)
    for d in (0, 4, 8, 12):
        blocks[d | 2] = flip(blocks[d], "vox", 2)
    for d in (0, 2, 4, 6, 8, 10, 12, 14):
        blocks[d | 1] = flip(blocks[d], "vox", 1)
    return [[blocks[d] for d in order] for order in ORDER]


ORDER = ((0, 1, 2, 3), (4, 5, 6, 7), (8, 9, 10, 11), (12, 13, 14, 15))


def shards(voltages, sample_delays, timing_offsets, reference_station):
    stations_here, pols, samples_here = voltages.shape
    slices_here = samples_here // WIN
    count = lax.axis_size("vox")
    station_ref = reference_station[0]
    owner = station_ref // stations_here
    swap = lax.axis_size("stn") == 2 and count == 16

    candidate = lax.dynamic_index_in_dim(voltages, station_ref % stations_here, 0, keepdims=False)
    extended = extend_paired(candidate, owner) if swap else extend(candidate, owner)

    windowed = (
        voltages.reshape(stations_here, pols, slices_here, WIN).astype(jnp.float32)
        * taper_weights()
    ).astype(jnp.bfloat16)
    windowed = jnp.transpose(windowed.reshape(stations_here, pols, samples_here), (1, 0, 2))

    corr = correlate(windowed, extended, reference_station)
    target = targets(sample_delays, timing_offsets, stations_here)
    if swap:
        groups = gather_paired(corr)
    else:
        gathered = lax.all_gather(corr, "vox", axis=0, tiled=False)
        mine = lax.axis_index("vox")
        every = [
            lax.dynamic_index_in_dim(gathered, mine ^ j, 0, keepdims=False) for j in range(count)
        ]
        groups = [every[j : j + 4] for j in range(0, count, 4)]
    pieces, scales = zip(*[split(blocks) for blocks in groups], strict=True)
    if not swap:
        (partial,) = image(pieces, scales, target, False, 0, 1)
        return lax.psum_scatter(partial, "stn", scatter_dimension=0, tiled=True)
    operands = []
    for part in range(PARTS):
        kept, sent = image(pieces, scales, target, True, part, PARTS)
        operands += [kept, flip(sent, "stn", 1)]
    return pl.pallas_call(
        add_kernel,
        out_shape=jax.ShapeDtypeStruct((operands[0].shape[0], sample_delays.shape[1]), jnp.float32),
        in_specs=[VMEM] * len(operands),
        out_specs=VMEM,
        compiler_params=pltpu.CompilerParams(vmem_limit_bytes=16 << 20),
    )(*operands)


PARTS = 2


def solution(mesh):
    return jax.shard_map(
        shards,
        mesh=mesh,
        in_specs=(P("stn", None, "vox"), P(None, "vox"), P(), P()),
        out_specs=P("stn", "vox"),
        check_vma=False,
    )
```

time: 59.4 us -> 50.3 us (0.85)
  blocking collectives: 26.5 us -> 0 us
  starting transfers between devices: 6.7 us -> 21.7 us
  local copies, waits for them, and re-layouts: 0.75 us -> 3.28 us
  other arithmetic: 3.22 us -> 1.37 us
  waiting for transfers between devices: 12 us -> 13.3 us
    all_gather x1 -> x0, blocking collectives: 26.5 us -> none  [shards(): gathered = lax.all_gather(corr, 'vox', axis=0, tiled=False)]
    ppermute x4 -> x21, starting transfers between devices: 6.7 us -> 21.7 us  [the longest x19 20.4 us: flip(): return lax.ppermute(block, axis, [(i, i ^ mask) for i in range(count)])]
    unnamed x4 -> x6, local copies, waits for them, and re-layouts: 0.01 us -> 2.53 us
    add x1 -> x0, other arithmetic: 1.89 us -> none  [shards(): return kept + received.astype(jnp.float32)]
    ppermute x4 -> x21, waiting for transfers between devices: 12 us -> 13.3 us  [the longest x19 13.3 us: flip(): return lax.ppermute(block, axis, [(i, i ^ mask) for i in range(count)])]
    pallas_call x1 -> x8, Pallas kernels: 7.12 us -> 7.31 us  [the longest x2 4.25 us: image(): pl.pallas_call(functools.partial(image_kernel, swap, len(pieces)), grid=(...]
  transfers between devices with their start and end apart: 4 -> 21, of which waited for: 3 -> 8; matrix products, arithmetic and copies ran while one was open for 2% -> 4% of each run, Pallas kernels for 0% -> 4%
where the time goes in v2:
time: 50.3 us; the launch traced here: 50 us
  starting transfers between devices  21.7 us (43%)
  waiting for transfers between devices  13.3 us (26%)
  Pallas kernels  9.4 us (19%)
  local copies, waits for them, and re-layouts  3.28 us (7%)
  other arithmetic  1.37 us (3%)
  between operations  0.89 us (2%)
    ppermute x19, starting transfers between devices, flip(): return lax.ppermute(block, axis, [(i, i ^ mask) for i in range(count)])  20.4 us
    ppermute x19, waiting for transfers between devices, flip(): return lax.ppermute(block, axis, [(i, i ^ mask) for i in range(count)])  13.3 us
    pallas_call x2, Pallas kernels, image(): pl.pallas_call(functools.partial(image_kernel, swap, len(pieces)), grid=(...  4.25 us
    unnamed x6, local copies, waits for them, and re-layouts  2.53 us
    pallas_call x1, Pallas kernels, correlate(): pl.pallas_call(functools.partial(corr_kernel, norm_inverse()), out_shape=...  2.1 us
    transpose x1, other arithmetic, shards(): jnp.transpose(windowed.reshape(stations_here, pols, samples_here), (1, 0,...  1.29 us
    pallas_call x4, Pallas kernels, split(): pl.pallas_call(split_kernel, out_shape=[jax.ShapeDtypeStruct((rows, colum...  1.26 us
  transfers between devices with their start and end apart: 21, of which 8 were waited for; matrix products, arithmetic and copies ran while one was open for 4% of the time, Pallas kernels for 4%

profile of v2, /device:TPU:0, one launch (start us, length us, event | category | flops | bytes accessed | tf_op | source)
XLA Modules:
  0.0 50.0 jit_solution(6354234079945031293)
XLA Ops:
  0.7 0.7 %dynamic-slice_bitcast_fusion = bf16[2,4096]{1,0:T(2,128)(2,1)S(1)} fusion(bf16[28,2,4096]{2,1,0:T(2,128)(2,1)} %param.5, s32[]{:T(128)S(6)} %select_n.58), kind=kLoop, calls=%fused_computation.6 | loop fusion | bytes 32772 | tf_op jit(solution)/shard_map/jit(dynamic_index_in_dim)/squeeze | solution.py:332
  1.4 0.7 %collective-permute-start.2 = (bf16[2,128]{1,0:T(2,128)(2,1)S(1)}, bf16[2,128]{1,0:T(2,128)(2,1)S(1)}, u32[]{:S(2)}, u32[]{:S(2)}) collective-permute-start(bf16[2,128]{1,0:T(2,128)(2,1)S(1)} %get-tuple-element.31), channel_id=1, source_target_pairs={{1,2},{3,4},{5,6},{7,8},{9,10},{11,12},{13,14},{2,1},{4,3},{6,5},{... | collective-permute-start | bytes 1544 | tf_op jit(solution)/shard_map/ppermute | solution.py:282
  2.1 0.7 %collective-permute-start.3 = (bf16[2,128]{1,0:T(2,128)(2,1)S(1)}, bf16[2,128]{1,0:T(2,128)(2,1)S(1)}, u32[]{:S(2)}, u32[]{:S(2)}) collective-permute-start(bf16[2,128]{1,0:T(2,128)(2,1)S(1)} %get-tuple-element.31), channel_id=1, source_target_pairs={{1,18},{3,20},{5,22},{7,24},{9,26},{11,28},{13,30},{2,17},{4,19},{... | collective-permute-start | bytes 1544 | tf_op jit(solution)/shard_map/ppermute | solution.py:286
  2.8 6.6 %collective-permute-start = (bf16[2,128]{1,0:T(2,128)(2,1)S(1)}, bf16[2,128]{1,0:T(2,128)(2,1)S(1)}, u32[]{:S(2)}, u32[]{:S(2)}) collective-permute-start(bf16[2,128]{1,0:T(2,128)(2,1)S(1)} %get-tuple-element.32), channel_id=1, source_target_pairs={{0,1},{1,0},{2,3},{3,2},{4,5},{5,4},{6,7},{7,6},{8,9},{9,8},{10,11... | collective-permute-start | bytes 1544 | tf_op jit(solution)/shard_map/ppermute | solution.py:273
  9.3 0.7 %broadcast_bitcast_fusion = f32[1,8,4,128]{3,2,1,0:T(4,128)S(1)} fusion(f32[1024]{0:T(1024)} %constant.48.clone), kind=kLoop, calls=%fused_computation.7 | loop fusion | bytes 20480
  10.2 0.6 %collective-permute-start.1 = (bf16[2,4224]{1,0:T(2,128)(2,1)S(1)}, bf16[2,4224]{1,0:T(2,128)(2,1)S(1)}, u32[]{:S(2)}, u32[]{:S(2)}) collective-permute-start(bf16[2,4224]{1,0:T(2,128)(2,1)S(1)} %pad_maximum_fusion.1), channel_id=1, source_target_pairs={{0,16},{16,0},{1,17},{17,1},{2,18},{18,2},{3,19},{19,3},{4,20},{20... | collective-permute-start | bytes 50696 | tf_op jit(solution)/shard_map/ppermute | solution.py:273
  10.8 1.3 %fusion.win_ref = bf16[2,28,4096]{2,1,0:T(8,128)(2,1)S(1)} fusion(bf16[28,2,4096]{2,1,0:T(2,128)(2,1)} %param.5, f32[4096]{0:T(1024)S(1)} %bitcast.12), kind=kLoop, calls=%fused_computation.1 | loop fusion | flops 688128 | bytes 933888 | tf_op jit(solution)/shard_map/transpose | solution.py:339
  12.1 1.9 %collective-permute-done.1 = bf16[2,4224]{1,0:T(2,128)(2,1)S(1)} collective-permute-done((bf16[2,4224]{1,0:T(2,128)(2,1)S(1)}, bf16[2,4224]{1,0:T(2,128)(2,1)S(1)}, u32[]{:S(2)}, u32[]{:S(2)}) %collective-permute-start.1) | collective-permute-done | bytes 16928 | tf_op jit(solution)/shard_map/ppermute | solution.py:273
  14.1 2.1 %shard_map.56.refs_0_ = bf16[4,7168]{1,0:T(4,128)(2,1)S(1)} custom-call(s32[1]{0:T(128)S(6)} %copy.11.ref_ref, bf16[2,28,4096]{2,1,0:T(8,128)(2,1)S(1)} %fusion.win_ref, bf16[2,4352]{1,0:T(2,128)(2,1)S(1)} %pad_maximum_fusion.ext_ref), custom_call_target="tpu_custom_call" | custom-call | flops 117440512 | bytes 458752 | tf_op jit(solution)/shard_map/pallas_call | solution.py:108
  16.2 5.0 %collective-permute-start.15 = (bf16[4,7168]{1,0:T(4,128)(2,1)S(1)}, bf16[4,7168]{1,0:T(4,128)(2,1)S(1)}, u32[]{:S(2)}, u32[]{:S(2)}) collective-permute-start(bf16[4,7168]{1,0:T(4,128)(2,1)S(1)} %shard_map.56.refs_0_), channel_id=1, source_target_pairs={{0,12},{1,13},{2,14},{3,15},{4,8},{5,9},{6,10},{7,11},{8,4},{9,5},... | collective-permute-start | bytes 172040 | tf_op jit(solution)/shard_map/ppermute | solution.py:273
  21.2 0.6 %collective-permute-start.7 = (bf16[4,7168]{1,0:T(4,128)(2,1)S(1)}, bf16[4,7168]{1,0:T(4,128)(2,1)S(1)}, u32[]{:S(2)}, u32[]{:S(2)}) collective-permute-start(bf16[4,7168]{1,0:T(4,128)(2,1)S(1)} %shard_map.56.refs_0_), channel_id=1, source_target_pairs={{0,4},{1,5},{2,6},{3,7},{4,0},{5,1},{6,2},{7,3},{8,12},{9,13},{10,... | collective-permute-start | bytes 172040 | tf_op jit(solution)/shard_map/ppermute | solution.py:273
  21.8 1.2 %collective-permute-start.5 = (bf16[4,7168]{1,0:T(4,128)(2,1)S(1)}, bf16[4,7168]{1,0:T(4,128)(2,1)S(1)}, u32[]{:S(2)}, u32[]{:S(2)}) collective-permute-start(bf16[4,7168]{1,0:T(4,128)(2,1)S(1)} %shard_map.56.refs_0_), channel_id=1, source_target_pairs={{0,2},{1,3},{2,0},{3,1},{4,6},{5,7},{6,4},{7,5},{8,10},{9,11},{10,... | collective-permute-start | bytes 172040 | tf_op jit(solution)/shard_map/ppermute | solution.py:273
  23.0 0.8 %collective-permute-done.15.refs_0_ = bf16[4,7168]{1,0:T(4,128)(2,1)S(1)} collective-permute-done((bf16[4,7168]{1,0:T(4,128)(2,1)S(1)}, bf16[4,7168]{1,0:T(4,128)(2,1)S(1)}, u32[]{:S(2)}, u32[]{:S(2)}) %collective-permute-start.15) | collective-permute-done | bytes 57376 | tf_op jit(solution)/shard_map/ppermute | solution.py:273
  23.8 1.1 %collective-permute-start.17 = (bf16[4,7168]{1,0:T(4,128)(2,1)S(1)}, bf16[4,7168]{1,0:T(4,128)(2,1)S(1)}, u32[]{:S(2)}, u32[]{:S(2)}) collective-permute-start(bf16[4,7168]{1,0:T(4,128)(2,1)S(1)} %collective-permute-done.15.refs_0_), channel_id=1, source_target_pairs={{0,2},{1,3},{2,0},{3,1},{4,6},{5,7},{6,4},{7,5},{8,10},{9,11},{10,... | collective-permute-start | bytes 172040 | tf_op jit(solution)/shard_map/ppermute | solution.py:273
  24.9 1.4 %collective-permute-done.11.refs_0_ = bf16[4,7168]{1,0:T(4,128)(2,1)S(1)} collective-permute-done((bf16[4,7168]{1,0:T(4,128)(2,1)S(1)}, bf16[4,7168]{1,0:T(4,128)(2,1)S(1)}, u32[]{:S(2)}, u32[]{:S(2)}) %collective-permute-start.11) | collective-permute-done | bytes 57376 | tf_op jit(solution)/shard_map/ppermute | solution.py:273
  26.4 0.7 %collective-permute-start.13 = (bf16[4,7168]{1,0:T(4,128)(2,1)S(1)}, bf16[4,7168]{1,0:T(4,128)(2,1)S(1)}, u32[]{:S(2)}, u32[]{:S(2)}) collective-permute-start(bf16[4,7168]{1,0:T(4,128)(2,1)S(1)} %collective-permute-done.11.refs_0_), channel_id=1, source_target_pairs={{0,2},{1,3},{2,0},{3,1},{4,6},{5,7},{6,4},{7,5},{8,10},{9,11},{10,... | collective-permute-start | bytes 172040 | tf_op jit(solution)/shard_map/ppermute | solution.py:273
  27.1 1.3 %collective-permute-start.9 = (bf16[4,7168]{1,0:T(4,128)(2,1)S(1)}, bf16[4,7168]{1,0:T(4,128)(2,1)S(1)}, u32[]{:S(2)}, u32[]{:S(2)}) collective-permute-start(bf16[4,7168]{1,0:T(4,128)(2,1)S(1)} %collective-permute-done.7.refs_0_), channel_id=1, source_target_pairs={{0,2},{1,3},{2,0},{3,1},{4,6},{5,7},{6,4},{7,5},{8,10},{9,11},{10,... | collective-permute-start | bytes 172040 | tf_op jit(solution)/shard_map/ppermute | solution.py:273
  28.4 0.5 %collective-permute-start.18 = (bf16[4,7168]{1,0:T(4,128)(2,1)S(1)}, bf16[4,7168]{1,0:T(4,128)(2,1)S(1)}, u32[]{:S(2)}, u32[]{:S(2)}) collective-permute-start(bf16[4,7168]{1,0:T(4,128)(2,1)S(1)} %collective-permute-done.17.refs_2_), channel_id=1, source_target_pairs={{0,1},{1,0},{2,3},{3,2},{4,5},{5,4},{6,7},{7,6},{8,9},{9,8},{10,11... | collective-permute-start | bytes 172040 | tf_op jit(solution)/shard_map/ppermute | solution.py:273
  29.0 2.1 %collective-permute-done.13.refs_2_ = bf16[4,7168]{1,0:T(4,128)(2,1)S(1)} collective-permute-done((bf16[4,7168]{1,0:T(4,128)(2,1)S(1)}, bf16[4,7168]{1,0:T(4,128)(2,1)S(1)}, u32[]{:S(2)}, u32[]{:S(2)}) %collective-permute-start.13) | collective-permute-done | bytes 57376 | tf_op jit(solution)/shard_map/ppermute | solution.py:273
  31.1 0.8 %collective-permute-done.9.refs_2_ = bf16[4,7168]{1,0:T(4,128)(2,1)S(1)} collective-permute-done((bf16[4,7168]{1,0:T(4,128)(2,1)S(1)}, bf16[4,7168]{1,0:T(4,128)(2,1)S(1)}, u32[]{:S(2)}, u32[]{:S(2)}) %collective-permute-start.9) | collective-permute-done | bytes 57376 | tf_op jit(solution)/shard_map/ppermute | solution.py:273
  31.9 0.5 %collective-permute-start.10 = (bf16[4,7168]{1,0:T(4,128)(2,1)S(1)}, bf16[4,7168]{1,0:T(4,128)(2,1)S(1)}, u32[]{:S(2)}, u32[]{:S(2)}) collective-permute-start(bf16[4,7168]{1,0:T(4,128)(2,1)S(1)} %collective-permute-done.9.refs_2_), channel_id=1, source_target_pairs={{0,1},{1,0},{2,3},{3,2},{4,5},{5,4},{6,7},{7,6},{8,9},{9,8},{10,11... | collective-permute-start | bytes 172040 | tf_op jit(solution)/shard_map/ppermute | solution.py:273
  32.5 1.2 %copy-done = s32[56,4096]{1,0:T(8,128)S(1)} copy-done((s32[56,4096]{1,0:T(8,128)S(1)}, s32[56,4096]{1,0:T(8,128)}, u32[]{:S(2)}) %copy-start) | copy-done | bytes 917528
  33.6 0.7 %copy-done.1 = s32[56]{0:T(128)S(1)} copy-done((s32[56]{0:T(128)S(1)}, s32[56]{0:T(128)}, u32[]{:S(2)}) %copy-start.1) | copy-done | bytes 248
  34.3 1.0 %shard_map.55.target_ref = s8[28,32,4096]{2,1,0:T(32,128)(4,1)S(1)} custom-call(s32[56]{0:T(128)S(1)} %copy-done.1, s32[56,4096]{1,0:T(8,128)S(1)} %copy-done), custom_call_target="tpu_custom_call" | custom-call | flops 3670016 | bytes 4128768 | tf_op jit(solution)/shard_map/pallas_call | solution.py:173
  35.9 0.3 shard_map.59
  36.6 2.1 %shard_map.62 = (f32[32,2048]{1,0:T(8,128)S(1)}, bf16[32,2048]{1,0:T(8,128)(2,1)S(1)}) custom-call(s8[28,32,4096]{2,1,0:T(32,128)(4,1)S(1)} %shard_map.55.target_ref, f8e4m3fn[32,7168]{1,0:T(32,128)(4,1)S(1)} %get-tuple-element.17.refs_0_, f8e4m3fn[32,7168]{1,0:T(32,128)(4,1)S(1)} %get-tuple-element.18.refs_1_, ...), custom_call_target="tpu_custom_call" | custom-call | flops 3758096384 | bytes 524288 | tf_op jit(solution)/shard_map/pallas_call | solution.py:245
  38.7 2.1 %shard_map.61 = (f32[32,2048]{1,0:T(8,128)S(1)}, bf16[32,2048]{1,0:T(8,128)(2,1)S(1)}) custom-call(s8[28,32,4096]{2,1,0:T(32,128)(4,1)S(1)} %shard_map.55.target_ref, f8e4m3fn[32,7168]{1,0:T(32,128)(4,1)S(1)} %get-tuple-element.17.refs_0_, f8e4m3fn[32,7168]{1,0:T(32,128)(4,1)S(1)} %get-tuple-element.18.refs_1_, ...), custom_call_target="tpu_custom_call" | custom-call | flops 3758096384 | bytes 524288 | tf_op jit(solution)/shard_map/pallas_call | solution.py:245
  40.8 0.6 %collective-permute-start.20 = (bf16[32,2048]{1,0:T(8,128)(2,1)S(1)}, bf16[32,2048]{1,0:T(8,128)(2,1)S(1)}, u32[]{:S(2)}, u32[]{:S(2)}) collective-permute-start(bf16[32,2048]{1,0:T(8,128)(2,1)S(1)} %get-tuple-element.28), channel_id=1, source_target_pairs={{0,16},{16,0},{1,17},{17,1},{2,18},{18,2},{3,19},{19,3},{4,20},{20... | collective-permute-start | bytes 393224 | tf_op jit(solution)/shard_map/ppermute | solution.py:273
  41.4 1.5 %collective-permute-start.19 = (bf16[32,2048]{1,0:T(8,128)(2,1)S(1)}, bf16[32,2048]{1,0:T(8,128)(2,1)S(1)}, u32[]{:S(2)}, u32[]{:S(2)}) collective-permute-start(bf16[32,2048]{1,0:T(8,128)(2,1)S(1)} %get-tuple-element.26), channel_id=1, source_target_pairs={{0,16},{16,0},{1,17},{17,1},{2,18},{18,2},{3,19},{19,3},{4,20},{20... | collective-permute-start | bytes 393224 | tf_op jit(solution)/shard_map/ppermute | solution.py:273
  42.9 4.3 %collective-permute-done.20.refs_3_ = bf16[32,2048]{1,0:T(8,128)(2,1)S(1)} collective-permute-done((bf16[32,2048]{1,0:T(8,128)(2,1)S(1)}, bf16[32,2048]{1,0:T(8,128)(2,1)S(1)}, u32[]{:S(2)}, u32[]{:S(2)}) %collective-permute-start.20) | collective-permute-done | bytes 131104 | tf_op jit(solution)/shard_map/ppermute | solution.py:273
  47.3 1.8 %collective-permute-done.19.refs_1_ = bf16[32,2048]{1,0:T(8,128)(2,1)S(1)} collective-permute-done((bf16[32,2048]{1,0:T(8,128)(2,1)S(1)}, bf16[32,2048]{1,0:T(8,128)(2,1)S(1)}, u32[]{:S(2)}, u32[]{:S(2)}) %collective-permute-start.19) | collective-permute-done | bytes 131104 | tf_op jit(solution)/shard_map/ppermute | solution.py:273
  49.1 0.8 %shard_map.63 = f32[32,4096]{1,0:T(8,128)} custom-call(f32[32,2048]{1,0:T(8,128)S(1)} %get-tuple-element.25.refs_0_, bf16[32,2048]{1,0:T(8,128)(2,1)S(1)} %collective-permute-done.19.refs_1_, f32[32,2048]{1,0:T(8,128)S(1)} %get-tuple-element.27.refs_2_, bf16[32,2048]{1,0:T(8,128)(2,1)S(1)} %collective-permute-done.20.refs_3_), custom_call_target="tpu_custom_call" | custom-call | tf_op jit(solution)/shard_map/pallas_call | solution.py:360
  (33 shorter events, 1.3 us)
Async XLA Ops:
  1.4 12.6 %collective-permute-start.2 = (bf16[2,128]{1,0:T(2,128)(2,1)S(1)}, bf16[2,128]{1,0:T(2,128)(2,1)S(1)}, u32[]{:S(2)}, u32[]{:S(2)}) collective-permute-start(bf16[2,128]{1,0:T(2,128)(2,1)S(1)} %get-tuple-element.31), channel_id=1, source_target_pairs={{1,2},{3,4},{5,6},{7,8},{9,10},{11,12},{13,14},{2,1},{4,3},{6,5},{... | collective-permute-start | bytes 1544 | tf_op jit(solution)/shard_map/ppermute | solution.py:282
  2.1 12.0 %collective-permute-start.3 = (bf16[2,128]{1,0:T(2,128)(2,1)S(1)}, bf16[2,128]{1,0:T(2,128)(2,1)S(1)}, u32[]{:S(2)}, u32[]{:S(2)}) collective-permute-start(bf16[2,128]{1,0:T(2,128)(2,1)S(1)} %get-tuple-element.31), channel_id=1, source_target_pairs={{1,18},{3,20},{5,22},{7,24},{9,26},{11,28},{13,30},{2,17},{4,19},{... | collective-permute-start | bytes 1544 | tf_op jit(solution)/shard_map/ppermute | solution.py:286
  2.8 7.4 %collective-permute-start = (bf16[2,128]{1,0:T(2,128)(2,1)S(1)}, bf16[2,128]{1,0:T(2,128)(2,1)S(1)}, u32[]{:S(2)}, u32[]{:S(2)}) collective-permute-start(bf16[2,128]{1,0:T(2,128)(2,1)S(1)} %get-tuple-element.32), channel_id=1, source_target_pairs={{0,1},{1,0},{2,3},{3,2},{4,5},{5,4},{6,7},{7,6},{8,9},{9,8},{10,11... | collective-permute-start | bytes 1544 | tf_op jit(solution)/shard_map/ppermute | solution.py:273
  10.2 3.8 %collective-permute-start.1 = (bf16[2,4224]{1,0:T(2,128)(2,1)S(1)}, bf16[2,4224]{1,0:T(2,128)(2,1)S(1)}, u32[]{:S(2)}, u32[]{:S(2)}) collective-permute-start(bf16[2,4224]{1,0:T(2,128)(2,1)S(1)} %pad_maximum_fusion.1), channel_id=1, source_target_pairs={{0,16},{16,0},{1,17},{17,1},{2,18},{18,2},{3,19},{19,3},{4,20},{20... | collective-permute-start | bytes 50696 | tf_op jit(solution)/shard_map/ppermute | solution.py:273
  16.2 7.6 %collective-permute-start.15 = (bf16[4,7168]{1,0:T(4,128)(2,1)S(1)}, bf16[4,7168]{1,0:T(4,128)(2,1)S(1)}, u32[]{:S(2)}, u32[]{:S(2)}) collective-permute-start(bf16[4,7168]{1,0:T(4,128)(2,1)S(1)} %shard_map.56.refs_0_), channel_id=1, source_target_pairs={{0,12},{1,13},{2,14},{3,15},{4,8},{5,9},{6,10},{7,11},{8,4},{9,5},... | collective-permute-start | bytes 172040 | tf_op jit(solution)/shard_map/ppermute | solution.py:273
  21.2 5.2 %collective-permute-start.11 = (bf16[4,7168]{1,0:T(4,128)(2,1)S(1)}, bf16[4,7168]{1,0:T(4,128)(2,1)S(1)}, u32[]{:S(2)}, u32[]{:S(2)}) collective-permute-start(bf16[4,7168]{1,0:T(4,128)(2,1)S(1)} %shard_map.56.refs_0_), channel_id=1, source_target_pairs={{0,8},{1,9},{2,10},{3,11},{4,12},{5,13},{6,14},{7,15},{8,0},{9,1},... | collective-permute-start | bytes 172040 | tf_op jit(solution)/shard_map/ppermute | solution.py:273
  21.2 5.2 %collective-permute-start.7 = (bf16[4,7168]{1,0:T(4,128)(2,1)S(1)}, bf16[4,7168]{1,0:T(4,128)(2,1)S(1)}, u32[]{:S(2)}, u32[]{:S(2)}) collective-permute-start(bf16[4,7168]{1,0:T(4,128)(2,1)S(1)} %shard_map.56.refs_0_), channel_id=1, source_target_pairs={{0,4},{1,5},{2,6},{3,7},{4,0},{5,1},{6,2},{7,3},{8,12},{9,13},{10,... | collective-permute-start | bytes 172040 | tf_op jit(solution)/shard_map/ppermute | solution.py:273
  21.8 5.3 %collective-permute-start.5 = (bf16[4,7168]{1,0:T(4,128)(2,1)S(1)}, bf16[4,7168]{1,0:T(4,128)(2,1)S(1)}, u32[]{:S(2)}, u32[]{:S(2)}) collective-permute-start(bf16[4,7168]{1,0:T(4,128)(2,1)S(1)} %shard_map.56.refs_0_), channel_id=1, source_target_pairs={{0,2},{1,3},{2,0},{3,1},{4,6},{5,7},{6,4},{7,5},{8,10},{9,11},{10,... | collective-permute-start | bytes 172040 | tf_op jit(solution)/shard_map/ppermute | solution.py:273
  23.0 5.4 %collective-permute-start.4 = (bf16[4,7168]{1,0:T(4,128)(2,1)S(1)}, bf16[4,7168]{1,0:T(4,128)(2,1)S(1)}, u32[]{:S(2)}, u32[]{:S(2)}) collective-permute-start(bf16[4,7168]{1,0:T(4,128)(2,1)S(1)} %shard_map.56.refs_0_), channel_id=1, source_target_pairs={{0,1},{1,0},{2,3},{3,2},{4,5},{5,4},{6,7},{7,6},{8,9},{9,8},{10,11... | collective-permute-start | bytes 172040 | tf_op jit(solution)/shard_map/ppermute | solution.py:273
  23.8 4.6 %collective-permute-start.17 = (bf16[4,7168]{1,0:T(4,128)(2,1)S(1)}, bf16[4,7168]{1,0:T(4,128)(2,1)S(1)}, u32[]{:S(2)}, u32[]{:S(2)}) collective-permute-start(bf16[4,7168]{1,0:T(4,128)(2,1)S(1)} %collective-permute-done.15.refs_0_), channel_id=1, source_target_pairs={{0,2},{1,3},{2,0},{3,1},{4,6},{5,7},{6,4},{7,5},{8,10},{9,11},{10,... | collective-permute-start | bytes 172040 | tf_op jit(solution)/shard_map/ppermute | solution.py:273
  26.4 2.6 %collective-permute-start.16 = (bf16[4,7168]{1,0:T(4,128)(2,1)S(1)}, bf16[4,7168]{1,0:T(4,128)(2,1)S(1)}, u32[]{:S(2)}, u32[]{:S(2)}) collective-permute-start(bf16[4,7168]{1,0:T(4,128)(2,1)S(1)} %collective-permute-done.15.refs_0_), channel_id=1, source_target_pairs={{0,1},{1,0},{2,3},{3,2},{4,5},{5,4},{6,7},{7,6},{8,9},{9,8},{10,11... | collective-permute-start | bytes 172040 | tf_op jit(solution)/shard_map/ppermute | solution.py:273
  26.4 4.7 %collective-permute-start.13 = (bf16[4,7168]{1,0:T(4,128)(2,1)S(1)}, bf16[4,7168]{1,0:T(4,128)(2,1)S(1)}, u32[]{:S(2)}, u32[]{:S(2)}) collective-permute-start(bf16[4,7168]{1,0:T(4,128)(2,1)S(1)} %collective-permute-done.11.refs_0_), channel_id=1, source_target_pairs={{0,2},{1,3},{2,0},{3,1},{4,6},{5,7},{6,4},{7,5},{8,10},{9,11},{10,... | collective-permute-start | bytes 172040 | tf_op jit(solution)/shard_map/ppermute | solution.py:273
  27.1 4.8 %collective-permute-start.9 = (bf16[4,7168]{1,0:T(4,128)(2,1)S(1)}, bf16[4,7168]{1,0:T(4,128)(2,1)S(1)}, u32[]{:S(2)}, u32[]{:S(2)}) collective-permute-start(bf16[4,7168]{1,0:T(4,128)(2,1)S(1)} %collective-permute-done.7.refs_0_), channel_id=1, source_target_pairs={{0,2},{1,3},{2,0},{3,1},{4,6},{5,7},{6,4},{7,5},{8,10},{9,11},{10,... | collective-permute-start | bytes 172040 | tf_op jit(solution)/shard_map/ppermute | solution.py:273
  28.4 3.5 %collective-permute-start.6 = (bf16[4,7168]{1,0:T(4,128)(2,1)S(1)}, bf16[4,7168]{1,0:T(4,128)(2,1)S(1)}, u32[]{:S(2)}, u32[]{:S(2)}) collective-permute-start(bf16[4,7168]{1,0:T(4,128)(2,1)S(1)} %collective-permute-done.5.refs_2_), channel_id=1, source_target_pairs={{0,1},{1,0},{2,3},{3,2},{4,5},{5,4},{6,7},{7,6},{8,9},{9,8},{10,11... | collective-permute-start | bytes 172040 | tf_op jit(solution)/shard_map/ppermute | solution.py:273
  28.4 7.1 %collective-permute-start.18 = (bf16[4,7168]{1,0:T(4,128)(2,1)S(1)}, bf16[4,7168]{1,0:T(4,128)(2,1)S(1)}, u32[]{:S(2)}, u32[]{:S(2)}) collective-permute-start(bf16[4,7168]{1,0:T(4,128)(2,1)S(1)} %collective-permute-done.17.refs_2_), channel_id=1, source_target_pairs={{0,1},{1,0},{2,3},{3,2},{4,5},{5,4},{6,7},{7,6},{8,9},{9,8},{10,11... | collective-permute-start | bytes 172040 | tf_op jit(solution)/shard_map/ppermute | solution.py:273
  28.9 7.0 %collective-permute-start.12 = (bf16[4,7168]{1,0:T(4,128)(2,1)S(1)}, bf16[4,7168]{1,0:T(4,128)(2,1)S(1)}, u32[]{:S(2)}, u32[]{:S(2)}) collective-permute-start(bf16[4,7168]{1,0:T(4,128)(2,1)S(1)} %collective-permute-done.11.refs_0_), channel_id=1, source_target_pairs={{0,1},{1,0},{2,3},{3,2},{4,5},{5,4},{6,7},{7,6},{8,9},{9,8},{10,11... | collective-permute-start | bytes 172040 | tf_op jit(solution)/shard_map/ppermute | solution.py:273
  31.1 4.8 %collective-permute-start.14 = (bf16[4,7168]{1,0:T(4,128)(2,1)S(1)}, bf16[4,7168]{1,0:T(4,128)(2,1)S(1)}, u32[]{:S(2)}, u32[]{:S(2)}) collective-permute-start(bf16[4,7168]{1,0:T(4,128)(2,1)S(1)} %collective-permute-done.13.refs_2_), channel_id=1, source_target_pairs={{0,1},{1,0},{2,3},{3,2},{4,5},{5,4},{6,7},{7,6},{8,9},{9,8},{10,11... | collective-permute-start | bytes 172040 | tf_op jit(solution)/shard_map/ppermute | solution.py:273
  31.9 4.3 %collective-permute-start.8 = (bf16[4,7168]{1,0:T(4,128)(2,1)S(1)}, bf16[4,7168]{1,0:T(4,128)(2,1)S(1)}, u32[]{:S(2)}, u32[]{:S(2)}) collective-permute-start(bf16[4,7168]{1,0:T(4,128)(2,1)S(1)} %collective-permute-done.7.refs_0_), channel_id=1, source_target_pairs={{0,1},{1,0},{2,3},{3,2},{4,5},{5,4},{6,7},{7,6},{8,9},{9,8},{10,11... | collective-permute-start | bytes 172040 | tf_op jit(solution)/shard_map/ppermute | solution.py:273
  31.9 4.3 %collective-permute-start.10 = (bf16[4,7168]{1,0:T(4,128)(2,1)S(1)}, bf16[4,7168]{1,0:T(4,128)(2,1)S(1)}, u32[]{:S(2)}, u32[]{:S(2)}) collective-permute-start(bf16[4,7168]{1,0:T(4,128)(2,1)S(1)} %collective-permute-done.9.refs_2_), channel_id=1, source_target_pairs={{0,1},{1,0},{2,3},{3,2},{4,5},{5,4},{6,7},{7,6},{8,9},{9,8},{10,11... | collective-permute-start | bytes 172040 | tf_op jit(solution)/shard_map/ppermute | solution.py:273
  32.5 1.2 %copy-start = (s32[56,4096]{1,0:T(8,128)S(1)}, s32[56,4096]{1,0:T(8,128)}, u32[]{:S(2)}) copy-start(s32[56,4096]{1,0:T(8,128)} %delay_ref.1) | copy-start | bytes 2752516
  33.6 0.7 %copy-start.1 = (s32[56]{0:T(128)S(1)}, s32[56]{0:T(128)}, u32[]{:S(2)}) copy-start(s32[56]{0:T(128)} %offset_ref.1) | copy-start | bytes 676
  40.8 6.4 %collective-permute-start.20 = (bf16[32,2048]{1,0:T(8,128)(2,1)S(1)}, bf16[32,2048]{1,0:T(8,128)(2,1)S(1)}, u32[]{:S(2)}, u32[]{:S(2)}) collective-permute-start(bf16[32,2048]{1,0:T(8,128)(2,1)S(1)} %get-tuple-element.28), channel_id=1, source_target_pairs={{0,16},{16,0},{1,17},{17,1},{2,18},{18,2},{3,19},{19,3},{4,20},{20... | collective-permute-start | bytes 393224 | tf_op jit(solution)/shard_map/ppermute | solution.py:273
  41.4 7.7 %collective-permute-start.19 = (bf16[32,2048]{1,0:T(8,128)(2,1)S(1)}, bf16[32,2048]{1,0:T(8,128)(2,1)S(1)}, u32[]{:S(2)}, u32[]{:S(2)}) collective-permute-start(bf16[32,2048]{1,0:T(8,128)(2,1)S(1)} %get-tuple-element.26), channel_id=1, source_target_pairs={{0,16},{16,0},{1,17},{17,1},{2,18},{18,2},{3,19},{19,3},{4,20},{20... | collective-permute-start | bytes 393224 | tf_op jit(solution)/shard_map/ppermute | solution.py:273

commit v3 on v2

--- a/solution.py
+++ b/solution.py
@@ -182,11 +182,12 @@
     )(timing_offsets, sample_delays)
 
 
-def image_kernel(swap, parts, target_ref, *refs):
+def image_kernel(swap, parts, start, target_ref, *refs):
     piece_refs, scale_refs = refs[:parts], refs[parts : 2 * parts]
     *out_refs, sums_ref = refs[2 * parts :]
     rows = piece_refs[0].shape[0]
-    stations, tile, voxels = target_ref.shape
+    stations, tile, _ = target_ref.shape
+    voxels = sums_ref.shape[1]
     level = (lax.broadcasted_iota(jnp.int32, (LAGS, voxels), 0) - HALF).astype(jnp.int8)
     one = jnp.ones((LAGS, voxels), F8)
     zero = jnp.zeros((LAGS, voxels), F8)
@@ -194,7 +195,7 @@
     for s0 in range(0, stations, 2):
         hots = []
         for s in range(s0, min(s0 + 2, stations)):
-            target = jnp.concatenate([target_ref[s]] * (LAGS // tile), axis=0)
+            target = jnp.concatenate([target_ref[s, :, start : start + voxels]] * (LAGS // tile), axis=0)
             hots.append(jnp.where(level == target, one, zero))
         hot = jnp.concatenate(hots, axis=0) if len(hots) > 1 else hots[0]
         at = LAGS * s0
@@ -211,8 +212,11 @@
     first = lax.broadcasted_iota(jnp.int32, (8, voxels), 0) < 4
     lower = None
     for j in range(0, groups, 2):
-        here = sums_ref[pl.ds(pl.multiple_of(8 * (mine ^ j), 8), 8), :]
-        there = sums_ref[pl.ds(pl.multiple_of(8 * (mine ^ (j + 1)), 8), 8), :]
+        here, there = mine ^ j, mine ^ (j + 1)
+        if swap:
+            here, there = [(d & 3) * 4 + d // 4 for d in (here, there)]
+        here = sums_ref[pl.ds(pl.multiple_of(8 * here, 8), 8), :]
+        there = sums_ref[pl.ds(pl.multiple_of(8 * there, 8), 8), :]
         value = jnp.where(
             first,
             here + pltpu.roll(here, 4, 0),
@@ -230,11 +234,9 @@
             lower = None
 
 
-def image(pieces, scales, target, swap, part, count):
+def image(pieces, scales, target, swap, start, voxels):
     rows, columns = pieces[0].shape
     total = len(pieces) * rows // 2
-    stations, tile, voxels = target.shape
-    voxels = voxels // count
     if swap:
         out_shape = [
             jax.ShapeDtypeStruct((total // 2, voxels), jnp.float32),
@@ -243,11 +245,9 @@
     else:
         out_shape = [jax.ShapeDtypeStruct((total, voxels), jnp.float32)]
     return pl.pallas_call(
-        functools.partial(image_kernel, swap, len(pieces)),
-        grid=(1,),
+        functools.partial(image_kernel, swap, len(pieces), start),
         out_shape=out_shape,
-        in_specs=[pl.BlockSpec((stations, tile, voxels), lambda i: (0, 0, part))]
-        + [VMEM] * (2 * len(pieces)),
+        in_specs=[VMEM] * (1 + 2 * len(pieces)),
         out_specs=[VMEM] * len(out_shape),
         scratch_shapes=[pltpu.VMEM((2 * total, voxels), jnp.float32)],
         cost_estimate=pl.CostEstimate(
@@ -278,22 +278,12 @@
     odd = lax.axis_index("vox") % 2 == 1
     first, last = candidate[:, :HALF], candidate[:, candidate.shape[1] - HALF :]
     steps = [(b, b + 1) for b in range(1, count - 1, 2)] + [(b + 1, b) for b in range(1, count - 1, 2)]
-    outer = jnp.where(odd, last, first)
-    here = lax.ppermute(outer, "vox", steps)
-    cross = [
-        (x * count + source, (1 - x) * count + target) for x in range(2) for source, target in steps
-    ]
-    there = lax.ppermute(outer, ("stn", "vox"), cross)
+    outer = lax.ppermute(jnp.where(odd, last, first), "vox", steps)
     inner = flip(jnp.where(odd, first, last), "vox", 1)
-    wide = jnp.concatenate([candidate, inner], axis=1)
-    other = flip(wide, "stn", 1)
-    mine = lax.axis_index("stn") == owner
-    wide = jnp.where(mine, wide, other)
-    outer = jnp.where(mine, here, there)
-    body, inner = wide[:, : candidate.shape[1]], wide[:, candidate.shape[1] :]
-    return jnp.concatenate(
-        [jnp.where(odd, inner, outer), body, jnp.where(odd, outer, inner)], axis=1
-    )
+    low, high = jnp.where(odd, inner, outer), jnp.where(odd, outer, inner)
+    extended = jnp.concatenate([low, candidate, high], axis=1)
+    other = flip(extended, "stn", 1)
+    return jnp.where(lax.axis_index("stn") == owner, extended, other)
 
 
 def extend(candidate, owner):
@@ -313,12 +303,16 @@
         blocks[d] = flip(block, "vox", d)
     for d in (0, 4, 8, 12):
         blocks[d | 2] = flip(blocks[d], "vox", 2)
-    for d in (0, 2, 4, 6, 8, 10, 12, 14):
+    for d in (0, 4, 8, 12, 2, 6):
         blocks[d | 1] = flip(blocks[d], "vox", 1)
-    return [[blocks[d] for d in order] for order in ORDER]
-
-
-ORDER = ((0, 1, 2, 3), (4, 5, 6, 7), (8, 9, 10, 11), (12, 13, 14, 15))
+    done = [split([blocks[d] for d in order]) for order in ORDER[:2]]
+    blocks[10], blocks[14], done = lax.optimization_barrier((blocks[10], blocks[14], done))
+    for d in (10, 14):
+        blocks[d | 1] = flip(blocks[d], "vox", 1)
+    return done + [split([blocks[d] for d in order]) for order in ORDER[2:]]
+
+
+ORDER = ((0, 4, 8, 12), (1, 5, 9, 13), (2, 6, 10, 14), (3, 7, 11, 15))
 
 
 def shards(voltages, sample_delays, timing_offsets, reference_station):
@@ -338,25 +332,29 @@
     ).astype(jnp.bfloat16)
     windowed = jnp.transpose(windowed.reshape(stations_here, pols, samples_here), (1, 0, 2))
 
+    target = targets(sample_delays, timing_offsets, stations_here)
+    extended, target = lax.optimization_barrier((extended, target))
     corr = correlate(windowed, extended, reference_station)
-    target = targets(sample_delays, timing_offsets, stations_here)
     if swap:
-        groups = gather_paired(corr)
+        pairs = gather_paired(corr)
     else:
         gathered = lax.all_gather(corr, "vox", axis=0, tiled=False)
         mine = lax.axis_index("vox")
         every = [
             lax.dynamic_index_in_dim(gathered, mine ^ j, 0, keepdims=False) for j in range(count)
         ]
-        groups = [every[j : j + 4] for j in range(0, count, 4)]
-    pieces, scales = zip(*[split(blocks) for blocks in groups], strict=True)
+        pairs = [split(every[j : j + 4]) for j in range(0, count, 4)]
+    pieces, scales = zip(*pairs, strict=True)
     if not swap:
-        (partial,) = image(pieces, scales, target, False, 0, 1)
+        (partial,) = image(pieces, scales, target, False, 0, sample_delays.shape[1])
         return lax.psum_scatter(partial, "stn", scatter_dimension=0, tiled=True)
     operands = []
-    for part in range(PARTS):
-        kept, sent = image(pieces, scales, target, True, part, PARTS)
+    start = 0
+    for share in SHARES:
+        voxels = sample_delays.shape[1] * share // sum(SHARES)
+        kept, sent = image(pieces, scales, target, True, start, voxels)
         operands += [kept, flip(sent, "stn", 1)]
+        start += voxels
     return pl.pallas_call(
         add_kernel,
         out_shape=jax.ShapeDtypeStruct((operands[0].shape[0], sample_delays.shape[1]), jnp.float32),
@@ -366,7 +364,7 @@
     )(*operands)
 
 
-PARTS = 2
+SHARES = (9, 7)
 
 
 def solution(mesh):

time: 50.3 us -> 46 us (0.915)
  waiting for transfers between devices: 13.3 us -> 11.1 us
  starting transfers between devices: 21.7 us -> 19.7 us
    ppermute x19, waiting for transfers between devices: 13.3 us -> 11.1 us  [flip(): return lax.ppermute(block, axis, [(i, i ^ mask) for i in range(count)])]
    ppermute x19, starting transfers between devices: 20.4 us -> 19 us  [flip(): return lax.ppermute(block, axis, [(i, i ^ mask) for i in range(count)])]
    ppermute x2 -> x1, starting transfers between devices: 1.32 us -> 0.65 us  [extend_paired(): outer = lax.ppermute(jnp.where(odd, last, first), 'vox', steps)]
  transfers between devices with their start and end apart: 21 -> 20, of which waited for: 8 -> 9; matrix products, arithmetic and copies ran while one was open for 4% -> 4% of each run, Pallas kernels for 4% -> 8%
where the time goes in v3:
time: 46 us; the launch traced here: 45.7 us
  starting transfers between devices  19.7 us (43%)
  waiting for transfers between devices  11.1 us (24%)
  Pallas kernels  9.38 us (20%)
  local copies, waits for them, and re-layouts  3.26 us (7%)
  other arithmetic  1.35 us (3%)
  between operations  0.86 us (2%)
    ppermute x19, starting transfers between devices, flip(): return lax.ppermute(block, axis, [(i, i ^ mask) for i in range(count)])  19 us
    ppermute x19, waiting for transfers between devices, flip(): return lax.ppermute(block, axis, [(i, i ^ mask) for i in range(count)])  11.1 us
    pallas_call x2, Pallas kernels, image(): pl.pallas_call(functools.partial(image_kernel, swap, len(pieces), start),...  4.25 us
    unnamed x6, local copies, waits for them, and re-layouts  2.53 us
    pallas_call x1, Pallas kernels, correlate(): pl.pallas_call(functools.partial(corr_kernel, norm_inverse()), out_shape=...  2.1 us
    transpose x1, other arithmetic, shards(): jnp.transpose(windowed.reshape(stations_here, pols, samples_here), (1, 0,...  1.29 us
    pallas_call x4, Pallas kernels, split(): pl.pallas_call(split_kernel, out_shape=[jax.ShapeDtypeStruct((rows, colum...  1.24 us
    pallas_call x1, Pallas kernels, targets(): pl.pallas_call(target_kernel, out_shape=jax.ShapeDtypeStruct((stations, 3...  0.95 us
  transfers between devices with their start and end apart: 20, of which 9 were waited for; matrix products, arithmetic and copies ran while one was open for 4% of the time, Pallas kernels for 8%

profile of v3, /device:TPU:0, one launch (start us, length us, event | category | flops | bytes accessed | tf_op | source)
XLA Modules:
  0.0 45.7 jit_solution(1012649729803745594)
XLA Ops:
  0.7 0.7 %dynamic-slice_bitcast_fusion = bf16[2,4096]{1,0:T(2,128)(2,1)S(1)} fusion(bf16[28,2,4096]{2,1,0:T(2,128)(2,1)} %param.5, s32[]{:T(128)S(6)} %select_n.52), kind=kLoop, calls=%fused_computation.5 | loop fusion | bytes 32772 | tf_op jit(solution)/shard_map/jit(dynamic_index_in_dim)/squeeze | solution.py:326
  1.4 0.5 %collective-permute-start = (bf16[2,128]{1,0:T(2,128)(2,1)S(1)}, bf16[2,128]{1,0:T(2,128)(2,1)S(1)}, u32[]{:S(2)}, u32[]{:S(2)}) collective-permute-start(bf16[2,128]{1,0:T(2,128)(2,1)S(1)} %get-tuple-element.45), channel_id=1, source_target_pairs={{0,1},{1,0},{2,3},{3,2},{4,5},{5,4},{6,7},{7,6},{8,9},{9,8},{10,11... | collective-permute-start | bytes 1544 | tf_op jit(solution)/shard_map/ppermute | solution.py:273
  1.9 0.6 %collective-permute-start.1 = (bf16[2,128]{1,0:T(2,128)(2,1)S(1)}, bf16[2,128]{1,0:T(2,128)(2,1)S(1)}, u32[]{:S(2)}, u32[]{:S(2)}) collective-permute-start(bf16[2,128]{1,0:T(2,128)(2,1)S(1)} %get-tuple-element.46), channel_id=1, source_target_pairs={{1,2},{3,4},{5,6},{7,8},{9,10},{11,12},{13,14},{2,1},{4,3},{6,5},{... | collective-permute-start | bytes 1544 | tf_op jit(solution)/shard_map/ppermute | solution.py:281
  2.6 0.7 %broadcast_bitcast_fusion = f32[1,8,4,128]{3,2,1,0:T(4,128)S(1)} fusion(f32[1024]{0:T(1024)} %constant.48.clone), kind=kLoop, calls=%fused_computation.6 | loop fusion | bytes 20480
  3.4 2.6 %collective-permute-start.2 = (bf16[2,4352]{1,0:T(2,128)(2,1)S(1)}, bf16[2,4352]{1,0:T(2,128)(2,1)S(1)}, u32[]{:S(2)}, u32[]{:S(2)}) collective-permute-start(bf16[2,4352]{1,0:T(2,128)(2,1)S(1)} %pad_maximum_fusion), channel_id=1, source_target_pairs={{0,16},{16,0},{1,17},{17,1},{2,18},{18,2},{3,19},{19,3},{4,20},{20... | collective-permute-start | bytes 52232 | tf_op jit(solution)/shard_map/ppermute | solution.py:273
  5.9 1.3 %fusion.win_ref = bf16[2,28,4096]{2,1,0:T(8,128)(2,1)S(1)} fusion(bf16[28,2,4096]{2,1,0:T(2,128)(2,1)} %param.5, f32[4096]{0:T(1024)S(1)} %bitcast.12), kind=kLoop, calls=%fused_computation.1 | loop fusion | flops 688128 | bytes 933888 | tf_op jit(solution)/shard_map/transpose | solution.py:333
  7.3 1.2 %copy-done = s32[56,4096]{1,0:T(8,128)S(1)} copy-done((s32[56,4096]{1,0:T(8,128)S(1)}, s32[56,4096]{1,0:T(8,128)}, u32[]{:S(2)}) %copy-start) | copy-done | bytes 917528
  8.4 0.7 %copy-done.1 = s32[56]{0:T(128)S(1)} copy-done((s32[56]{0:T(128)S(1)}, s32[56]{0:T(128)}, u32[]{:S(2)}) %copy-start.1) | copy-done | bytes 248
  9.1 1.0 %shard_map.55.target_ref = s8[28,32,4096]{2,1,0:T(32,128)(4,1)S(1)} custom-call(s32[56]{0:T(128)S(1)} %copy-done.1, s32[56,4096]{1,0:T(8,128)S(1)} %copy-done), custom_call_target="tpu_custom_call" | custom-call | flops 3670016 | bytes 4128768 | tf_op jit(solution)/shard_map/pallas_call | solution.py:173
  10.1 2.1 %shard_map.56.refs_0_ = bf16[4,7168]{1,0:T(4,128)(2,1)S(1)} custom-call(s32[1]{0:T(128)S(6)} %copy.11.ref_ref, bf16[2,28,4096]{2,1,0:T(8,128)(2,1)S(1)} %fusion.win_ref, bf16[2,4352]{1,0:T(2,128)(2,1)S(1)} %broadcast_select_fusion.ext_ref), custom_call_target="tpu_custom_call" | custom-call | flops 117440512 | bytes 458752 | tf_op jit(solution)/shard_map/pallas_call | solution.py:108
  12.2 7.0 %collective-permute-start.3 = (bf16[4,7168]{1,0:T(4,128)(2,1)S(1)}, bf16[4,7168]{1,0:T(4,128)(2,1)S(1)}, u32[]{:S(2)}, u32[]{:S(2)}) collective-permute-start(bf16[4,7168]{1,0:T(4,128)(2,1)S(1)} %shard_map.56.refs_0_), channel_id=1, source_target_pairs={{0,8},{1,9},{2,10},{3,11},{4,12},{5,13},{6,14},{7,15},{8,0},{9,1},... | collective-permute-start | bytes 172040 | tf_op jit(solution)/shard_map/ppermute | solution.py:273
  19.2 1.4 %collective-permute-start.5 = (bf16[4,7168]{1,0:T(4,128)(2,1)S(1)}, bf16[4,7168]{1,0:T(4,128)(2,1)S(1)}, u32[]{:S(2)}, u32[]{:S(2)}) collective-permute-start(bf16[4,7168]{1,0:T(4,128)(2,1)S(1)} %shard_map.56.refs_0_), channel_id=1, source_target_pairs={{0,12},{1,13},{2,14},{3,15},{4,8},{5,9},{6,10},{7,11},{8,4},{9,5},... | collective-permute-start | bytes 172040 | tf_op jit(solution)/shard_map/ppermute | solution.py:273
  20.8 0.9 %collective-permute-start.12 = (bf16[4,7168]{1,0:T(4,128)(2,1)S(1)}, bf16[4,7168]{1,0:T(4,128)(2,1)S(1)}, u32[]{:S(2)}, u32[]{:S(2)}) collective-permute-start(bf16[4,7168]{1,0:T(4,128)(2,1)S(1)} %shard_map.56.refs_0_), channel_id=1, source_target_pairs={{0,2},{1,3},{2,0},{3,1},{4,6},{5,7},{6,4},{7,5},{8,10},{9,11},{10,... | collective-permute-start | bytes 172040 | tf_op jit(solution)/shard_map/ppermute | solution.py:273
  21.8 3.6 %collective-permute-done.5.refs_3_ = bf16[4,7168]{1,0:T(4,128)(2,1)S(1)} collective-permute-done((bf16[4,7168]{1,0:T(4,128)(2,1)S(1)}, bf16[4,7168]{1,0:T(4,128)(2,1)S(1)}, u32[]{:S(2)}, u32[]{:S(2)}) %collective-permute-start.5) | collective-permute-done | bytes 57376 | tf_op jit(solution)/shard_map/ppermute | solution.py:273
  25.4 0.5 collective-permute-start.9
  25.8 1.2 %collective-permute-start.4 = (bf16[4,7168]{1,0:T(4,128)(2,1)S(1)}, bf16[4,7168]{1,0:T(4,128)(2,1)S(1)}, u32[]{:S(2)}, u32[]{:S(2)}) collective-permute-start(bf16[4,7168]{1,0:T(4,128)(2,1)S(1)} %collective-permute-done.3.refs_2_), channel_id=1, source_target_pairs={{0,2},{1,3},{2,0},{3,1},{4,6},{5,7},{6,4},{7,5},{8,10},{9,11},{10,... | collective-permute-start | bytes 172040 | tf_op jit(solution)/shard_map/ppermute | solution.py:273
  27.0 0.9 %collective-permute-start.6 = (bf16[4,7168]{1,0:T(4,128)(2,1)S(1)}, bf16[4,7168]{1,0:T(4,128)(2,1)S(1)}, u32[]{:S(2)}, u32[]{:S(2)}) collective-permute-start(bf16[4,7168]{1,0:T(4,128)(2,1)S(1)} %collective-permute-done.5.refs_3_), channel_id=1, source_target_pairs={{0,2},{1,3},{2,0},{3,1},{4,6},{5,7},{6,4},{7,5},{8,10},{9,11},{10,... | collective-permute-start | bytes 172040 | tf_op jit(solution)/shard_map/ppermute | solution.py:273
  27.9 1.2 %collective-permute-start.13 = (bf16[4,7168]{1,0:T(4,128)(2,1)S(1)}, bf16[4,7168]{1,0:T(4,128)(2,1)S(1)}, u32[]{:S(2)}, u32[]{:S(2)}) collective-permute-start(bf16[4,7168]{1,0:T(4,128)(2,1)S(1)} %collective-permute-done.7.refs_1_), channel_id=1, source_target_pairs={{0,2},{1,3},{2,0},{3,1},{4,6},{5,7},{6,4},{7,5},{8,10},{9,11},{10,... | collective-permute-start | bytes 172040 | tf_op jit(solution)/shard_map/ppermute | solution.py:273
  29.1 0.3 shard_map.57
  29.5 0.3 shard_map.58
  29.8 0.6 %collective-permute-done.4.refs_2_ = bf16[4,7168]{1,0:T(4,128)(2,1)S(1)} collective-permute-done((bf16[4,7168]{1,0:T(4,128)(2,1)S(1)}, bf16[4,7168]{1,0:T(4,128)(2,1)S(1)}, u32[]{:S(2)}, u32[]{:S(2)}) %collective-permute-start.4) | collective-permute-done | bytes 57376 | tf_op jit(solution)/shard_map/ppermute | solution.py:273
  30.4 1.4 %collective-permute-done.6.refs_3_ = bf16[4,7168]{1,0:T(4,128)(2,1)S(1)} collective-permute-done((bf16[4,7168]{1,0:T(4,128)(2,1)S(1)}, bf16[4,7168]{1,0:T(4,128)(2,1)S(1)}, u32[]{:S(2)}, u32[]{:S(2)}) %collective-permute-start.6) | collective-permute-done | bytes 57376 | tf_op jit(solution)/shard_map/ppermute | solution.py:273
  31.8 0.5 %collective-permute-start.17 = (bf16[4,7168]{1,0:T(4,128)(2,1)S(1)}, bf16[4,7168]{1,0:T(4,128)(2,1)S(1)}, u32[]{:S(2)}, u32[]{:S(2)}) collective-permute-start(bf16[4,7168]{1,0:T(4,128)(2,1)S(1)} %collective-permute-done.6.refs_3_), channel_id=1, source_target_pairs={{0,1},{1,0},{2,3},{3,2},{4,5},{5,4},{6,7},{7,6},{8,9},{9,8},{10,11... | collective-permute-start | bytes 172040 | tf_op jit(solution)/shard_map/ppermute | solution.py:273
  32.5 0.3 shard_map.59
  33.2 0.5 %collective-permute-done.15.refs_1_ = bf16[4,7168]{1,0:T(4,128)(2,1)S(1)} collective-permute-done((bf16[4,7168]{1,0:T(4,128)(2,1)S(1)}, bf16[4,7168]{1,0:T(4,128)(2,1)S(1)}, u32[]{:S(2)}, u32[]{:S(2)}) %collective-permute-start.15) | collective-permute-done | bytes 57376 | tf_op jit(solution)/shard_map/ppermute | solution.py:273
  33.7 0.3 shard_map.60
  34.0 2.4 %shard_map.61 = (f32[32,2304]{1,0:T(8,128)S(1)}, bf16[32,2304]{1,0:T(8,128)(2,1)S(1)}) custom-call(s8[28,32,4096]{2,1,0:T(32,128)(4,1)S(1)} %shard_map.55.target_ref, f8e4m3fn[32,7168]{1,0:T(32,128)(4,1)S(1)} %get-tuple-element.31.refs_0_, f8e4m3fn[32,7168]{1,0:T(32,128)(4,1)S(1)} %get-tuple-element.32.refs_1_, ...), custom_call_target="tpu_custom_call" | custom-call | flops 4227858432 | bytes 589824 | tf_op jit(solution)/shard_map/pallas_call | solution.py:247
  36.4 0.6 %collective-permute-start.18 = (bf16[32,2304]{1,0:T(8,128)(2,1)S(1)}, bf16[32,2304]{1,0:T(8,128)(2,1)S(1)}, u32[]{:S(2)}, u32[]{:S(2)}) collective-permute-start(bf16[32,2304]{1,0:T(8,128)(2,1)S(1)} %get-tuple-element.42), channel_id=1, source_target_pairs={{0,16},{16,0},{1,17},{17,1},{2,18},{18,2},{3,19},{19,3},{4,20},{20... | collective-permute-start | bytes 442376 | tf_op jit(solution)/shard_map/ppermute | solution.py:273
  37.0 1.9 %shard_map.62 = (f32[32,1792]{1,0:T(8,128)S(1)}, bf16[32,1792]{1,0:T(8,128)(2,1)S(1)}) custom-call(s8[28,32,4096]{2,1,0:T(32,128)(4,1)S(1)} %shard_map.55.target_ref, f8e4m3fn[32,7168]{1,0:T(32,128)(4,1)S(1)} %get-tuple-element.31.refs_0_, f8e4m3fn[32,7168]{1,0:T(32,128)(4,1)S(1)} %get-tuple-element.32.refs_1_, ...), custom_call_target="tpu_custom_call" | custom-call | flops 3288334336 | bytes 458752 | tf_op jit(solution)/shard_map/pallas_call | solution.py:247
  38.9 1.6 %collective-permute-start.19 = (bf16[32,1792]{1,0:T(8,128)(2,1)S(1)}, bf16[32,1792]{1,0:T(8,128)(2,1)S(1)}, u32[]{:S(2)}, u32[]{:S(2)}) collective-permute-start(bf16[32,1792]{1,0:T(8,128)(2,1)S(1)} %get-tuple-element.44), channel_id=1, source_target_pairs={{0,16},{16,0},{1,17},{17,1},{2,18},{18,2},{3,19},{19,3},{4,20},{20... | collective-permute-start | bytes 344072 | tf_op jit(solution)/shard_map/ppermute | solution.py:273
  40.4 4.4 %collective-permute-done.19.refs_3_ = bf16[32,1792]{1,0:T(8,128)(2,1)S(1)} collective-permute-done((bf16[32,1792]{1,0:T(8,128)(2,1)S(1)}, bf16[32,1792]{1,0:T(8,128)(2,1)S(1)}, u32[]{:S(2)}, u32[]{:S(2)}) %collective-permute-start.19) | collective-permute-done | bytes 114720 | tf_op jit(solution)/shard_map/ppermute | solution.py:273
  44.8 0.8 %shard_map.63 = f32[32,4096]{1,0:T(8,128)} custom-call(f32[32,2304]{1,0:T(8,128)S(1)} %get-tuple-element.41.refs_0_, bf16[32,2304]{1,0:T(8,128)(2,1)S(1)} %collective-permute-done.18.refs_1_, f32[32,1792]{1,0:T(8,128)S(1)} %get-tuple-element.43.refs_2_, bf16[32,1792]{1,0:T(8,128)(2,1)S(1)} %collective-permute-done.19.refs_3_), custom_call_target="tpu_custom_call" | custom-call | tf_op jit(solution)/shard_map/pallas_call | solution.py:358
  (29 shorter events, 1.0 us)
Async XLA Ops:
  1.4 1.9 %collective-permute-start = (bf16[2,128]{1,0:T(2,128)(2,1)S(1)}, bf16[2,128]{1,0:T(2,128)(2,1)S(1)}, u32[]{:S(2)}, u32[]{:S(2)}) collective-permute-start(bf16[2,128]{1,0:T(2,128)(2,1)S(1)} %get-tuple-element.45), channel_id=1, source_target_pairs={{0,1},{1,0},{2,3},{3,2},{4,5},{5,4},{6,7},{7,6},{8,9},{9,8},{10,11... | collective-permute-start | bytes 1544 | tf_op jit(solution)/shard_map/ppermute | solution.py:273
  1.9 1.4 %collective-permute-start.1 = (bf16[2,128]{1,0:T(2,128)(2,1)S(1)}, bf16[2,128]{1,0:T(2,128)(2,1)S(1)}, u32[]{:S(2)}, u32[]{:S(2)}) collective-permute-start(bf16[2,128]{1,0:T(2,128)(2,1)S(1)} %get-tuple-element.46), channel_id=1, source_target_pairs={{1,2},{3,4},{5,6},{7,8},{9,10},{11,12},{13,14},{2,1},{4,3},{6,5},{... | collective-permute-start | bytes 1544 | tf_op jit(solution)/shard_map/ppermute | solution.py:281
  3.4 6.7 %collective-permute-start.2 = (bf16[2,4352]{1,0:T(2,128)(2,1)S(1)}, bf16[2,4352]{1,0:T(2,128)(2,1)S(1)}, u32[]{:S(2)}, u32[]{:S(2)}) collective-permute-start(bf16[2,4352]{1,0:T(2,128)(2,1)S(1)} %pad_maximum_fusion), channel_id=1, source_target_pairs={{0,16},{16,0},{1,17},{17,1},{2,18},{18,2},{3,19},{19,3},{4,20},{20... | collective-permute-start | bytes 52232 | tf_op jit(solution)/shard_map/ppermute | solution.py:273
  7.3 1.2 %copy-start = (s32[56,4096]{1,0:T(8,128)S(1)}, s32[56,4096]{1,0:T(8,128)}, u32[]{:S(2)}) copy-start(s32[56,4096]{1,0:T(8,128)} %delay_ref.1) | copy-start | bytes 2752516
  8.4 0.7 %copy-start.1 = (s32[56]{0:T(128)S(1)}, s32[56]{0:T(128)}, u32[]{:S(2)}) copy-start(s32[56]{0:T(128)} %offset_ref.1) | copy-start | bytes 676
  12.2 9.5 %collective-permute-start.3 = (bf16[4,7168]{1,0:T(4,128)(2,1)S(1)}, bf16[4,7168]{1,0:T(4,128)(2,1)S(1)}, u32[]{:S(2)}, u32[]{:S(2)}) collective-permute-start(bf16[4,7168]{1,0:T(4,128)(2,1)S(1)} %shard_map.56.refs_0_), channel_id=1, source_target_pairs={{0,8},{1,9},{2,10},{3,11},{4,12},{5,13},{6,14},{7,15},{8,0},{9,1},... | collective-permute-start | bytes 172040 | tf_op jit(solution)/shard_map/ppermute | solution.py:273
  19.2 6.1 %collective-permute-start.5 = (bf16[4,7168]{1,0:T(4,128)(2,1)S(1)}, bf16[4,7168]{1,0:T(4,128)(2,1)S(1)}, u32[]{:S(2)}, u32[]{:S(2)}) collective-permute-start(bf16[4,7168]{1,0:T(4,128)(2,1)S(1)} %shard_map.56.refs_0_), channel_id=1, source_target_pairs={{0,12},{1,13},{2,14},{3,15},{4,8},{5,9},{6,10},{7,11},{8,4},{9,5},... | collective-permute-start | bytes 172040 | tf_op jit(solution)/shard_map/ppermute | solution.py:273
  20.6 4.8 %collective-permute-start.7 = (bf16[4,7168]{1,0:T(4,128)(2,1)S(1)}, bf16[4,7168]{1,0:T(4,128)(2,1)S(1)}, u32[]{:S(2)}, u32[]{:S(2)}) collective-permute-start(bf16[4,7168]{1,0:T(4,128)(2,1)S(1)} %shard_map.56.refs_0_), channel_id=1, source_target_pairs={{0,4},{1,5},{2,6},{3,7},{4,0},{5,1},{6,2},{7,3},{8,12},{9,13},{10,... | collective-permute-start | bytes 172040 | tf_op jit(solution)/shard_map/ppermute | solution.py:273
  20.8 5.0 %collective-permute-start.8 = (bf16[4,7168]{1,0:T(4,128)(2,1)S(1)}, bf16[4,7168]{1,0:T(4,128)(2,1)S(1)}, u32[]{:S(2)}, u32[]{:S(2)}) collective-permute-start(bf16[4,7168]{1,0:T(4,128)(2,1)S(1)} %shard_map.56.refs_0_), channel_id=1, source_target_pairs={{0,1},{1,0},{2,3},{3,2},{4,5},{5,4},{6,7},{7,6},{8,9},{9,8},{10,11... | collective-permute-start | bytes 172040 | tf_op jit(solution)/shard_map/ppermute | solution.py:273
  20.8 6.2 %collective-permute-start.12 = (bf16[4,7168]{1,0:T(4,128)(2,1)S(1)}, bf16[4,7168]{1,0:T(4,128)(2,1)S(1)}, u32[]{:S(2)}, u32[]{:S(2)}) collective-permute-start(bf16[4,7168]{1,0:T(4,128)(2,1)S(1)} %shard_map.56.refs_0_), channel_id=1, source_target_pairs={{0,2},{1,3},{2,0},{3,1},{4,6},{5,7},{6,4},{7,5},{8,10},{9,11},{10,... | collective-permute-start | bytes 172040 | tf_op jit(solution)/shard_map/ppermute | solution.py:273
  21.7 6.1 %collective-permute-start.10 = (bf16[4,7168]{1,0:T(4,128)(2,1)S(1)}, bf16[4,7168]{1,0:T(4,128)(2,1)S(1)}, u32[]{:S(2)}, u32[]{:S(2)}) collective-permute-start(bf16[4,7168]{1,0:T(4,128)(2,1)S(1)} %collective-permute-done.3.refs_2_), channel_id=1, source_target_pairs={{0,1},{1,0},{2,3},{3,2},{4,5},{5,4},{6,7},{7,6},{8,9},{9,8},{10,11... | collective-permute-start | bytes 172040 | tf_op jit(solution)/shard_map/ppermute | solution.py:273
  25.3 4.1 %collective-permute-start.11 = (bf16[4,7168]{1,0:T(4,128)(2,1)S(1)}, bf16[4,7168]{1,0:T(4,128)(2,1)S(1)}, u32[]{:S(2)}, u32[]{:S(2)}) collective-permute-start(bf16[4,7168]{1,0:T(4,128)(2,1)S(1)} %collective-permute-done.5.refs_3_), channel_id=1, source_target_pairs={{0,1},{1,0},{2,3},{3,2},{4,5},{5,4},{6,7},{7,6},{8,9},{9,8},{10,11... | collective-permute-start | bytes 172040 | tf_op jit(solution)/shard_map/ppermute | solution.py:273
  25.4 4.1 %collective-permute-start.9 = (bf16[4,7168]{1,0:T(4,128)(2,1)S(1)}, bf16[4,7168]{1,0:T(4,128)(2,1)S(1)}, u32[]{:S(2)}, u32[]{:S(2)}) collective-permute-start(bf16[4,7168]{1,0:T(4,128)(2,1)S(1)} %collective-permute-done.7.refs_1_), channel_id=1, source_target_pairs={{0,1},{1,0},{2,3},{3,2},{4,5},{5,4},{6,7},{7,6},{8,9},{9,8},{10,11... | collective-permute-start | bytes 172040 | tf_op jit(solution)/shard_map/ppermute | solution.py:273
  25.8 4.6 %collective-permute-start.4 = (bf16[4,7168]{1,0:T(4,128)(2,1)S(1)}, bf16[4,7168]{1,0:T(4,128)(2,1)S(1)}, u32[]{:S(2)}, u32[]{:S(2)}) collective-permute-start(bf16[4,7168]{1,0:T(4,128)(2,1)S(1)} %collective-permute-done.3.refs_2_), channel_id=1, source_target_pairs={{0,2},{1,3},{2,0},{3,1},{4,6},{5,7},{6,4},{7,5},{8,10},{9,11},{10,... | collective-permute-start | bytes 172040 | tf_op jit(solution)/shard_map/ppermute | solution.py:273
  27.0 4.8 %collective-permute-start.6 = (bf16[4,7168]{1,0:T(4,128)(2,1)S(1)}, bf16[4,7168]{1,0:T(4,128)(2,1)S(1)}, u32[]{:S(2)}, u32[]{:S(2)}) collective-permute-start(bf16[4,7168]{1,0:T(4,128)(2,1)S(1)} %collective-permute-done.5.refs_3_), channel_id=1, source_target_pairs={{0,2},{1,3},{2,0},{3,1},{4,6},{5,7},{6,4},{7,5},{8,10},{9,11},{10,... | collective-permute-start | bytes 172040 | tf_op jit(solution)/shard_map/ppermute | solution.py:273
  27.9 4.6 %collective-permute-start.13 = (bf16[4,7168]{1,0:T(4,128)(2,1)S(1)}, bf16[4,7168]{1,0:T(4,128)(2,1)S(1)}, u32[]{:S(2)}, u32[]{:S(2)}) collective-permute-start(bf16[4,7168]{1,0:T(4,128)(2,1)S(1)} %collective-permute-done.7.refs_1_), channel_id=1, source_target_pairs={{0,2},{1,3},{2,0},{3,1},{4,6},{5,7},{6,4},{7,5},{8,10},{9,11},{10,... | collective-permute-start | bytes 172040 | tf_op jit(solution)/shard_map/ppermute | solution.py:273
  29.4 3.4 %collective-permute-start.14 = (bf16[4,7168]{1,0:T(4,128)(2,1)S(1)}, bf16[4,7168]{1,0:T(4,128)(2,1)S(1)}, u32[]{:S(2)}, u32[]{:S(2)}) collective-permute-start(bf16[4,7168]{1,0:T(4,128)(2,1)S(1)} %collective-permute-done.12.refs_0_), channel_id=1, source_target_pairs={{0,1},{1,0},{2,3},{3,2},{4,5},{5,4},{6,7},{7,6},{8,9},{9,8},{10,11... | collective-permute-start | bytes 172040 | tf_op jit(solution)/shard_map/ppermute | solution.py:273
  31.8 1.2 %collective-permute-start.16 = (bf16[4,7168]{1,0:T(4,128)(2,1)S(1)}, bf16[4,7168]{1,0:T(4,128)(2,1)S(1)}, u32[]{:S(2)}, u32[]{:S(2)}) collective-permute-start(bf16[4,7168]{1,0:T(4,128)(2,1)S(1)} %collective-permute-done.4.refs_2_), channel_id=1, source_target_pairs={{0,1},{1,0},{2,3},{3,2},{4,5},{5,4},{6,7},{7,6},{8,9},{9,8},{10,11... | collective-permute-start | bytes 172040 | tf_op jit(solution)/shard_map/ppermute | solution.py:273
  31.8 1.4 %collective-permute-start.17 = (bf16[4,7168]{1,0:T(4,128)(2,1)S(1)}, bf16[4,7168]{1,0:T(4,128)(2,1)S(1)}, u32[]{:S(2)}, u32[]{:S(2)}) collective-permute-start(bf16[4,7168]{1,0:T(4,128)(2,1)S(1)} %collective-permute-done.6.refs_3_), channel_id=1, source_target_pairs={{0,1},{1,0},{2,3},{3,2},{4,5},{5,4},{6,7},{7,6},{8,9},{9,8},{10,11... | collective-permute-start | bytes 172040 | tf_op jit(solution)/shard_map/ppermute | solution.py:273
  32.5 1.2 %collective-permute-start.15 = (bf16[4,7168]{1,0:T(4,128)(2,1)S(1)}, bf16[4,7168]{1,0:T(4,128)(2,1)S(1)}, u32[]{:S(2)}, u32[]{:S(2)}) collective-permute-start(bf16[4,7168]{1,0:T(4,128)(2,1)S(1)} %collective-permute-done.13.refs_1_), channel_id=1, source_target_pairs={{0,1},{1,0},{2,3},{3,2},{4,5},{5,4},{6,7},{7,6},{8,9},{9,8},{10,11... | collective-permute-start | bytes 172040 | tf_op jit(solution)/shard_map/ppermute | solution.py:273
  36.4 8.4 %collective-permute-start.18 = (bf16[32,2304]{1,0:T(8,128)(2,1)S(1)}, bf16[32,2304]{1,0:T(8,128)(2,1)S(1)}, u32[]{:S(2)}, u32[]{:S(2)}) collective-permute-start(bf16[32,2304]{1,0:T(8,128)(2,1)S(1)} %get-tuple-element.42), channel_id=1, source_target_pairs={{0,16},{16,0},{1,17},{17,1},{2,18},{18,2},{3,19},{19,3},{4,20},{20... | collective-permute-start | bytes 442376 | tf_op jit(solution)/shard_map/ppermute | solution.py:273
  38.9 6.0 %collective-permute-start.19 = (bf16[32,1792]{1,0:T(8,128)(2,1)S(1)}, bf16[32,1792]{1,0:T(8,128)(2,1)S(1)}, u32[]{:S(2)}, u32[]{:S(2)}) collective-permute-start(bf16[32,1792]{1,0:T(8,128)(2,1)S(1)} %get-tuple-element.44), channel_id=1, source_target_pairs={{0,16},{16,0},{1,17},{17,1},{2,18},{18,2},{3,19},{19,3},{4,20},{20... | collective-permute-start | bytes 344072 | tf_op jit(solution)/shard_map/ppermute | solution.py:273

commit v4 on v3

--- a/solution.py
+++ b/solution.py
@@ -45,45 +45,86 @@
     )
 
 
-def corr_kernel(norm, ref_ref, win_ref, ext_ref, out_ref, rev_ref, shift_ref, rows_ref):
+def reverse_block(block):
+    mirror = LANES - 1 - lax.broadcasted_iota(jnp.int32, (8, LANES), 1)
+    piece = block.astype(jnp.float32)
+    return lane_gather(jnp.concatenate([piece] * (8 // piece.shape[0]), axis=0), mirror)
+
+
+def shifted_copies(pair):
+    pair = jnp.broadcast_to(pair, (LANES, 2 * LANES))
+    return pltpu.roll(pair, 0, 1, stride=1, stride_axis=0)[:, LANES:].astype(jnp.bfloat16)
+
+
+def chunk_product(windowed, left, middle, right):
+    hankel = jnp.concatenate(
+        [jnp.concatenate([middle, right], axis=1), jnp.concatenate([left, middle], axis=1)], axis=0
+    )
+    return jnp.dot(windowed, hankel, preferred_element_type=jnp.float32)
+
+
+def corr_kernel(win_ref, ref_ref, out_ref, rev_ref, shift_ref):
     pols, stations, samples = win_ref.shape
     slices = samples // WIN
-    blocks = ext_ref.shape[1] // LANES
-    pitch = rows_ref.shape[1] // slices
-    mirror = LANES - 1 - lax.broadcasted_iota(jnp.int32, (8, LANES), 1)
+    pitch = out_ref.shape[0] // slices
+    blocks = samples // LANES
     for m in range(blocks):
-        piece = ext_ref[:, LANES * m : LANES * (m + 1)].astype(jnp.float32)
-        piece = jnp.concatenate([piece] * (8 // pols), axis=0)
         at = LANES * (blocks - 1 - m)
-        rev_ref[:, at : at + LANES] = lane_gather(piece, mirror)
+        rev_ref[:, at : at + LANES] = reverse_block(ref_ref[:, LANES * m : LANES * (m + 1)])
     for p in range(pols):
-        for m in range(blocks - 1):
-            pair = jnp.broadcast_to(
-                rev_ref[p : p + 1, LANES * m : LANES * (m + 2)], (LANES, 2 * LANES)
+        for m in range(1, blocks):
+            shift_ref[p, :, LANES * m : LANES * (m + 1)] = shifted_copies(
+                rev_ref[p : p + 1, LANES * (m - 1) : LANES * (m + 1)]
             )
-            rolled = pltpu.roll(pair, 0, 1, stride=1, stride_axis=0)
-            shift_ref[p, :, LANES * (m + 1) : LANES * (m + 2)] = rolled[:, LANES:].astype(
-                jnp.bfloat16
-            )
+    chunks = WIN // LAGS
+    for k in range(slices):
+        total = jnp.zeros((stations, LAGS), jnp.float32)
+        for p in range(pols):
+            for a in range(chunks):
+                if (k, a) in ((0, 0), (slices - 1, chunks - 1)):
+                    continue
+                first = WIN * k + LAGS * a
+                at = samples - first - LANES
+                total = total + chunk_product(
+                    win_ref[p, :, first : first + LAGS],
+                    shift_ref[p, :, at - LANES : at],
+                    shift_ref[p, :, at : at + LANES],
+                    shift_ref[p, :, at + LANES : at + 2 * LANES],
+                )
+        out_ref[pitch * k : pitch * k + stations, :] = total
+
+
+def finish_kernel(norm, ref_ref, win_ref, body_ref, low_ref, high_ref, part_ref, out_ref, rows_ref):
+    pols, stations, samples = win_ref.shape
+    slices = samples // WIN
+    pitch = part_ref.shape[0] // slices
+    early = [reverse_block(body_ref[:, LANES * m : LANES * (m + 1)]) for m in (2, 1, 0)]
+    early.append(reverse_block(low_ref[...]))
+    ends = samples - LANES
+    late = [reverse_block(high_ref[...])]
+    late += [
+        reverse_block(body_ref[:, ends - LANES * m : ends - LANES * (m - 1)]) for m in (0, 1, 2)
+    ]
+    extra = []
+    for first, row in ((0, early), (samples - LAGS, late)):
+        total = jnp.zeros((stations, LAGS), jnp.float32)
+        for p in range(pols):
+            copies = [
+                shifted_copies(jnp.concatenate([row[m][p : p + 1], row[m + 1][p : p + 1]], axis=1))
+                for m in range(3)
+            ]
+            total = total + chunk_product(win_ref[p, :, first : first + LAGS], *copies)
+        extra.append(total)
     station = lax.broadcasted_iota(jnp.int32, (stations, LAGS), 0)
     column = lax.broadcasted_iota(jnp.int32, (stations, LAGS), 1)
     mine = ref_ref[0] - lax.axis_index("stn") * stations
     factor = jnp.where((station == mine) | (column == 0), 0.0, norm)
     for k in range(slices):
-        total = jnp.zeros((stations, LAGS), jnp.float32)
-        for p in range(pols):
-            for a in range(WIN // LAGS):
-                first = WIN * k + LAGS * a
-                at = samples - first
-                hankel = jnp.concatenate(
-                    [shift_ref[p, :, at : at + LAGS], shift_ref[p, :, at - LANES : at + LANES]],
-                    axis=0,
-                )
-                total = total + jnp.dot(
-                    win_ref[p, :, first : first + LAGS],
-                    hankel,
-                    preferred_element_type=jnp.float32,
-                )
+        total = part_ref[pitch * k : pitch * k + stations, :]
+        if k == 0:
+            total = total + extra[0]
+        if k == slices - 1:
+            total = total + extra[1]
         total = total * factor
         top = jnp.max(jnp.max(jnp.abs(total), axis=1, keepdims=True), axis=0, keepdims=True)
         power = jnp.floor(jnp.log2(224.0 / jnp.maximum(top, 1e-35)))
@@ -101,27 +142,40 @@
             )
 
 
-def correlate(windowed, extended, reference_station):
+def correlate(windowed, body, halos, reference_station):
     pols, stations, samples = windowed.shape
     slices = samples // WIN
     pitch = -(-stations // 8) * 8
-    return pl.pallas_call(
-        functools.partial(corr_kernel, norm_inverse()),
-        out_shape=jax.ShapeDtypeStruct((slices, stations * LAGS), jnp.bfloat16),
-        in_specs=[SMEM, VMEM, VMEM],
+    params = pltpu.CompilerParams(vmem_limit_bytes=24 << 20)
+    part = pl.pallas_call(
+        corr_kernel,
+        out_shape=jax.ShapeDtypeStruct((pitch * slices, LAGS), jnp.float32),
+        in_specs=[VMEM, VMEM],
         out_specs=VMEM,
         scratch_shapes=[
-            pltpu.VMEM((8, samples + LAGS), jnp.float32),
-            pltpu.VMEM((pols, LANES, samples + LAGS), jnp.bfloat16),
-            pltpu.VMEM((LAGS // LANES, pitch * slices, LANES), jnp.float32),
+            pltpu.VMEM((8, samples), jnp.float32),
+            pltpu.VMEM((pols, LANES, samples), jnp.bfloat16),
         ],
         cost_estimate=pl.CostEstimate(
             flops=2 * pols * stations * samples * LAGS,
             bytes_accessed=2 * pols * stations * samples,
             transcendentals=0,
         ),
-        compiler_params=pltpu.CompilerParams(vmem_limit_bytes=24 << 20),
-    )(reference_station, windowed, extended)
+        compiler_params=params,
+    )(windowed, body)
+    return pl.pallas_call(
+        functools.partial(finish_kernel, norm_inverse()),
+        out_shape=jax.ShapeDtypeStruct((slices, stations * LAGS), jnp.bfloat16),
+        in_specs=[SMEM] + [VMEM] * 5,
+        out_specs=VMEM,
+        scratch_shapes=[pltpu.VMEM((LAGS // LANES, pitch * slices, LANES), jnp.float32)],
+        cost_estimate=pl.CostEstimate(
+            flops=4 * pols * stations * LAGS * LAGS,
+            bytes_accessed=2 * pols * stations * LAGS,
+            transcendentals=0,
+        ),
+        compiler_params=params,
+    )(reference_station, windowed, body, *halos, part)
 
 
 def split_kernel(*refs):
@@ -160,21 +214,39 @@
     )(*blocks)
 
 
-def target_kernel(offset_ref, delay_ref, out_ref):
-    stations, rows, voxels = out_ref.shape
+def target_kernel(stations, offset_ref, delay_ref, out_ref, rows_ref, offsets_ref, semaphores):
+    rows = rows_ref.shape[0]
+    tile, voxels = out_ref.shape[1:]
+    first = lax.axis_index("stn") * stations
+    start = pl.multiple_of(jnp.minimum(first // 8, (delay_ref.shape[0] - rows) // 8) * 8, 8)
+    copies = [
+        pltpu.make_async_copy(delay_ref.at[pl.ds(start, rows), :], rows_ref, semaphores.at[0]),
+        pltpu.make_async_copy(offset_ref, offsets_ref, semaphores.at[1]),
+    ]
+    for copy in copies:
+        copy.start()
+    for copy in copies:
+        copy.wait()
     for s in range(stations):
-        row = lax.axis_index("stn") * stations + s
-        target = (HALF - 1 - offset_ref[row]) - delay_ref[pl.ds(row, 1), :]
-        out_ref[s] = jnp.broadcast_to(target, (rows, voxels)).astype(jnp.int8)
+        delays = rows_ref[pl.ds(first - start + s, 1), :]
+        target = (HALF - 1 - offsets_ref[first + s]) - delays
+        out_ref[s] = jnp.broadcast_to(target, (tile, voxels)).astype(jnp.int8)
 
 
 def targets(sample_delays, timing_offsets, stations):
-    voxels = sample_delays.shape[1]
+    total, voxels = sample_delays.shape
+    slack = max(a * stations % 8 for a in range(total // stations))
+    rows = min(-(-(slack + stations) // 8) * 8, total)
     return pl.pallas_call(
-        target_kernel,
+        functools.partial(target_kernel, stations),
         out_shape=jax.ShapeDtypeStruct((stations, 32, voxels), jnp.int8),
-        in_specs=[SMEM, VMEM],
+        in_specs=[pl.BlockSpec(memory_space=pltpu.HBM)] * 2,
         out_specs=VMEM,
+        scratch_shapes=[
+            pltpu.VMEM((rows, voxels), jnp.int32),
+            pltpu.SMEM(timing_offsets.shape, jnp.int32),
+            pltpu.SemaphoreType.DMA((2,)),
+        ],
         cost_estimate=pl.CostEstimate(
             flops=32 * stations * voxels, bytes_accessed=36 * stations * voxels, transcendentals=0
         ),
@@ -273,43 +345,47 @@
     return lax.ppermute(block, axis, [(i, i ^ mask) for i in range(count)])
 
 
-def extend_paired(candidate, owner):
+def halos_paired(body):
     count = lax.axis_size("vox")
     odd = lax.axis_index("vox") % 2 == 1
-    first, last = candidate[:, :HALF], candidate[:, candidate.shape[1] - HALF :]
-    steps = [(b, b + 1) for b in range(1, count - 1, 2)] + [(b + 1, b) for b in range(1, count - 1, 2)]
+    first, last = body[:, :HALF], body[:, body.shape[1] - HALF :]
+    steps = [(b, b + 1) for b in range(1, count - 1, 2)]
+    steps += [(target, source) for source, target in steps]
     outer = lax.ppermute(jnp.where(odd, last, first), "vox", steps)
     inner = flip(jnp.where(odd, first, last), "vox", 1)
-    low, high = jnp.where(odd, inner, outer), jnp.where(odd, outer, inner)
-    extended = jnp.concatenate([low, candidate, high], axis=1)
-    other = flip(extended, "stn", 1)
-    return jnp.where(lax.axis_index("stn") == owner, extended, other)
-
-
-def extend(candidate, owner):
-    kept = jnp.where(lax.axis_index("stn") == owner, candidate, 0).astype(candidate.dtype)
-    block = lax.psum(kept, "stn")
-    count = lax.axis_size("vox")
-    forward = [(i, i + 1) for i in range(count - 1)]
-    backward = [(target, source) for source, target in forward]
-    low = lax.ppermute(block[:, block.shape[1] - HALF :], "vox", forward)
-    high = lax.ppermute(block[:, :HALF], "vox", backward)
-    return jnp.concatenate([low, block, high], axis=1)
-
-
-def gather_paired(block):
+    return jnp.where(odd, inner, outer), jnp.where(odd, outer, inner)
+
+
+def after(value, *others):
+    return lax.optimization_barrier((value, *others))[0]
+
+
+def gather_paired(block, sample_delays, timing_offsets, stations):
     blocks = {0: block}
-    for d in (12, 8, 4):
+    for d in (12, 8, 4, 2):
         blocks[d] = flip(block, "vox", d)
-    for d in (0, 4, 8, 12):
-        blocks[d | 2] = flip(blocks[d], "vox", 2)
-    for d in (0, 4, 8, 12, 2, 6):
+    blocks[1] = flip(block, "vox", 1)
+    blocks[6] = flip(blocks[4], "vox", 2)
+    target = targets(after(sample_delays, blocks[4]), timing_offsets, stations)
+    near, target = lax.optimization_barrier((blocks[8], blocks[4], target, blocks[1]))[::2]
+    blocks[10] = flip(near, "vox", 2)
+    far = after(blocks[12], near)
+    blocks[14] = flip(far, "vox", 2)
+    blocks[2], blocks[4], blocks[6], blocks[8], blocks[12] = lax.optimization_barrier(
+        (blocks[2], blocks[4], blocks[6], near, far)
+    )
+    for d in (2, 4, 6):
         blocks[d | 1] = flip(blocks[d], "vox", 1)
-    done = [split([blocks[d] for d in order]) for order in ORDER[:2]]
-    blocks[10], blocks[14], done = lax.optimization_barrier((blocks[10], blocks[14], done))
-    for d in (10, 14):
+    early = split([blocks[d] for d in ORDER[0]])
+    blocks[8], blocks[10], early, blocks[12] = lax.optimization_barrier(
+        (blocks[8], blocks[10], early, blocks[12])
+    )
+    for d in (8, 10, 12):
         blocks[d | 1] = flip(blocks[d], "vox", 1)
-    return done + [split([blocks[d] for d in order]) for order in ORDER[2:]]
+    middle = split([blocks[d] for d in ORDER[1]])
+    blocks[14], blocks[13] = lax.optimization_barrier((blocks[14], blocks[13]))
+    blocks[15] = flip(blocks[14], "vox", 1)
+    return [early, middle] + [split([blocks[d] for d in order]) for order in ORDER[2:]], target
 
 
 ORDER = ((0, 4, 8, 12), (1, 5, 9, 13), (2, 6, 10, 14), (3, 7, 11, 15))
@@ -324,24 +400,33 @@
     swap = lax.axis_size("stn") == 2 and count == 16
 
     candidate = lax.dynamic_index_in_dim(voltages, station_ref % stations_here, 0, keepdims=False)
-    extended = extend_paired(candidate, owner) if swap else extend(candidate, owner)
-
-    windowed = (
-        voltages.reshape(stations_here, pols, slices_here, WIN).astype(jnp.float32)
-        * taper_weights()
-    ).astype(jnp.bfloat16)
-    windowed = jnp.transpose(windowed.reshape(stations_here, pols, samples_here), (1, 0, 2))
-
-    target = targets(sample_delays, timing_offsets, stations_here)
-    extended, target = lax.optimization_barrier((extended, target))
-    corr = correlate(windowed, extended, reference_station)
+    candidate = lax.optimization_barrier(candidate)
+    mine = lax.axis_index("stn") == owner
     if swap:
-        pairs = gather_paired(corr)
+        body = jnp.where(mine, candidate, flip(candidate, "stn", 1))
+        halos = halos_paired(body)
     else:
+        body = lax.psum(jnp.where(mine, candidate, 0).astype(candidate.dtype), "stn")
+        forward = [(i, i + 1) for i in range(count - 1)]
+        backward = [(target, source) for source, target in forward]
+        halos = (
+            lax.ppermute(body[:, samples_here - HALF :], "vox", forward),
+            lax.ppermute(body[:, :HALF], "vox", backward),
+        )
+
+    taper = np.tile(taper_weights(), slices_here)
+    windowed = (voltages.astype(jnp.float32) * taper).astype(jnp.bfloat16)
+    windowed = jnp.transpose(windowed, (1, 0, 2))
+
+    corr = correlate(windowed, body, halos, reference_station)
+    if swap:
+        pairs, target = gather_paired(corr, sample_delays, timing_offsets, stations_here)
+    else:
+        target = targets(sample_delays, timing_offsets, stations_here)
         gathered = lax.all_gather(corr, "vox", axis=0, tiled=False)
-        mine = lax.axis_index("vox")
+        place = lax.axis_index("vox")
         every = [
-            lax.dynamic_index_in_dim(gathered, mine ^ j, 0, keepdims=False) for j in range(count)
+            lax.dynamic_index_in_dim(gathered, place ^ j, 0, keepdims=False) for j in range(count)
         ]
         pairs = [split(every[j : j + 4]) for j in range(0, count, 4)]
     pieces, scales = zip(*pairs, strict=True)

time: 46 us -> 42.2 us (0.917)
  waiting for transfers between devices: 11.1 us -> 7.87 us
  local copies, waits for them, and re-layouts: 3.26 us -> 2.57 us
    ppermute x19, waiting for transfers between devices: 11.1 us -> 7.86 us  [flip(): return lax.ppermute(block, axis, [(i, i ^ mask) for i in range(count)])]
    unnamed x6 -> x4, local copies, waits for them, and re-layouts: 2.53 us -> 1.83 us
    pallas_call x2 -> x3, Pallas kernels: 3.05 us -> 3.39 us  [the longest x1 1.78 us: correlate(): pl.pallas_call(corr_kernel, out_shape=jax.ShapeDtypeStruct((pitch * slice...]
  transfers between devices with their start and end apart: 20 -> 20, of which waited for: 9 -> 7; matrix products, arithmetic and copies ran while one was open for 4% -> 3% of each run, Pallas kernels for 8% -> 13%
where the time goes in v4:
time: 42.2 us; the launch traced here: 41.9 us
  starting transfers between devices  19.6 us (46%)
  Pallas kernels  9.73 us (23%)
  waiting for transfers between devices  7.87 us (19%)
  local copies, waits for them, and re-layouts  2.57 us (6%)
  other arithmetic  1.33 us (3%)
  between operations  0.85 us (2%)
    ppermute x19, starting transfers between devices, flip(): return lax.ppermute(block, axis, [(i, i ^ mask) for i in range(count)])  18.9 us
    ppermute x19, waiting for transfers between devices, flip(): return lax.ppermute(block, axis, [(i, i ^ mask) for i in range(count)])  7.86 us
    pallas_call x2, Pallas kernels, image(): pl.pallas_call(functools.partial(image_kernel, swap, len(pieces), start),...  4.25 us
    unnamed x4, local copies, waits for them, and re-layouts  1.83 us
    pallas_call x1, Pallas kernels, correlate(): pl.pallas_call(corr_kernel, out_shape=jax.ShapeDtypeStruct((pitch * slice...  1.78 us
    transpose x1, other arithmetic, shards(): windowed = jnp.transpose(windowed, (1, 0, 2))  1.29 us
    pallas_call x4, Pallas kernels, split(): pl.pallas_call(split_kernel, out_shape=[jax.ShapeDtypeStruct((rows, colum...  1.25 us
    pallas_call x1, Pallas kernels, targets(): pl.pallas_call(functools.partial(target_kernel, stations), out_shape=jax....  0.99 us
  transfers between devices with their start and end apart: 20, of which 7 were waited for; matrix products, arithmetic and copies ran while one was open for 3% of the time, Pallas kernels for 13%

profile of v4, /device:TPU:0, one launch (start us, length us, event | category | flops | bytes accessed | tf_op | source)
XLA Modules:
  0.0 41.9 jit_solution(723874163106708991)
XLA Ops:
  0.7 0.7 %dynamic-slice_bitcast_fusion = bf16[2,4096]{1,0:T(2,128)(2,1)S(1)} fusion(bf16[28,2,4096]{2,1,0:T(2,128)(2,1)} %param.5, s32[]{:T(128)S(6)} %select_n.50), kind=kLoop, calls=%fused_computation.3 | loop fusion | bytes 32772 | tf_op jit(solution)/shard_map/jit(dynamic_index_in_dim)/squeeze | solution.py:402
  1.4 3.0 %collective-permute-start = (bf16[2,4096]{1,0:T(2,128)(2,1)S(1)}, bf16[2,4096]{1,0:T(2,128)(2,1)S(1)}, u32[]{:S(2)}, u32[]{:S(2)}) collective-permute-start(bf16[2,4096]{1,0:T(2,128)(2,1)S(1)} %dynamic-slice_bitcast_fusion), channel_id=1, source_target_pairs={{0,16},{16,0},{1,17},{17,1},{2,18},{18,2},{3,19},{19,3},{4,20},{20... | collective-permute-start | bytes 49160 | tf_op jit(solution)/shard_map/ppermute | solution.py:345
  4.4 1.3 %fusion.win_ref = bf16[2,28,4096]{2,1,0:T(8,128)(2,1)S(1)} fusion(bf16[28,2,4096]{2,1,0:T(2,128)(2,1)} %param.5, f32[4096]{0:T(1024)} %constant.48.clone), kind=kLoop, calls=%fused_computation.1 | loop fusion | flops 688128 | bytes 933888 | tf_op jit(solution)/shard_map/transpose | solution.py:419
  5.7 0.4 collective-permute-done
  6.3 0.7 %collective-permute-start.2 = (bf16[2,128]{1,0:T(2,128)(2,1)S(1)}, bf16[2,128]{1,0:T(2,128)(2,1)S(1)}, u32[]{:S(2)}, u32[]{:S(2)}) collective-permute-start(bf16[2,128]{1,0:T(2,128)(2,1)S(1)} %get-tuple-element.59), channel_id=1, source_target_pairs={{1,2},{3,4},{5,6},{7,8},{9,10},{11,12},{13,14},{2,1},{4,3},{6,5},{... | collective-permute-start | bytes 1544 | tf_op jit(solution)/shard_map/ppermute | solution.py:354
  6.9 1.8 %shard_map.55.part_ref = f32[128,256]{1,0:T(8,128)S(1)} custom-call(bf16[2,28,4096]{2,1,0:T(8,128)(2,1)S(1)} %fusion.win_ref, bf16[2,4096]{1,0:T(2,128)(2,1)S(1)} %broadcast_select_fusion.ref_ref.body_ref), custom_call_target="tpu_custom_call" | custom-call | flops 117440512 | bytes 458752 | tf_op jit(solution)/shard_map/pallas_call | solution.py:150
  8.7 0.6 %shard_map.56.refs_0_ = bf16[4,7168]{1,0:T(4,128)(2,1)S(1)} custom-call(s32[1]{0:T(128)S(6)} %copy.8.ref_ref, bf16[2,28,4096]{2,1,0:T(8,128)(2,1)S(1)} %fusion.win_ref, bf16[2,4096]{1,0:T(2,128)(2,1)S(1)} %broadcast_select_fusion.ref_ref.body_ref, bf16[2,128]{1,0:T(2,128)(2,1)S(1)} %get-tuple-element.62.low_ref, ...), custom_call_target="tpu_custom_call" | custom-call | flops 14680064 | bytes 28672 | tf_op jit(solution)/shard_map/pallas_call | solution.py:166
  9.4 5.4 %collective-permute-start.4 = (bf16[4,7168]{1,0:T(4,128)(2,1)S(1)}, bf16[4,7168]{1,0:T(4,128)(2,1)S(1)}, u32[]{:S(2)}, u32[]{:S(2)}) collective-permute-start(bf16[4,7168]{1,0:T(4,128)(2,1)S(1)} %shard_map.56.refs_0_), channel_id=1, source_target_pairs={{0,4},{1,5},{2,6},{3,7},{4,0},{5,1},{6,2},{7,3},{8,12},{9,13},{10,... | collective-permute-start | bytes 172040 | tf_op jit(solution)/shard_map/ppermute | solution.py:345
  14.8 2.6 %collective-permute-start.3 = (bf16[4,7168]{1,0:T(4,128)(2,1)S(1)}, bf16[4,7168]{1,0:T(4,128)(2,1)S(1)}, u32[]{:S(2)}, u32[]{:S(2)}) collective-permute-start(bf16[4,7168]{1,0:T(4,128)(2,1)S(1)} %shard_map.56.refs_0_), channel_id=1, source_target_pairs={{0,8},{1,9},{2,10},{3,11},{4,12},{5,13},{6,14},{7,15},{8,0},{9,1},... | collective-permute-start | bytes 172040 | tf_op jit(solution)/shard_map/ppermute | solution.py:345
  17.4 1.7 %collective-permute-start.6 = (bf16[4,7168]{1,0:T(4,128)(2,1)S(1)}, bf16[4,7168]{1,0:T(4,128)(2,1)S(1)}, u32[]{:S(2)}, u32[]{:S(2)}) collective-permute-start(bf16[4,7168]{1,0:T(4,128)(2,1)S(1)} %shard_map.56.refs_0_), channel_id=1, source_target_pairs={{0,2},{1,3},{2,0},{3,1},{4,6},{5,7},{6,4},{7,5},{8,10},{9,11},{10,... | collective-permute-start | bytes 172040 | tf_op jit(solution)/shard_map/ppermute | solution.py:345
  19.1 0.4 collective-permute-start.7
  19.4 1.2 %copy-done = s32[56,4096]{1,0:T(8,128)S(1)} copy-done((s32[56,4096]{1,0:T(8,128)S(1)}, s32[56,4096]{1,0:T(8,128)}, u32[]{:S(2)}) %copy-start) | copy-done | bytes 917528
  20.6 0.7 %copy-done.1 = s32[56]{0:T(128)S(1)} copy-done((s32[56]{0:T(128)S(1)}, s32[56]{0:T(128)}, u32[]{:S(2)}) %copy-start.1) | copy-done | bytes 248
  21.3 1.0 %shard_map.57.target_ref = s8[28,32,4096]{2,1,0:T(32,128)(4,1)S(1)} custom-call(s32[56]{0:T(128)S(1)} %copy-done.1, s32[56,4096]{1,0:T(8,128)S(1)} %copy-done), custom_call_target="tpu_custom_call" | custom-call | flops 3670016 | bytes 4128768 | tf_op jit(solution)/shard_map/pallas_call | solution.py:240
  22.3 1.7 %collective-permute-start.9 = (bf16[4,7168]{1,0:T(4,128)(2,1)S(1)}, bf16[4,7168]{1,0:T(4,128)(2,1)S(1)}, u32[]{:S(2)}, u32[]{:S(2)}) collective-permute-start(bf16[4,7168]{1,0:T(4,128)(2,1)S(1)} %collective-permute-done.3.refs_2_), channel_id=1, source_target_pairs={{0,2},{1,3},{2,0},{3,1},{4,6},{5,7},{6,4},{7,5},{8,10},{9,11},{10,... | collective-permute-start | bytes 172040 | tf_op jit(solution)/shard_map/ppermute | solution.py:345
  24.0 0.4 collective-permute-start.13
  24.4 0.3 shard_map.58
  24.7 2.4 %collective-permute-done.9.refs_2_ = bf16[4,7168]{1,0:T(4,128)(2,1)S(1)} collective-permute-done((bf16[4,7168]{1,0:T(4,128)(2,1)S(1)}, bf16[4,7168]{1,0:T(4,128)(2,1)S(1)}, u32[]{:S(2)}, u32[]{:S(2)}) %collective-permute-start.9) | collective-permute-done | bytes 57376 | tf_op jit(solution)/shard_map/ppermute | solution.py:345
  27.1 0.5 %collective-permute-start.11 = (bf16[4,7168]{1,0:T(4,128)(2,1)S(1)}, bf16[4,7168]{1,0:T(4,128)(2,1)S(1)}, u32[]{:S(2)}, u32[]{:S(2)}) collective-permute-start(bf16[4,7168]{1,0:T(4,128)(2,1)S(1)} %collective-permute-done.3.refs_2_), channel_id=1, source_target_pairs={{0,1},{1,0},{2,3},{3,2},{4,5},{5,4},{6,7},{7,6},{8,9},{9,8},{10,11... | collective-permute-start | bytes 172040 | tf_op jit(solution)/shard_map/ppermute | solution.py:345
  27.6 0.5 %collective-permute-start.16 = (bf16[4,7168]{1,0:T(4,128)(2,1)S(1)}, bf16[4,7168]{1,0:T(4,128)(2,1)S(1)}, u32[]{:S(2)}, u32[]{:S(2)}) collective-permute-start(bf16[4,7168]{1,0:T(4,128)(2,1)S(1)} %collective-permute-done.9.refs_2_), channel_id=1, source_target_pairs={{0,1},{1,0},{2,3},{3,2},{4,5},{5,4},{6,7},{7,6},{8,9},{9,8},{10,11... | collective-permute-start | bytes 172040 | tf_op jit(solution)/shard_map/ppermute | solution.py:345
  28.2 0.1 collective-permute-done.12.refs_3_
  28.3 0.4 collective-permute-start.15
  28.8 0.3 shard_map.60
  29.2 0.3 shard_map.59
  29.6 0.4 collective-permute-done.17.refs_3_
  30.0 0.3 shard_map.61
  30.3 2.4 %shard_map.62 = (f32[32,2304]{1,0:T(8,128)S(1)}, bf16[32,2304]{1,0:T(8,128)(2,1)S(1)}) custom-call(s8[28,32,4096]{2,1,0:T(32,128)(4,1)S(1)} %shard_map.57.target_ref, f8e4m3fn[32,7168]{1,0:T(32,128)(4,1)S(1)} %get-tuple-element.41.refs_0_, f8e4m3fn[32,7168]{1,0:T(32,128)(4,1)S(1)} %get-tuple-element.44.refs_1_, ...), custom_call_target="tpu_custom_call" | custom-call | flops 4227858432 | bytes 589824 | tf_op jit(solution)/shard_map/pallas_call | solution.py:319
  32.7 1.6 %collective-permute-start.18 = (bf16[32,2304]{1,0:T(8,128)(2,1)S(1)}, bf16[32,2304]{1,0:T(8,128)(2,1)S(1)}, u32[]{:S(2)}, u32[]{:S(2)}) collective-permute-start(bf16[32,2304]{1,0:T(8,128)(2,1)S(1)} %get-tuple-element.56), channel_id=1, source_target_pairs={{0,16},{16,0},{1,17},{17,1},{2,18},{18,2},{3,19},{19,3},{4,20},{20... | collective-permute-start | bytes 442376 | tf_op jit(solution)/shard_map/ppermute | solution.py:345
  34.2 1.9 %shard_map.63 = (f32[32,1792]{1,0:T(8,128)S(1)}, bf16[32,1792]{1,0:T(8,128)(2,1)S(1)}) custom-call(s8[28,32,4096]{2,1,0:T(32,128)(4,1)S(1)} %shard_map.57.target_ref, f8e4m3fn[32,7168]{1,0:T(32,128)(4,1)S(1)} %get-tuple-element.41.refs_0_, f8e4m3fn[32,7168]{1,0:T(32,128)(4,1)S(1)} %get-tuple-element.44.refs_1_, ...), custom_call_target="tpu_custom_call" | custom-call | flops 3288334336 | bytes 458752 | tf_op jit(solution)/shard_map/pallas_call | solution.py:319
  36.1 0.6 %collective-permute-start.19 = (bf16[32,1792]{1,0:T(8,128)(2,1)S(1)}, bf16[32,1792]{1,0:T(8,128)(2,1)S(1)}, u32[]{:S(2)}, u32[]{:S(2)}) collective-permute-start(bf16[32,1792]{1,0:T(8,128)(2,1)S(1)} %get-tuple-element.58), channel_id=1, source_target_pairs={{0,16},{16,0},{1,17},{17,1},{2,18},{18,2},{3,19},{19,3},{4,20},{20... | collective-permute-start | bytes 344072 | tf_op jit(solution)/shard_map/ppermute | solution.py:345
  36.7 4.4 %collective-permute-done.19.refs_3_ = bf16[32,1792]{1,0:T(8,128)(2,1)S(1)} collective-permute-done((bf16[32,1792]{1,0:T(8,128)(2,1)S(1)}, bf16[32,1792]{1,0:T(8,128)(2,1)S(1)}, u32[]{:S(2)}, u32[]{:S(2)}) %collective-permute-start.19) | collective-permute-done | bytes 114720 | tf_op jit(solution)/shard_map/ppermute | solution.py:345
  41.1 0.8 %shard_map.64 = f32[32,4096]{1,0:T(8,128)} custom-call(f32[32,2304]{1,0:T(8,128)S(1)} %get-tuple-element.55.refs_0_, bf16[32,2304]{1,0:T(8,128)(2,1)S(1)} %collective-permute-done.18.refs_1_, f32[32,1792]{1,0:T(8,128)S(1)} %get-tuple-element.57.refs_2_, bf16[32,1792]{1,0:T(8,128)(2,1)S(1)} %collective-permute-done.19.refs_3_), custom_call_target="tpu_custom_call" | custom-call | tf_op jit(solution)/shard_map/pallas_call | solution.py:443
  (27 shorter events, 0.5 us)
Async XLA Ops:
  1.4 4.7 %collective-permute-start = (bf16[2,4096]{1,0:T(2,128)(2,1)S(1)}, bf16[2,4096]{1,0:T(2,128)(2,1)S(1)}, u32[]{:S(2)}, u32[]{:S(2)}) collective-permute-start(bf16[2,4096]{1,0:T(2,128)(2,1)S(1)} %dynamic-slice_bitcast_fusion), channel_id=1, source_target_pairs={{0,16},{16,0},{1,17},{17,1},{2,18},{18,2},{3,19},{19,3},{4,20},{20... | collective-permute-start | bytes 49160 | tf_op jit(solution)/shard_map/ppermute | solution.py:345
  6.2 2.5 %collective-permute-start.1 = (bf16[2,128]{1,0:T(2,128)(2,1)S(1)}, bf16[2,128]{1,0:T(2,128)(2,1)S(1)}, u32[]{:S(2)}, u32[]{:S(2)}) collective-permute-start(bf16[2,128]{1,0:T(2,128)(2,1)S(1)} %get-tuple-element.60), channel_id=1, source_target_pairs={{0,1},{1,0},{2,3},{3,2},{4,5},{5,4},{6,7},{7,6},{8,9},{9,8},{10,11... | collective-permute-start | bytes 1544 | tf_op jit(solution)/shard_map/ppermute | solution.py:345
  6.3 2.5 %collective-permute-start.2 = (bf16[2,128]{1,0:T(2,128)(2,1)S(1)}, bf16[2,128]{1,0:T(2,128)(2,1)S(1)}, u32[]{:S(2)}, u32[]{:S(2)}) collective-permute-start(bf16[2,128]{1,0:T(2,128)(2,1)S(1)} %get-tuple-element.59), channel_id=1, source_target_pairs={{1,2},{3,4},{5,6},{7,8},{9,10},{11,12},{13,14},{2,1},{4,3},{6,5},{... | collective-permute-start | bytes 1544 | tf_op jit(solution)/shard_map/ppermute | solution.py:354
  9.4 9.7 %collective-permute-start.4 = (bf16[4,7168]{1,0:T(4,128)(2,1)S(1)}, bf16[4,7168]{1,0:T(4,128)(2,1)S(1)}, u32[]{:S(2)}, u32[]{:S(2)}) collective-permute-start(bf16[4,7168]{1,0:T(4,128)(2,1)S(1)} %shard_map.56.refs_0_), channel_id=1, source_target_pairs={{0,4},{1,5},{2,6},{3,7},{4,0},{5,1},{6,2},{7,3},{8,12},{9,13},{10,... | collective-permute-start | bytes 172040 | tf_op jit(solution)/shard_map/ppermute | solution.py:345
  14.8 7.5 %collective-permute-start.3 = (bf16[4,7168]{1,0:T(4,128)(2,1)S(1)}, bf16[4,7168]{1,0:T(4,128)(2,1)S(1)}, u32[]{:S(2)}, u32[]{:S(2)}) collective-permute-start(bf16[4,7168]{1,0:T(4,128)(2,1)S(1)} %shard_map.56.refs_0_), channel_id=1, source_target_pairs={{0,8},{1,9},{2,10},{3,11},{4,12},{5,13},{6,14},{7,15},{8,0},{9,1},... | collective-permute-start | bytes 172040 | tf_op jit(solution)/shard_map/ppermute | solution.py:345
  17.4 4.9 %collective-permute-start.5 = (bf16[4,7168]{1,0:T(4,128)(2,1)S(1)}, bf16[4,7168]{1,0:T(4,128)(2,1)S(1)}, u32[]{:S(2)}, u32[]{:S(2)}) collective-permute-start(bf16[4,7168]{1,0:T(4,128)(2,1)S(1)} %shard_map.56.refs_0_), channel_id=1, source_target_pairs={{0,1},{1,0},{2,3},{3,2},{4,5},{5,4},{6,7},{7,6},{8,9},{9,8},{10,11... | collective-permute-start | bytes 172040 | tf_op jit(solution)/shard_map/ppermute | solution.py:345
  17.4 6.6 %collective-permute-start.8 = (bf16[4,7168]{1,0:T(4,128)(2,1)S(1)}, bf16[4,7168]{1,0:T(4,128)(2,1)S(1)}, u32[]{:S(2)}, u32[]{:S(2)}) collective-permute-start(bf16[4,7168]{1,0:T(4,128)(2,1)S(1)} %shard_map.56.refs_0_), channel_id=1, source_target_pairs={{0,12},{1,13},{2,14},{3,15},{4,8},{5,9},{6,10},{7,11},{8,4},{9,5},... | collective-permute-start | bytes 172040 | tf_op jit(solution)/shard_map/ppermute | solution.py:345
  17.4 7.0 %collective-permute-start.6 = (bf16[4,7168]{1,0:T(4,128)(2,1)S(1)}, bf16[4,7168]{1,0:T(4,128)(2,1)S(1)}, u32[]{:S(2)}, u32[]{:S(2)}) collective-permute-start(bf16[4,7168]{1,0:T(4,128)(2,1)S(1)} %shard_map.56.refs_0_), channel_id=1, source_target_pairs={{0,2},{1,3},{2,0},{3,1},{4,6},{5,7},{6,4},{7,5},{8,10},{9,11},{10,... | collective-permute-start | bytes 172040 | tf_op jit(solution)/shard_map/ppermute | solution.py:345
  19.1 5.3 %collective-permute-start.7 = (bf16[4,7168]{1,0:T(4,128)(2,1)S(1)}, bf16[4,7168]{1,0:T(4,128)(2,1)S(1)}, u32[]{:S(2)}, u32[]{:S(2)}) collective-permute-start(bf16[4,7168]{1,0:T(4,128)(2,1)S(1)} %collective-permute-done.4.refs_1_), channel_id=1, source_target_pairs={{0,2},{1,3},{2,0},{3,1},{4,6},{5,7},{6,4},{7,5},{8,10},{9,11},{10,... | collective-permute-start | bytes 172040 | tf_op jit(solution)/shard_map/ppermute | solution.py:345
  19.4 1.2 %copy-start = (s32[56,4096]{1,0:T(8,128)S(1)}, s32[56,4096]{1,0:T(8,128)}, u32[]{:S(2)}) copy-start(s32[56,4096]{1,0:T(8,128)} %delay_ref) | copy-start | bytes 2752516
  20.6 0.7 %copy-start.1 = (s32[56]{0:T(128)S(1)}, s32[56]{0:T(128)}, u32[]{:S(2)}) copy-start(s32[56]{0:T(128)} %offset_ref.1) | copy-start | bytes 676
  22.3 4.8 %collective-permute-start.9 = (bf16[4,7168]{1,0:T(4,128)(2,1)S(1)}, bf16[4,7168]{1,0:T(4,128)(2,1)S(1)}, u32[]{:S(2)}, u32[]{:S(2)}) collective-permute-start(bf16[4,7168]{1,0:T(4,128)(2,1)S(1)} %collective-permute-done.3.refs_2_), channel_id=1, source_target_pairs={{0,2},{1,3},{2,0},{3,1},{4,6},{5,7},{6,4},{7,5},{8,10},{9,11},{10,... | collective-permute-start | bytes 172040 | tf_op jit(solution)/shard_map/ppermute | solution.py:345
  24.0 4.2 %collective-permute-start.13 = (bf16[4,7168]{1,0:T(4,128)(2,1)S(1)}, bf16[4,7168]{1,0:T(4,128)(2,1)S(1)}, u32[]{:S(2)}, u32[]{:S(2)}) collective-permute-start(bf16[4,7168]{1,0:T(4,128)(2,1)S(1)} %collective-permute-done.8.refs_3_), channel_id=1, source_target_pairs={{0,2},{1,3},{2,0},{3,1},{4,6},{5,7},{6,4},{7,5},{8,10},{9,11},{10,... | collective-permute-start | bytes 172040 | tf_op jit(solution)/shard_map/ppermute | solution.py:345
  27.1 1.2 %collective-permute-start.12 = (bf16[4,7168]{1,0:T(4,128)(2,1)S(1)}, bf16[4,7168]{1,0:T(4,128)(2,1)S(1)}, u32[]{:S(2)}, u32[]{:S(2)}) collective-permute-start(bf16[4,7168]{1,0:T(4,128)(2,1)S(1)} %collective-permute-done.8.refs_3_), channel_id=1, source_target_pairs={{0,1},{1,0},{2,3},{3,2},{4,5},{5,4},{6,7},{7,6},{8,9},{9,8},{10,11... | collective-permute-start | bytes 172040 | tf_op jit(solution)/shard_map/ppermute | solution.py:345
  27.1 1.6 %collective-permute-start.11 = (bf16[4,7168]{1,0:T(4,128)(2,1)S(1)}, bf16[4,7168]{1,0:T(4,128)(2,1)S(1)}, u32[]{:S(2)}, u32[]{:S(2)}) collective-permute-start(bf16[4,7168]{1,0:T(4,128)(2,1)S(1)} %collective-permute-done.3.refs_2_), channel_id=1, source_target_pairs={{0,1},{1,0},{2,3},{3,2},{4,5},{5,4},{6,7},{7,6},{8,9},{9,8},{10,11... | collective-permute-start | bytes 172040 | tf_op jit(solution)/shard_map/ppermute | solution.py:345
  27.6 1.6 %collective-permute-start.10 = (bf16[4,7168]{1,0:T(4,128)(2,1)S(1)}, bf16[4,7168]{1,0:T(4,128)(2,1)S(1)}, u32[]{:S(2)}, u32[]{:S(2)}) collective-permute-start(bf16[4,7168]{1,0:T(4,128)(2,1)S(1)} %collective-permute-done.4.refs_1_), channel_id=1, source_target_pairs={{0,1},{1,0},{2,3},{3,2},{4,5},{5,4},{6,7},{7,6},{8,9},{9,8},{10,11... | collective-permute-start | bytes 172040 | tf_op jit(solution)/shard_map/ppermute | solution.py:345
  27.6 1.9 %collective-permute-start.16 = (bf16[4,7168]{1,0:T(4,128)(2,1)S(1)}, bf16[4,7168]{1,0:T(4,128)(2,1)S(1)}, u32[]{:S(2)}, u32[]{:S(2)}) collective-permute-start(bf16[4,7168]{1,0:T(4,128)(2,1)S(1)} %collective-permute-done.9.refs_2_), channel_id=1, source_target_pairs={{0,1},{1,0},{2,3},{3,2},{4,5},{5,4},{6,7},{7,6},{8,9},{9,8},{10,11... | collective-permute-start | bytes 172040 | tf_op jit(solution)/shard_map/ppermute | solution.py:345
  28.2 1.3 %collective-permute-start.14 = (bf16[4,7168]{1,0:T(4,128)(2,1)S(1)}, bf16[4,7168]{1,0:T(4,128)(2,1)S(1)}, u32[]{:S(2)}, u32[]{:S(2)}) collective-permute-start(bf16[4,7168]{1,0:T(4,128)(2,1)S(1)} %collective-permute-done.6.refs_0_), channel_id=1, source_target_pairs={{0,1},{1,0},{2,3},{3,2},{4,5},{5,4},{6,7},{7,6},{8,9},{9,8},{10,11... | collective-permute-start | bytes 172040 | tf_op jit(solution)/shard_map/ppermute | solution.py:345
  28.3 1.3 %collective-permute-start.15 = (bf16[4,7168]{1,0:T(4,128)(2,1)S(1)}, bf16[4,7168]{1,0:T(4,128)(2,1)S(1)}, u32[]{:S(2)}, u32[]{:S(2)}) collective-permute-start(bf16[4,7168]{1,0:T(4,128)(2,1)S(1)} %collective-permute-done.7.refs_1_), channel_id=1, source_target_pairs={{0,1},{1,0},{2,3},{3,2},{4,5},{5,4},{6,7},{7,6},{8,9},{9,8},{10,11... | collective-permute-start | bytes 172040 | tf_op jit(solution)/shard_map/ppermute | solution.py:345
  28.7 1.2 %collective-permute-start.17 = (bf16[4,7168]{1,0:T(4,128)(2,1)S(1)}, bf16[4,7168]{1,0:T(4,128)(2,1)S(1)}, u32[]{:S(2)}, u32[]{:S(2)}) collective-permute-start(bf16[4,7168]{1,0:T(4,128)(2,1)S(1)} %collective-permute-done.13.refs_3_), channel_id=1, source_target_pairs={{0,1},{1,0},{2,3},{3,2},{4,5},{5,4},{6,7},{7,6},{8,9},{9,8},{10,11... | collective-permute-start | bytes 172040 | tf_op jit(solution)/shard_map/ppermute | solution.py:345
  32.7 8.4 %collective-permute-start.18 = (bf16[32,2304]{1,0:T(8,128)(2,1)S(1)}, bf16[32,2304]{1,0:T(8,128)(2,1)S(1)}, u32[]{:S(2)}, u32[]{:S(2)}) collective-permute-start(bf16[32,2304]{1,0:T(8,128)(2,1)S(1)} %get-tuple-element.56), channel_id=1, source_target_pairs={{0,16},{16,0},{1,17},{17,1},{2,18},{18,2},{3,19},{19,3},{4,20},{20... | collective-permute-start | bytes 442376 | tf_op jit(solution)/shard_map/ppermute | solution.py:345
  36.1 5.0 %collective-permute-start.19 = (bf16[32,1792]{1,0:T(8,128)(2,1)S(1)}, bf16[32,1792]{1,0:T(8,128)(2,1)S(1)}, u32[]{:S(2)}, u32[]{:S(2)}) collective-permute-start(bf16[32,1792]{1,0:T(8,128)(2,1)S(1)} %get-tuple-element.58), channel_id=1, source_target_pairs={{0,16},{16,0},{1,17},{17,1},{2,18},{18,2},{3,19},{19,3},{4,20},{20... | collective-permute-start | bytes 344072 | tf_op jit(solution)/shard_map/ppermute | solution.py:345

commit v5 on v4

--- a/solution.py
+++ b/solution.py
@@ -323,21 +323,39 @@
         out_specs=[VMEM] * len(out_shape),
         scratch_shapes=[pltpu.VMEM((2 * total, voxels), jnp.float32)],
         cost_estimate=pl.CostEstimate(
-            flops=4 * total * columns * voxels,
-            bytes_accessed=4 * total * voxels,
+            flops=4 * total * voxels,
+            bytes_accessed=total,
             transcendentals=0,
         ),
         compiler_params=pltpu.CompilerParams(vmem_limit_bytes=48 << 20),
     )(target, *pieces, *scales)
 
 
-def add_kernel(*refs):
-    *in_refs, out_ref = refs
-    at = 0
-    for kept_ref, came_ref in zip(in_refs[::2], in_refs[1::2], strict=True):
-        width = kept_ref.shape[1]
-        out_ref[:, at : at + width] = kept_ref[...] + came_ref[...].astype(jnp.float32)
-        at += width
+def add_kernel(start, kept_ref, came_ref, *refs):
+    out_ref, total_ref, semaphore = refs[-3:]
+    total_ref[...] = kept_ref[...] + came_ref[...].astype(jnp.float32)
+    copy = pltpu.make_async_copy(
+        total_ref, out_ref.at[:, pl.ds(start, total_ref.shape[1])], semaphore
+    )
+    copy.start()
+    copy.wait()
+
+
+def add_part(kept, came, out, start, voxels):
+    anywhere = pl.BlockSpec(memory_space=pltpu.HBM)
+    before = () if out is None else (out,)
+    return pl.pallas_call(
+        functools.partial(add_kernel, start),
+        out_shape=jax.ShapeDtypeStruct((kept.shape[0], voxels), jnp.float32),
+        in_specs=[VMEM, VMEM] + [anywhere] * len(before),
+        out_specs=anywhere,
+        scratch_shapes=[pltpu.VMEM(kept.shape, jnp.float32), pltpu.SemaphoreType.DMA],
+        input_output_aliases={2: 0} if before else {},
+        cost_estimate=pl.CostEstimate(
+            flops=kept.size, bytes_accessed=4 * kept.size, transcendentals=0
+        ),
+        compiler_params=pltpu.CompilerParams(vmem_limit_bytes=16 << 20),
+    )(kept, came, *before)
 
 
 def flip(block, axis, mask):
@@ -377,14 +395,14 @@
     for d in (2, 4, 6):
         blocks[d | 1] = flip(blocks[d], "vox", 1)
     early = split([blocks[d] for d in ORDER[0]])
-    blocks[8], blocks[10], early, blocks[12] = lax.optimization_barrier(
-        (blocks[8], blocks[10], early, blocks[12])
-    )
-    for d in (8, 10, 12):
+    gate = lax.optimization_barrier((blocks[8], blocks[12], early, blocks[5]))
+    blocks[8], blocks[12], early = gate[:3]
+    for d in (8, 12):
         blocks[d | 1] = flip(blocks[d], "vox", 1)
+    blocks[11] = flip(blocks[10], "vox", 1)
+    blocks[14] = after(blocks[14], blocks[11], blocks[13])
+    blocks[15] = flip(blocks[14], "vox", 1)
     middle = split([blocks[d] for d in ORDER[1]])
-    blocks[14], blocks[13] = lax.optimization_barrier((blocks[14], blocks[13]))
-    blocks[15] = flip(blocks[14], "vox", 1)
     return [early, middle] + [split([blocks[d] for d in order]) for order in ORDER[2:]], target
 
 
@@ -433,23 +451,20 @@
     if not swap:
         (partial,) = image(pieces, scales, target, False, 0, sample_delays.shape[1])
         return lax.psum_scatter(partial, "stn", scatter_dimension=0, tiled=True)
-    operands = []
+    parts = []
     start = 0
     for share in SHARES:
         voxels = sample_delays.shape[1] * share // sum(SHARES)
         kept, sent = image(pieces, scales, target, True, start, voxels)
-        operands += [kept, flip(sent, "stn", 1)]
+        parts.append((start, kept, flip(sent, "stn", 1)))
         start += voxels
-    return pl.pallas_call(
-        add_kernel,
-        out_shape=jax.ShapeDtypeStruct((operands[0].shape[0], sample_delays.shape[1]), jnp.float32),
-        in_specs=[VMEM] * len(operands),
-        out_specs=VMEM,
-        compiler_params=pltpu.CompilerParams(vmem_limit_bytes=16 << 20),
-    )(*operands)
-
-
-SHARES = (9, 7)
+    out = None
+    for start, kept, came in parts:
+        out = add_part(kept, came, out, start, sample_delays.shape[1])
+    return out
+
+
+SHARES = (14, 10, 8)
 
 
 def solution(mesh):

time: 42.2 us -> 41.6 us (0.986)
  waiting for transfers between devices: 7.87 us -> 4.39 us
  starting transfers between devices: 19.6 us -> 21.1 us
  Pallas kernels: 9.73 us -> 11.1 us
    ppermute x19 -> x20, waiting for transfers between devices: 7.86 us -> 4.39 us  [flip(): return lax.ppermute(block, axis, [(i, i ^ mask) for i in range(count)])]
    ppermute x19 -> x20, starting transfers between devices: 18.9 us -> 20.5 us  [flip(): return lax.ppermute(block, axis, [(i, i ^ mask) for i in range(count)])]
    pallas_call x1 -> x3, Pallas kernels: 0.84 us -> 2.08 us  [add_part(): pl.pallas_call(functools.partial(add_kernel, start), out_shape=jax.ShapeD...]
    pallas_call x2 -> x3, Pallas kernels: 4.25 us -> 4.38 us  [image(): pl.pallas_call(functools.partial(image_kernel, swap, len(pieces), start),...]
  transfers between devices with their start and end apart: 20 -> 21, of which waited for: 7 -> 8; matrix products, arithmetic and copies ran while one was open for 3% -> 3% of each run, Pallas kernels for 13% -> 18%
where the time goes in v5:
time: 41.6 us; the launch traced here: 41.4 us
  starting transfers between devices  21.1 us (51%)
  Pallas kernels  11.1 us (27%)
  waiting for transfers between devices  4.39 us (11%)
  local copies, waits for them, and re-layouts  2.57 us (6%)
  other arithmetic  1.33 us (3%)
  between operations  0.87 us (2%)
    ppermute x20, starting transfers between devices, flip(): return lax.ppermute(block, axis, [(i, i ^ mask) for i in range(count)])  20.5 us
    ppermute x20, waiting for transfers between devices, flip(): return lax.ppermute(block, axis, [(i, i ^ mask) for i in range(count)])  4.39 us
    pallas_call x3, Pallas kernels, image(): pl.pallas_call(functools.partial(image_kernel, swap, len(pieces), start),...  4.38 us
    pallas_call x3, Pallas kernels, add_part(): pl.pallas_call(functools.partial(add_kernel, start), out_shape=jax.ShapeD...  2.08 us
    unnamed x4, local copies, waits for them, and re-layouts  1.83 us
    pallas_call x1, Pallas kernels, correlate(): pl.pallas_call(corr_kernel, out_shape=jax.ShapeDtypeStruct((pitch * slice...  1.78 us
    transpose x1, other arithmetic, shards(): windowed = jnp.transpose(windowed, (1, 0, 2))  1.29 us
    pallas_call x4, Pallas kernels, split(): pl.pallas_call(split_kernel, out_shape=[jax.ShapeDtypeStruct((rows, colum...  1.25 us
  transfers between devices with their start and end apart: 21, of which 8 were waited for; matrix products, arithmetic and copies ran while one was open for 3% of the time, Pallas kernels for 18%

profile of v5, /device:TPU:0, one launch (start us, length us, event | category | flops | bytes accessed | tf_op | source)
XLA Modules:
  0.0 41.4 jit_solution(7917644674618819337)
XLA Ops:
  0.7 0.7 %dynamic-slice_bitcast_fusion = bf16[2,4096]{1,0:T(2,128)(2,1)S(1)} fusion(bf16[28,2,4096]{2,1,0:T(2,128)(2,1)} %param.5, s32[]{:T(128)S(6)} %select_n.50), kind=kLoop, calls=%fused_computation.3 | loop fusion | bytes 32772 | tf_op jit(solution)/shard_map/jit(dynamic_index_in_dim)/squeeze | solution.py:420
  1.4 3.0 %collective-permute-start = (bf16[2,4096]{1,0:T(2,128)(2,1)S(1)}, bf16[2,4096]{1,0:T(2,128)(2,1)S(1)}, u32[]{:S(2)}, u32[]{:S(2)}) collective-permute-start(bf16[2,4096]{1,0:T(2,128)(2,1)S(1)} %dynamic-slice_bitcast_fusion), channel_id=1, source_target_pairs={{0,16},{16,0},{1,17},{17,1},{2,18},{18,2},{3,19},{19,3},{4,20},{20... | collective-permute-start | bytes 49160 | tf_op jit(solution)/shard_map/ppermute | solution.py:363
  4.4 1.3 %fusion.win_ref = bf16[2,28,4096]{2,1,0:T(8,128)(2,1)S(1)} fusion(bf16[28,2,4096]{2,1,0:T(2,128)(2,1)} %param.5, f32[4096]{0:T(1024)} %constant.48.clone), kind=kLoop, calls=%fused_computation.1 | loop fusion | flops 688128 | bytes 933888 | tf_op jit(solution)/shard_map/transpose | solution.py:437
  5.7 0.4 collective-permute-done
  6.2 0.7 %collective-permute-start.2 = (bf16[2,128]{1,0:T(2,128)(2,1)S(1)}, bf16[2,128]{1,0:T(2,128)(2,1)S(1)}, u32[]{:S(2)}, u32[]{:S(2)}) collective-permute-start(bf16[2,128]{1,0:T(2,128)(2,1)S(1)} %get-tuple-element.61), channel_id=1, source_target_pairs={{1,2},{3,4},{5,6},{7,8},{9,10},{11,12},{13,14},{2,1},{4,3},{6,5},{... | collective-permute-start | bytes 1544 | tf_op jit(solution)/shard_map/ppermute | solution.py:372
  6.8 3.5 %collective-permute-start.1 = (bf16[2,128]{1,0:T(2,128)(2,1)S(1)}, bf16[2,128]{1,0:T(2,128)(2,1)S(1)}, u32[]{:S(2)}, u32[]{:S(2)}) collective-permute-start(bf16[2,128]{1,0:T(2,128)(2,1)S(1)} %get-tuple-element.62), channel_id=1, source_target_pairs={{0,1},{1,0},{2,3},{3,2},{4,5},{5,4},{6,7},{7,6},{8,9},{9,8},{10,11... | collective-permute-start | bytes 1544 | tf_op jit(solution)/shard_map/ppermute | solution.py:363
  10.3 1.8 %shard_map.55.part_ref = f32[128,256]{1,0:T(8,128)S(1)} custom-call(bf16[2,28,4096]{2,1,0:T(8,128)(2,1)S(1)} %fusion.win_ref, bf16[2,4096]{1,0:T(2,128)(2,1)S(1)} %broadcast_select_fusion.ref_ref.body_ref), custom_call_target="tpu_custom_call" | custom-call | flops 117440512 | bytes 458752 | tf_op jit(solution)/shard_map/pallas_call | solution.py:150
  12.1 0.6 %shard_map.56.refs_0_ = bf16[4,7168]{1,0:T(4,128)(2,1)S(1)} custom-call(s32[1]{0:T(128)S(6)} %copy.12.ref_ref, bf16[2,28,4096]{2,1,0:T(8,128)(2,1)S(1)} %fusion.win_ref, bf16[2,4096]{1,0:T(2,128)(2,1)S(1)} %broadcast_select_fusion.ref_ref.body_ref, bf16[2,128]{1,0:T(2,128)(2,1)S(1)} %get-tuple-element.64.low_ref, ...), custom_call_target="tpu_custom_call" | custom-call | flops 14680064 | bytes 28672 | tf_op jit(solution)/shard_map/pallas_call | solution.py:166
  12.8 2.0 %collective-permute-start.4 = (bf16[4,7168]{1,0:T(4,128)(2,1)S(1)}, bf16[4,7168]{1,0:T(4,128)(2,1)S(1)}, u32[]{:S(2)}, u32[]{:S(2)}) collective-permute-start(bf16[4,7168]{1,0:T(4,128)(2,1)S(1)} %shard_map.56.refs_0_), channel_id=1, source_target_pairs={{0,4},{1,5},{2,6},{3,7},{4,0},{5,1},{6,2},{7,3},{8,12},{9,13},{10,... | collective-permute-start | bytes 172040 | tf_op jit(solution)/shard_map/ppermute | solution.py:363
  14.7 2.6 %collective-permute-start.3 = (bf16[4,7168]{1,0:T(4,128)(2,1)S(1)}, bf16[4,7168]{1,0:T(4,128)(2,1)S(1)}, u32[]{:S(2)}, u32[]{:S(2)}) collective-permute-start(bf16[4,7168]{1,0:T(4,128)(2,1)S(1)} %shard_map.56.refs_0_), channel_id=1, source_target_pairs={{0,8},{1,9},{2,10},{3,11},{4,12},{5,13},{6,14},{7,15},{8,0},{9,1},... | collective-permute-start | bytes 172040 | tf_op jit(solution)/shard_map/ppermute | solution.py:363
  17.3 1.4 %collective-permute-start.6 = (bf16[4,7168]{1,0:T(4,128)(2,1)S(1)}, bf16[4,7168]{1,0:T(4,128)(2,1)S(1)}, u32[]{:S(2)}, u32[]{:S(2)}) collective-permute-start(bf16[4,7168]{1,0:T(4,128)(2,1)S(1)} %shard_map.56.refs_0_), channel_id=1, source_target_pairs={{0,2},{1,3},{2,0},{3,1},{4,6},{5,7},{6,4},{7,5},{8,10},{9,11},{10,... | collective-permute-start | bytes 172040 | tf_op jit(solution)/shard_map/ppermute | solution.py:363
  18.7 0.6 %collective-permute-start.7 = (bf16[4,7168]{1,0:T(4,128)(2,1)S(1)}, bf16[4,7168]{1,0:T(4,128)(2,1)S(1)}, u32[]{:S(2)}, u32[]{:S(2)}) collective-permute-start(bf16[4,7168]{1,0:T(4,128)(2,1)S(1)} %collective-permute-done.4.refs_1_), channel_id=1, source_target_pairs={{0,2},{1,3},{2,0},{3,1},{4,6},{5,7},{6,4},{7,5},{8,10},{9,11},{10,... | collective-permute-start | bytes 172040 | tf_op jit(solution)/shard_map/ppermute | solution.py:363
  19.4 1.2 %copy-done = s32[56,4096]{1,0:T(8,128)S(1)} copy-done((s32[56,4096]{1,0:T(8,128)S(1)}, s32[56,4096]{1,0:T(8,128)}, u32[]{:S(2)}) %copy-start) | copy-done | bytes 917528
  20.5 0.7 %copy-done.1 = s32[56]{0:T(128)S(1)} copy-done((s32[56]{0:T(128)S(1)}, s32[56]{0:T(128)}, u32[]{:S(2)}) %copy-start.1) | copy-done | bytes 248
  21.2 1.0 %shard_map.57.target_ref = s8[28,32,4096]{2,1,0:T(32,128)(4,1)S(1)} custom-call(s32[56]{0:T(128)S(1)} %copy-done.1, s32[56,4096]{1,0:T(8,128)S(1)} %copy-done), custom_call_target="tpu_custom_call" | custom-call | flops 3670016 | bytes 4128768 | tf_op jit(solution)/shard_map/pallas_call | solution.py:240
  22.2 1.5 %collective-permute-start.12 = (bf16[4,7168]{1,0:T(4,128)(2,1)S(1)}, bf16[4,7168]{1,0:T(4,128)(2,1)S(1)}, u32[]{:S(2)}, u32[]{:S(2)}) collective-permute-start(bf16[4,7168]{1,0:T(4,128)(2,1)S(1)} %collective-permute-done.3.refs_2_), channel_id=1, source_target_pairs={{0,2},{1,3},{2,0},{3,1},{4,6},{5,7},{6,4},{7,5},{8,10},{9,11},{10,... | collective-permute-start | bytes 172040 | tf_op jit(solution)/shard_map/ppermute | solution.py:363
  23.8 0.7 %collective-permute-start.13 = (bf16[4,7168]{1,0:T(4,128)(2,1)S(1)}, bf16[4,7168]{1,0:T(4,128)(2,1)S(1)}, u32[]{:S(2)}, u32[]{:S(2)}) collective-permute-start(bf16[4,7168]{1,0:T(4,128)(2,1)S(1)} %collective-permute-done.8.refs_3_), channel_id=1, source_target_pairs={{0,2},{1,3},{2,0},{3,1},{4,6},{5,7},{6,4},{7,5},{8,10},{9,11},{10,... | collective-permute-start | bytes 172040 | tf_op jit(solution)/shard_map/ppermute | solution.py:363
  24.5 2.0 %collective-permute-done.12.refs_2_ = bf16[4,7168]{1,0:T(4,128)(2,1)S(1)} collective-permute-done((bf16[4,7168]{1,0:T(4,128)(2,1)S(1)}, bf16[4,7168]{1,0:T(4,128)(2,1)S(1)}, u32[]{:S(2)}, u32[]{:S(2)}) %collective-permute-start.12) | collective-permute-done | bytes 57376 | tf_op jit(solution)/shard_map/ppermute | solution.py:363
  26.8 0.6 %collective-permute-start.11 = (bf16[4,7168]{1,0:T(4,128)(2,1)S(1)}, bf16[4,7168]{1,0:T(4,128)(2,1)S(1)}, u32[]{:S(2)}, u32[]{:S(2)}) collective-permute-start(bf16[4,7168]{1,0:T(4,128)(2,1)S(1)} %collective-permute-done.8.refs_3_), channel_id=1, source_target_pairs={{0,1},{1,0},{2,3},{3,2},{4,5},{5,4},{6,7},{7,6},{8,9},{9,8},{10,11... | collective-permute-start | bytes 172040 | tf_op jit(solution)/shard_map/ppermute | solution.py:363
  27.4 0.4 %collective-permute-start.10 = (bf16[4,7168]{1,0:T(4,128)(2,1)S(1)}, bf16[4,7168]{1,0:T(4,128)(2,1)S(1)}, u32[]{:S(2)}, u32[]{:S(2)}) collective-permute-start(bf16[4,7168]{1,0:T(4,128)(2,1)S(1)} %collective-permute-done.3.refs_2_), channel_id=1, source_target_pairs={{0,1},{1,0},{2,3},{3,2},{4,5},{5,4},{6,7},{7,6},{8,9},{9,8},{10,11... | collective-permute-start | bytes 172040 | tf_op jit(solution)/shard_map/ppermute | solution.py:363
  28.3 0.4 collective-permute-start.17
  29.8 1.9 %shard_map.64 = (f32[32,1792]{1,0:T(8,128)S(1)}, bf16[32,1792]{1,0:T(8,128)(2,1)S(1)}) custom-call(s8[28,32,4096]{2,1,0:T(32,128)(4,1)S(1)} %shard_map.57.target_ref, f8e4m3fn[32,7168]{1,0:T(32,128)(4,1)S(1)} %get-tuple-element.42.refs_0_, f8e4m3fn[32,7168]{1,0:T(32,128)(4,1)S(1)} %get-tuple-element.45.refs_1_, ...), custom_call_target="tpu_custom_call" | custom-call | flops 458752 | bytes 64 | tf_op jit(solution)/shard_map/pallas_call | solution.py:319
  31.7 1.6 %collective-permute-start.20 = (bf16[32,1792]{1,0:T(8,128)(2,1)S(1)}, bf16[32,1792]{1,0:T(8,128)(2,1)S(1)}, u32[]{:S(2)}, u32[]{:S(2)}) collective-permute-start(bf16[32,1792]{1,0:T(8,128)(2,1)S(1)} %get-tuple-element.60), channel_id=1, source_target_pairs={{0,16},{16,0},{1,17},{17,1},{2,18},{18,2},{3,19},{19,3},{4,20},{20... | collective-permute-start | bytes 344072 | tf_op jit(solution)/shard_map/ppermute | solution.py:363
  33.3 1.4 %shard_map.63 = (f32[32,1280]{1,0:T(8,128)S(1)}, bf16[32,1280]{1,0:T(8,128)(2,1)S(1)}) custom-call(s8[28,32,4096]{2,1,0:T(32,128)(4,1)S(1)} %shard_map.57.target_ref, f8e4m3fn[32,7168]{1,0:T(32,128)(4,1)S(1)} %get-tuple-element.42.refs_0_, f8e4m3fn[32,7168]{1,0:T(32,128)(4,1)S(1)} %get-tuple-element.45.refs_1_, ...), custom_call_target="tpu_custom_call" | custom-call | flops 327680 | bytes 64 | tf_op jit(solution)/shard_map/pallas_call | solution.py:319
  34.6 0.6 %collective-permute-start.19 = (bf16[32,1280]{1,0:T(8,128)(2,1)S(1)}, bf16[32,1280]{1,0:T(8,128)(2,1)S(1)}, u32[]{:S(2)}, u32[]{:S(2)}) collective-permute-start(bf16[32,1280]{1,0:T(8,128)(2,1)S(1)} %get-tuple-element.58), channel_id=1, source_target_pairs={{0,16},{16,0},{1,17},{17,1},{2,18},{18,2},{3,19},{19,3},{4,20},{20... | collective-permute-start | bytes 245768 | tf_op jit(solution)/shard_map/ppermute | solution.py:363
  35.3 1.1 %shard_map.62 = (f32[32,1024]{1,0:T(8,128)S(1)}, bf16[32,1024]{1,0:T(8,128)(2,1)S(1)}) custom-call(s8[28,32,4096]{2,1,0:T(32,128)(4,1)S(1)} %shard_map.57.target_ref, f8e4m3fn[32,7168]{1,0:T(32,128)(4,1)S(1)} %get-tuple-element.42.refs_0_, f8e4m3fn[32,7168]{1,0:T(32,128)(4,1)S(1)} %get-tuple-element.45.refs_1_, ...), custom_call_target="tpu_custom_call" | custom-call | flops 262144 | bytes 64 | tf_op jit(solution)/shard_map/pallas_call | solution.py:319
  36.4 1.6 %collective-permute-start.18 = (bf16[32,1024]{1,0:T(8,128)(2,1)S(1)}, bf16[32,1024]{1,0:T(8,128)(2,1)S(1)}, u32[]{:S(2)}, u32[]{:S(2)}) collective-permute-start(bf16[32,1024]{1,0:T(8,128)(2,1)S(1)} %get-tuple-element.56), channel_id=1, source_target_pairs={{0,16},{16,0},{1,17},{17,1},{2,18},{18,2},{3,19},{19,3},{4,20},{20... | collective-permute-start | bytes 196616 | tf_op jit(solution)/shard_map/ppermute | solution.py:363
  37.9 0.7 %shard_map.65.refs_0_ = f32[32,4096]{1,0:T(8,128)} custom-call(f32[32,1792]{1,0:T(8,128)S(1)} %get-tuple-element.59.kept_ref, bf16[32,1792]{1,0:T(8,128)(2,1)S(1)} %collective-permute-done.20.came_ref), custom_call_target="tpu_custom_call" | custom-call | flops 57344 | bytes 229376 | tf_op jit(solution)/shard_map/pallas_call | solution.py:347
  38.7 0.9 %collective-permute-done.19.came_ref = bf16[32,1280]{1,0:T(8,128)(2,1)S(1)} collective-permute-done((bf16[32,1280]{1,0:T(8,128)(2,1)S(1)}, bf16[32,1280]{1,0:T(8,128)(2,1)S(1)}, u32[]{:S(2)}, u32[]{:S(2)}) %collective-permute-start.19) | collective-permute-done | bytes 81952 | tf_op jit(solution)/shard_map/ppermute | solution.py:363
  39.5 0.7 %shard_map.66.refs_0_ = f32[32,4096]{1,0:T(8,128)} custom-call(f32[32,1280]{1,0:T(8,128)S(1)} %get-tuple-element.57.kept_ref, bf16[32,1280]{1,0:T(8,128)(2,1)S(1)} %collective-permute-done.19.came_ref, f32[32,4096]{1,0:T(8,128)} %shard_map.65.refs_0_), custom_call_target="tpu_custom_call", output_to_operand_aliasing={{}: (2, {})} | custom-call | flops 40960 | bytes 163840 | tf_op jit(solution)/shard_map/pallas_call | solution.py:347
  40.2 0.5 %collective-permute-done.18.came_ref = bf16[32,1024]{1,0:T(8,128)(2,1)S(1)} collective-permute-done((bf16[32,1024]{1,0:T(8,128)(2,1)S(1)}, bf16[32,1024]{1,0:T(8,128)(2,1)S(1)}, u32[]{:S(2)}, u32[]{:S(2)}) %collective-permute-start.18) | collective-permute-done | bytes 65568 | tf_op jit(solution)/shard_map/ppermute | solution.py:363
  40.7 0.7 %shard_map.67 = f32[32,4096]{1,0:T(8,128)} custom-call(f32[32,1024]{1,0:T(8,128)S(1)} %get-tuple-element.55.kept_ref, bf16[32,1024]{1,0:T(8,128)(2,1)S(1)} %collective-permute-done.18.came_ref, f32[32,4096]{1,0:T(8,128)} %shard_map.66.refs_0_), custom_call_target="tpu_custom_call", output_to_operand_aliasing={{}: (2, {})} | custom-call | flops 32768 | bytes 131072 | tf_op jit(solution)/shard_map/pallas_call | solution.py:347
  (32 shorter events, 2.1 us)
Async XLA Ops:
  1.4 4.7 %collective-permute-start = (bf16[2,4096]{1,0:T(2,128)(2,1)S(1)}, bf16[2,4096]{1,0:T(2,128)(2,1)S(1)}, u32[]{:S(2)}, u32[]{:S(2)}) collective-permute-start(bf16[2,4096]{1,0:T(2,128)(2,1)S(1)} %dynamic-slice_bitcast_fusion), channel_id=1, source_target_pairs={{0,16},{16,0},{1,17},{17,1},{2,18},{18,2},{3,19},{19,3},{4,20},{20... | collective-permute-start | bytes 49160 | tf_op jit(solution)/shard_map/ppermute | solution.py:363
  6.2 5.9 %collective-permute-start.2 = (bf16[2,128]{1,0:T(2,128)(2,1)S(1)}, bf16[2,128]{1,0:T(2,128)(2,1)S(1)}, u32[]{:S(2)}, u32[]{:S(2)}) collective-permute-start(bf16[2,128]{1,0:T(2,128)(2,1)S(1)} %get-tuple-element.61), channel_id=1, source_target_pairs={{1,2},{3,4},{5,6},{7,8},{9,10},{11,12},{13,14},{2,1},{4,3},{6,5},{... | collective-permute-start | bytes 1544 | tf_op jit(solution)/shard_map/ppermute | solution.py:372
  6.8 5.3 %collective-permute-start.1 = (bf16[2,128]{1,0:T(2,128)(2,1)S(1)}, bf16[2,128]{1,0:T(2,128)(2,1)S(1)}, u32[]{:S(2)}, u32[]{:S(2)}) collective-permute-start(bf16[2,128]{1,0:T(2,128)(2,1)S(1)} %get-tuple-element.62), channel_id=1, source_target_pairs={{0,1},{1,0},{2,3},{3,2},{4,5},{5,4},{6,7},{7,6},{8,9},{9,8},{10,11... | collective-permute-start | bytes 1544 | tf_op jit(solution)/shard_map/ppermute | solution.py:363
  12.8 6.0 %collective-permute-start.4 = (bf16[4,7168]{1,0:T(4,128)(2,1)S(1)}, bf16[4,7168]{1,0:T(4,128)(2,1)S(1)}, u32[]{:S(2)}, u32[]{:S(2)}) collective-permute-start(bf16[4,7168]{1,0:T(4,128)(2,1)S(1)} %shard_map.56.refs_0_), channel_id=1, source_target_pairs={{0,4},{1,5},{2,6},{3,7},{4,0},{5,1},{6,2},{7,3},{8,12},{9,13},{10,... | collective-permute-start | bytes 172040 | tf_op jit(solution)/shard_map/ppermute | solution.py:363
  14.7 7.5 %collective-permute-start.3 = (bf16[4,7168]{1,0:T(4,128)(2,1)S(1)}, bf16[4,7168]{1,0:T(4,128)(2,1)S(1)}, u32[]{:S(2)}, u32[]{:S(2)}) collective-permute-start(bf16[4,7168]{1,0:T(4,128)(2,1)S(1)} %shard_map.56.refs_0_), channel_id=1, source_target_pairs={{0,8},{1,9},{2,10},{3,11},{4,12},{5,13},{6,14},{7,15},{8,0},{9,1},... | collective-permute-start | bytes 172040 | tf_op jit(solution)/shard_map/ppermute | solution.py:363
  17.3 4.9 %collective-permute-start.5 = (bf16[4,7168]{1,0:T(4,128)(2,1)S(1)}, bf16[4,7168]{1,0:T(4,128)(2,1)S(1)}, u32[]{:S(2)}, u32[]{:S(2)}) collective-permute-start(bf16[4,7168]{1,0:T(4,128)(2,1)S(1)} %shard_map.56.refs_0_), channel_id=1, source_target_pairs={{0,1},{1,0},{2,3},{3,2},{4,5},{5,4},{6,7},{7,6},{8,9},{9,8},{10,11... | collective-permute-start | bytes 172040 | tf_op jit(solution)/shard_map/ppermute | solution.py:363
  17.3 6.4 %collective-permute-start.8 = (bf16[4,7168]{1,0:T(4,128)(2,1)S(1)}, bf16[4,7168]{1,0:T(4,128)(2,1)S(1)}, u32[]{:S(2)}, u32[]{:S(2)}) collective-permute-start(bf16[4,7168]{1,0:T(4,128)(2,1)S(1)} %shard_map.56.refs_0_), channel_id=1, source_target_pairs={{0,12},{1,13},{2,14},{3,15},{4,8},{5,9},{6,10},{7,11},{8,4},{9,5},... | collective-permute-start | bytes 172040 | tf_op jit(solution)/shard_map/ppermute | solution.py:363
  17.3 6.4 %collective-permute-start.6 = (bf16[4,7168]{1,0:T(4,128)(2,1)S(1)}, bf16[4,7168]{1,0:T(4,128)(2,1)S(1)}, u32[]{:S(2)}, u32[]{:S(2)}) collective-permute-start(bf16[4,7168]{1,0:T(4,128)(2,1)S(1)} %shard_map.56.refs_0_), channel_id=1, source_target_pairs={{0,2},{1,3},{2,0},{3,1},{4,6},{5,7},{6,4},{7,5},{8,10},{9,11},{10,... | collective-permute-start | bytes 172040 | tf_op jit(solution)/shard_map/ppermute | solution.py:363
  18.7 5.0 %collective-permute-start.7 = (bf16[4,7168]{1,0:T(4,128)(2,1)S(1)}, bf16[4,7168]{1,0:T(4,128)(2,1)S(1)}, u32[]{:S(2)}, u32[]{:S(2)}) collective-permute-start(bf16[4,7168]{1,0:T(4,128)(2,1)S(1)} %collective-permute-done.4.refs_1_), channel_id=1, source_target_pairs={{0,2},{1,3},{2,0},{3,1},{4,6},{5,7},{6,4},{7,5},{8,10},{9,11},{10,... | collective-permute-start | bytes 172040 | tf_op jit(solution)/shard_map/ppermute | solution.py:363
  19.4 1.2 %copy-start = (s32[56,4096]{1,0:T(8,128)S(1)}, s32[56,4096]{1,0:T(8,128)}, u32[]{:S(2)}) copy-start(s32[56,4096]{1,0:T(8,128)} %delay_ref) | copy-start | bytes 2752516
  20.5 0.7 %copy-start.1 = (s32[56]{0:T(128)S(1)}, s32[56]{0:T(128)}, u32[]{:S(2)}) copy-start(s32[56]{0:T(128)} %offset_ref.1) | copy-start | bytes 676
  22.2 4.2 %collective-permute-start.12 = (bf16[4,7168]{1,0:T(4,128)(2,1)S(1)}, bf16[4,7168]{1,0:T(4,128)(2,1)S(1)}, u32[]{:S(2)}, u32[]{:S(2)}) collective-permute-start(bf16[4,7168]{1,0:T(4,128)(2,1)S(1)} %collective-permute-done.3.refs_2_), channel_id=1, source_target_pairs={{0,2},{1,3},{2,0},{3,1},{4,6},{5,7},{6,4},{7,5},{8,10},{9,11},{10,... | collective-permute-start | bytes 172040 | tf_op jit(solution)/shard_map/ppermute | solution.py:363
  23.7 3.1 %collective-permute-start.9 = (bf16[4,7168]{1,0:T(4,128)(2,1)S(1)}, bf16[4,7168]{1,0:T(4,128)(2,1)S(1)}, u32[]{:S(2)}, u32[]{:S(2)}) collective-permute-start(bf16[4,7168]{1,0:T(4,128)(2,1)S(1)} %collective-permute-done.4.refs_1_), channel_id=1, source_target_pairs={{0,1},{1,0},{2,3},{3,2},{4,5},{5,4},{6,7},{7,6},{8,9},{9,8},{10,11... | collective-permute-start | bytes 172040 | tf_op jit(solution)/shard_map/ppermute | solution.py:363
  23.8 4.3 %collective-permute-start.13 = (bf16[4,7168]{1,0:T(4,128)(2,1)S(1)}, bf16[4,7168]{1,0:T(4,128)(2,1)S(1)}, u32[]{:S(2)}, u32[]{:S(2)}) collective-permute-start(bf16[4,7168]{1,0:T(4,128)(2,1)S(1)} %collective-permute-done.8.refs_3_), channel_id=1, source_target_pairs={{0,2},{1,3},{2,0},{3,1},{4,6},{5,7},{6,4},{7,5},{8,10},{9,11},{10,... | collective-permute-start | bytes 172040 | tf_op jit(solution)/shard_map/ppermute | solution.py:363
  26.5 1.7 %collective-permute-start.14 = (bf16[4,7168]{1,0:T(4,128)(2,1)S(1)}, bf16[4,7168]{1,0:T(4,128)(2,1)S(1)}, u32[]{:S(2)}, u32[]{:S(2)}) collective-permute-start(bf16[4,7168]{1,0:T(4,128)(2,1)S(1)} %collective-permute-done.12.refs_2_), channel_id=1, source_target_pairs={{0,1},{1,0},{2,3},{3,2},{4,5},{5,4},{6,7},{7,6},{8,9},{9,8},{10,11... | collective-permute-start | bytes 172040 | tf_op jit(solution)/shard_map/ppermute | solution.py:363
  26.8 1.5 %collective-permute-start.11 = (bf16[4,7168]{1,0:T(4,128)(2,1)S(1)}, bf16[4,7168]{1,0:T(4,128)(2,1)S(1)}, u32[]{:S(2)}, u32[]{:S(2)}) collective-permute-start(bf16[4,7168]{1,0:T(4,128)(2,1)S(1)} %collective-permute-done.8.refs_3_), channel_id=1, source_target_pairs={{0,1},{1,0},{2,3},{3,2},{4,5},{5,4},{6,7},{7,6},{8,9},{9,8},{10,11... | collective-permute-start | bytes 172040 | tf_op jit(solution)/shard_map/ppermute | solution.py:363
  27.4 1.9 %collective-permute-start.15 = (bf16[4,7168]{1,0:T(4,128)(2,1)S(1)}, bf16[4,7168]{1,0:T(4,128)(2,1)S(1)}, u32[]{:S(2)}, u32[]{:S(2)}) collective-permute-start(bf16[4,7168]{1,0:T(4,128)(2,1)S(1)} %collective-permute-done.6.refs_0_), channel_id=1, source_target_pairs={{0,1},{1,0},{2,3},{3,2},{4,5},{5,4},{6,7},{7,6},{8,9},{9,8},{10,11... | collective-permute-start | bytes 172040 | tf_op jit(solution)/shard_map/ppermute | solution.py:363
  27.4 1.5 %collective-permute-start.10 = (bf16[4,7168]{1,0:T(4,128)(2,1)S(1)}, bf16[4,7168]{1,0:T(4,128)(2,1)S(1)}, u32[]{:S(2)}, u32[]{:S(2)}) collective-permute-start(bf16[4,7168]{1,0:T(4,128)(2,1)S(1)} %collective-permute-done.3.refs_2_), channel_id=1, source_target_pairs={{0,1},{1,0},{2,3},{3,2},{4,5},{5,4},{6,7},{7,6},{8,9},{9,8},{10,11... | collective-permute-start | bytes 172040 | tf_op jit(solution)/shard_map/ppermute | solution.py:363
  28.1 1.2 %collective-permute-start.16 = (bf16[4,7168]{1,0:T(4,128)(2,1)S(1)}, bf16[4,7168]{1,0:T(4,128)(2,1)S(1)}, u32[]{:S(2)}, u32[]{:S(2)}) collective-permute-start(bf16[4,7168]{1,0:T(4,128)(2,1)S(1)} %collective-permute-done.7.refs_1_), channel_id=1, source_target_pairs={{0,1},{1,0},{2,3},{3,2},{4,5},{5,4},{6,7},{7,6},{8,9},{9,8},{10,11... | collective-permute-start | bytes 172040 | tf_op jit(solution)/shard_map/ppermute | solution.py:363
  28.3 1.3 %collective-permute-start.17 = (bf16[4,7168]{1,0:T(4,128)(2,1)S(1)}, bf16[4,7168]{1,0:T(4,128)(2,1)S(1)}, u32[]{:S(2)}, u32[]{:S(2)}) collective-permute-start(bf16[4,7168]{1,0:T(4,128)(2,1)S(1)} %collective-permute-done.13.refs_3_), channel_id=1, source_target_pairs={{0,1},{1,0},{2,3},{3,2},{4,5},{5,4},{6,7},{7,6},{8,9},{9,8},{10,11... | collective-permute-start | bytes 172040 | tf_op jit(solution)/shard_map/ppermute | solution.py:363
  31.7 6.2 %collective-permute-start.20 = (bf16[32,1792]{1,0:T(8,128)(2,1)S(1)}, bf16[32,1792]{1,0:T(8,128)(2,1)S(1)}, u32[]{:S(2)}, u32[]{:S(2)}) collective-permute-start(bf16[32,1792]{1,0:T(8,128)(2,1)S(1)} %get-tuple-element.60), channel_id=1, source_target_pairs={{0,16},{16,0},{1,17},{17,1},{2,18},{18,2},{3,19},{19,3},{4,20},{20... | collective-permute-start | bytes 344072 | tf_op jit(solution)/shard_map/ppermute | solution.py:363
  34.6 4.9 %collective-permute-start.19 = (bf16[32,1280]{1,0:T(8,128)(2,1)S(1)}, bf16[32,1280]{1,0:T(8,128)(2,1)S(1)}, u32[]{:S(2)}, u32[]{:S(2)}) collective-permute-start(bf16[32,1280]{1,0:T(8,128)(2,1)S(1)} %get-tuple-element.58), channel_id=1, source_target_pairs={{0,16},{16,0},{1,17},{17,1},{2,18},{18,2},{3,19},{19,3},{4,20},{20... | collective-permute-start | bytes 245768 | tf_op jit(solution)/shard_map/ppermute | solution.py:363
  36.4 4.3 %collective-permute-start.18 = (bf16[32,1024]{1,0:T(8,128)(2,1)S(1)}, bf16[32,1024]{1,0:T(8,128)(2,1)S(1)}, u32[]{:S(2)}, u32[]{:S(2)}) collective-permute-start(bf16[32,1024]{1,0:T(8,128)(2,1)S(1)} %get-tuple-element.56), channel_id=1, source_target_pairs={{0,16},{16,0},{1,17},{17,1},{2,18},{18,2},{3,19},{19,3},{4,20},{20... | collective-permute-start | bytes 196616 | tf_op jit(solution)/shard_map/ppermute | solution.py:363

commit v6 on v5

--- a/solution.py
+++ b/solution.py
@@ -127,7 +127,7 @@
             total = total + extra[1]
         total = total * factor
         top = jnp.max(jnp.max(jnp.abs(total), axis=1, keepdims=True), axis=0, keepdims=True)
-        power = jnp.floor(jnp.log2(224.0 / jnp.maximum(top, 1e-35)))
+        power = jnp.minimum(jnp.floor(jnp.log2(224.0 / jnp.maximum(top, 1e-35))), 118.0)
         scale = jnp.exp2(power).astype(jnp.bfloat16).astype(jnp.float32)
         total = jnp.where(column == 0, power, total * scale)
         for h in range(LAGS // LANES):

time: 41.6 us -> 41.6 us (level)
  no operation moved by 1% of the time
where the time goes in v6:
time: 41.6 us; the launch traced here: 41.4 us
  starting transfers between devices  21.1 us (51%)
  Pallas kernels  11.1 us (27%)
  waiting for transfers between devices  4.39 us (11%)
  local copies, waits for them, and re-layouts  2.57 us (6%)
  other arithmetic  1.33 us (3%)
  between operations  0.87 us (2%)
    ppermute x20, starting transfers between devices, flip(): return lax.ppermute(block, axis, [(i, i ^ mask) for i in range(count)])  20.5 us
    ppermute x20, waiting for transfers between devices, flip(): return lax.ppermute(block, axis, [(i, i ^ mask) for i in range(count)])  4.39 us
    pallas_call x3, Pallas kernels, image(): pl.pallas_call(functools.partial(image_kernel, swap, len(pieces), start),...  4.38 us
    pallas_call x3, Pallas kernels, add_part(): pl.pallas_call(functools.partial(add_kernel, start), out_shape=jax.ShapeD...  2.08 us
    unnamed x4, local copies, waits for them, and re-layouts  1.83 us
    pallas_call x1, Pallas kernels, correlate(): pl.pallas_call(corr_kernel, out_shape=jax.ShapeDtypeStruct((pitch * slice...  1.78 us
    transpose x1, other arithmetic, shards(): windowed = jnp.transpose(windowed, (1, 0, 2))  1.29 us
    pallas_call x4, Pallas kernels, split(): pl.pallas_call(split_kernel, out_shape=[jax.ShapeDtypeStruct((rows, colum...  1.25 us
  transfers between devices with their start and end apart: 21, of which 8 were waited for; matrix products, arithmetic and copies ran while one was open for 3% of the time, Pallas kernels for 18%

profile of v6, /device:TPU:0, one launch (start us, length us, event | category | flops | bytes accessed | tf_op | source)
XLA Modules:
  0.0 41.4 jit_solution(2499709036744346217)
XLA Ops:
  0.7 0.7 %dynamic-slice_bitcast_fusion = bf16[2,4096]{1,0:T(2,128)(2,1)S(1)} fusion(bf16[28,2,4096]{2,1,0:T(2,128)(2,1)} %param.5, s32[]{:T(128)S(6)} %select_n.50), kind=kLoop, calls=%fused_computation.3 | loop fusion | bytes 32772 | tf_op jit(solution)/shard_map/jit(dynamic_index_in_dim)/squeeze | solution.py:420
  1.4 3.0 %collective-permute-start = (bf16[2,4096]{1,0:T(2,128)(2,1)S(1)}, bf16[2,4096]{1,0:T(2,128)(2,1)S(1)}, u32[]{:S(2)}, u32[]{:S(2)}) collective-permute-start(bf16[2,4096]{1,0:T(2,128)(2,1)S(1)} %dynamic-slice_bitcast_fusion), channel_id=1, source_target_pairs={{0,16},{16,0},{1,17},{17,1},{2,18},{18,2},{3,19},{19,3},{4,20},{20... | collective-permute-start | bytes 49160 | tf_op jit(solution)/shard_map/ppermute | solution.py:363
  4.4 1.3 %fusion.win_ref = bf16[2,28,4096]{2,1,0:T(8,128)(2,1)S(1)} fusion(bf16[28,2,4096]{2,1,0:T(2,128)(2,1)} %param.5, f32[4096]{0:T(1024)} %constant.48.clone), kind=kLoop, calls=%fused_computation.1 | loop fusion | flops 688128 | bytes 933888 | tf_op jit(solution)/shard_map/transpose | solution.py:437
  5.7 0.4 collective-permute-done
  6.2 0.7 %collective-permute-start.2 = (bf16[2,128]{1,0:T(2,128)(2,1)S(1)}, bf16[2,128]{1,0:T(2,128)(2,1)S(1)}, u32[]{:S(2)}, u32[]{:S(2)}) collective-permute-start(bf16[2,128]{1,0:T(2,128)(2,1)S(1)} %get-tuple-element.61), channel_id=1, source_target_pairs={{1,2},{3,4},{5,6},{7,8},{9,10},{11,12},{13,14},{2,1},{4,3},{6,5},{... | collective-permute-start | bytes 1544 | tf_op jit(solution)/shard_map/ppermute | solution.py:372
  6.8 3.5 %collective-permute-start.1 = (bf16[2,128]{1,0:T(2,128)(2,1)S(1)}, bf16[2,128]{1,0:T(2,128)(2,1)S(1)}, u32[]{:S(2)}, u32[]{:S(2)}) collective-permute-start(bf16[2,128]{1,0:T(2,128)(2,1)S(1)} %get-tuple-element.62), channel_id=1, source_target_pairs={{0,1},{1,0},{2,3},{3,2},{4,5},{5,4},{6,7},{7,6},{8,9},{9,8},{10,11... | collective-permute-start | bytes 1544 | tf_op jit(solution)/shard_map/ppermute | solution.py:363
  10.3 1.8 %shard_map.55.part_ref = f32[128,256]{1,0:T(8,128)S(1)} custom-call(bf16[2,28,4096]{2,1,0:T(8,128)(2,1)S(1)} %fusion.win_ref, bf16[2,4096]{1,0:T(2,128)(2,1)S(1)} %broadcast_select_fusion.ref_ref.body_ref), custom_call_target="tpu_custom_call" | custom-call | flops 117440512 | bytes 458752 | tf_op jit(solution)/shard_map/pallas_call | solution.py:150
  12.1 0.6 %shard_map.56.refs_0_ = bf16[4,7168]{1,0:T(4,128)(2,1)S(1)} custom-call(s32[1]{0:T(128)S(6)} %copy.12.ref_ref, bf16[2,28,4096]{2,1,0:T(8,128)(2,1)S(1)} %fusion.win_ref, bf16[2,4096]{1,0:T(2,128)(2,1)S(1)} %broadcast_select_fusion.ref_ref.body_ref, bf16[2,128]{1,0:T(2,128)(2,1)S(1)} %get-tuple-element.64.low_ref, ...), custom_call_target="tpu_custom_call" | custom-call | flops 14680064 | bytes 28672 | tf_op jit(solution)/shard_map/pallas_call | solution.py:166
  12.8 2.0 %collective-permute-start.4 = (bf16[4,7168]{1,0:T(4,128)(2,1)S(1)}, bf16[4,7168]{1,0:T(4,128)(2,1)S(1)}, u32[]{:S(2)}, u32[]{:S(2)}) collective-permute-start(bf16[4,7168]{1,0:T(4,128)(2,1)S(1)} %shard_map.56.refs_0_), channel_id=1, source_target_pairs={{0,4},{1,5},{2,6},{3,7},{4,0},{5,1},{6,2},{7,3},{8,12},{9,13},{10,... | collective-permute-start | bytes 172040 | tf_op jit(solution)/shard_map/ppermute | solution.py:363
  14.7 2.6 %collective-permute-start.3 = (bf16[4,7168]{1,0:T(4,128)(2,1)S(1)}, bf16[4,7168]{1,0:T(4,128)(2,1)S(1)}, u32[]{:S(2)}, u32[]{:S(2)}) collective-permute-start(bf16[4,7168]{1,0:T(4,128)(2,1)S(1)} %shard_map.56.refs_0_), channel_id=1, source_target_pairs={{0,8},{1,9},{2,10},{3,11},{4,12},{5,13},{6,14},{7,15},{8,0},{9,1},... | collective-permute-start | bytes 172040 | tf_op jit(solution)/shard_map/ppermute | solution.py:363
  17.3 1.4 %collective-permute-start.6 = (bf16[4,7168]{1,0:T(4,128)(2,1)S(1)}, bf16[4,7168]{1,0:T(4,128)(2,1)S(1)}, u32[]{:S(2)}, u32[]{:S(2)}) collective-permute-start(bf16[4,7168]{1,0:T(4,128)(2,1)S(1)} %shard_map.56.refs_0_), channel_id=1, source_target_pairs={{0,2},{1,3},{2,0},{3,1},{4,6},{5,7},{6,4},{7,5},{8,10},{9,11},{10,... | collective-permute-start | bytes 172040 | tf_op jit(solution)/shard_map/ppermute | solution.py:363
  18.7 0.6 %collective-permute-start.7 = (bf16[4,7168]{1,0:T(4,128)(2,1)S(1)}, bf16[4,7168]{1,0:T(4,128)(2,1)S(1)}, u32[]{:S(2)}, u32[]{:S(2)}) collective-permute-start(bf16[4,7168]{1,0:T(4,128)(2,1)S(1)} %collective-permute-done.4.refs_1_), channel_id=1, source_target_pairs={{0,2},{1,3},{2,0},{3,1},{4,6},{5,7},{6,4},{7,5},{8,10},{9,11},{10,... | collective-permute-start | bytes 172040 | tf_op jit(solution)/shard_map/ppermute | solution.py:363
  19.4 1.2 %copy-done = s32[56,4096]{1,0:T(8,128)S(1)} copy-done((s32[56,4096]{1,0:T(8,128)S(1)}, s32[56,4096]{1,0:T(8,128)}, u32[]{:S(2)}) %copy-start) | copy-done | bytes 917528
  20.5 0.7 %copy-done.1 = s32[56]{0:T(128)S(1)} copy-done((s32[56]{0:T(128)S(1)}, s32[56]{0:T(128)}, u32[]{:S(2)}) %copy-start.1) | copy-done | bytes 248
  21.2 1.0 %shard_map.57.target_ref = s8[28,32,4096]{2,1,0:T(32,128)(4,1)S(1)} custom-call(s32[56]{0:T(128)S(1)} %copy-done.1, s32[56,4096]{1,0:T(8,128)S(1)} %copy-done), custom_call_target="tpu_custom_call" | custom-call | flops 3670016 | bytes 4128768 | tf_op jit(solution)/shard_map/pallas_call | solution.py:240
  22.2 1.5 %collective-permute-start.12 = (bf16[4,7168]{1,0:T(4,128)(2,1)S(1)}, bf16[4,7168]{1,0:T(4,128)(2,1)S(1)}, u32[]{:S(2)}, u32[]{:S(2)}) collective-permute-start(bf16[4,7168]{1,0:T(4,128)(2,1)S(1)} %collective-permute-done.3.refs_2_), channel_id=1, source_target_pairs={{0,2},{1,3},{2,0},{3,1},{4,6},{5,7},{6,4},{7,5},{8,10},{9,11},{10,... | collective-permute-start | bytes 172040 | tf_op jit(solution)/shard_map/ppermute | solution.py:363
  23.8 0.7 %collective-permute-start.13 = (bf16[4,7168]{1,0:T(4,128)(2,1)S(1)}, bf16[4,7168]{1,0:T(4,128)(2,1)S(1)}, u32[]{:S(2)}, u32[]{:S(2)}) collective-permute-start(bf16[4,7168]{1,0:T(4,128)(2,1)S(1)} %collective-permute-done.8.refs_3_), channel_id=1, source_target_pairs={{0,2},{1,3},{2,0},{3,1},{4,6},{5,7},{6,4},{7,5},{8,10},{9,11},{10,... | collective-permute-start | bytes 172040 | tf_op jit(solution)/shard_map/ppermute | solution.py:363
  24.5 2.0 %collective-permute-done.12.refs_2_ = bf16[4,7168]{1,0:T(4,128)(2,1)S(1)} collective-permute-done((bf16[4,7168]{1,0:T(4,128)(2,1)S(1)}, bf16[4,7168]{1,0:T(4,128)(2,1)S(1)}, u32[]{:S(2)}, u32[]{:S(2)}) %collective-permute-start.12) | collective-permute-done | bytes 57376 | tf_op jit(solution)/shard_map/ppermute | solution.py:363
  26.8 0.6 %collective-permute-start.11 = (bf16[4,7168]{1,0:T(4,128)(2,1)S(1)}, bf16[4,7168]{1,0:T(4,128)(2,1)S(1)}, u32[]{:S(2)}, u32[]{:S(2)}) collective-permute-start(bf16[4,7168]{1,0:T(4,128)(2,1)S(1)} %collective-permute-done.8.refs_3_), channel_id=1, source_target_pairs={{0,1},{1,0},{2,3},{3,2},{4,5},{5,4},{6,7},{7,6},{8,9},{9,8},{10,11... | collective-permute-start | bytes 172040 | tf_op jit(solution)/shard_map/ppermute | solution.py:363
  27.4 0.4 %collective-permute-start.10 = (bf16[4,7168]{1,0:T(4,128)(2,1)S(1)}, bf16[4,7168]{1,0:T(4,128)(2,1)S(1)}, u32[]{:S(2)}, u32[]{:S(2)}) collective-permute-start(bf16[4,7168]{1,0:T(4,128)(2,1)S(1)} %collective-permute-done.3.refs_2_), channel_id=1, source_target_pairs={{0,1},{1,0},{2,3},{3,2},{4,5},{5,4},{6,7},{7,6},{8,9},{9,8},{10,11... | collective-permute-start | bytes 172040 | tf_op jit(solution)/shard_map/ppermute | solution.py:363
  28.3 0.4 collective-permute-start.17
  29.8 1.9 %shard_map.64 = (f32[32,1792]{1,0:T(8,128)S(1)}, bf16[32,1792]{1,0:T(8,128)(2,1)S(1)}) custom-call(s8[28,32,4096]{2,1,0:T(32,128)(4,1)S(1)} %shard_map.57.target_ref, f8e4m3fn[32,7168]{1,0:T(32,128)(4,1)S(1)} %get-tuple-element.42.refs_0_, f8e4m3fn[32,7168]{1,0:T(32,128)(4,1)S(1)} %get-tuple-element.45.refs_1_, ...), custom_call_target="tpu_custom_call" | custom-call | flops 458752 | bytes 64 | tf_op jit(solution)/shard_map/pallas_call | solution.py:319
  31.7 1.6 %collective-permute-start.20 = (bf16[32,1792]{1,0:T(8,128)(2,1)S(1)}, bf16[32,1792]{1,0:T(8,128)(2,1)S(1)}, u32[]{:S(2)}, u32[]{:S(2)}) collective-permute-start(bf16[32,1792]{1,0:T(8,128)(2,1)S(1)} %get-tuple-element.60), channel_id=1, source_target_pairs={{0,16},{16,0},{1,17},{17,1},{2,18},{18,2},{3,19},{19,3},{4,20},{20... | collective-permute-start | bytes 344072 | tf_op jit(solution)/shard_map/ppermute | solution.py:363
  33.3 1.4 %shard_map.63 = (f32[32,1280]{1,0:T(8,128)S(1)}, bf16[32,1280]{1,0:T(8,128)(2,1)S(1)}) custom-call(s8[28,32,4096]{2,1,0:T(32,128)(4,1)S(1)} %shard_map.57.target_ref, f8e4m3fn[32,7168]{1,0:T(32,128)(4,1)S(1)} %get-tuple-element.42.refs_0_, f8e4m3fn[32,7168]{1,0:T(32,128)(4,1)S(1)} %get-tuple-element.45.refs_1_, ...), custom_call_target="tpu_custom_call" | custom-call | flops 327680 | bytes 64 | tf_op jit(solution)/shard_map/pallas_call | solution.py:319
  34.6 0.6 %collective-permute-start.19 = (bf16[32,1280]{1,0:T(8,128)(2,1)S(1)}, bf16[32,1280]{1,0:T(8,128)(2,1)S(1)}, u32[]{:S(2)}, u32[]{:S(2)}) collective-permute-start(bf16[32,1280]{1,0:T(8,128)(2,1)S(1)} %get-tuple-element.58), channel_id=1, source_target_pairs={{0,16},{16,0},{1,17},{17,1},{2,18},{18,2},{3,19},{19,3},{4,20},{20... | collective-permute-start | bytes 245768 | tf_op jit(solution)/shard_map/ppermute | solution.py:363
  35.3 1.1 %shard_map.62 = (f32[32,1024]{1,0:T(8,128)S(1)}, bf16[32,1024]{1,0:T(8,128)(2,1)S(1)}) custom-call(s8[28,32,4096]{2,1,0:T(32,128)(4,1)S(1)} %shard_map.57.target_ref, f8e4m3fn[32,7168]{1,0:T(32,128)(4,1)S(1)} %get-tuple-element.42.refs_0_, f8e4m3fn[32,7168]{1,0:T(32,128)(4,1)S(1)} %get-tuple-element.45.refs_1_, ...), custom_call_target="tpu_custom_call" | custom-call | flops 262144 | bytes 64 | tf_op jit(solution)/shard_map/pallas_call | solution.py:319
  36.4 1.6 %collective-permute-start.18 = (bf16[32,1024]{1,0:T(8,128)(2,1)S(1)}, bf16[32,1024]{1,0:T(8,128)(2,1)S(1)}, u32[]{:S(2)}, u32[]{:S(2)}) collective-permute-start(bf16[32,1024]{1,0:T(8,128)(2,1)S(1)} %get-tuple-element.56), channel_id=1, source_target_pairs={{0,16},{16,0},{1,17},{17,1},{2,18},{18,2},{3,19},{19,3},{4,20},{20... | collective-permute-start | bytes 196616 | tf_op jit(solution)/shard_map/ppermute | solution.py:363
  37.9 0.7 %shard_map.65.refs_0_ = f32[32,4096]{1,0:T(8,128)} custom-call(f32[32,1792]{1,0:T(8,128)S(1)} %get-tuple-element.59.kept_ref, bf16[32,1792]{1,0:T(8,128)(2,1)S(1)} %collective-permute-done.20.came_ref), custom_call_target="tpu_custom_call" | custom-call | flops 57344 | bytes 229376 | tf_op jit(solution)/shard_map/pallas_call | solution.py:347
  38.7 0.9 %collective-permute-done.19.came_ref = bf16[32,1280]{1,0:T(8,128)(2,1)S(1)} collective-permute-done((bf16[32,1280]{1,0:T(8,128)(2,1)S(1)}, bf16[32,1280]{1,0:T(8,128)(2,1)S(1)}, u32[]{:S(2)}, u32[]{:S(2)}) %collective-permute-start.19) | collective-permute-done | bytes 81952 | tf_op jit(solution)/shard_map/ppermute | solution.py:363
  39.5 0.7 %shard_map.66.refs_0_ = f32[32,4096]{1,0:T(8,128)} custom-call(f32[32,1280]{1,0:T(8,128)S(1)} %get-tuple-element.57.kept_ref, bf16[32,1280]{1,0:T(8,128)(2,1)S(1)} %collective-permute-done.19.came_ref, f32[32,4096]{1,0:T(8,128)} %shard_map.65.refs_0_), custom_call_target="tpu_custom_call", output_to_operand_aliasing={{}: (2, {})} | custom-call | flops 40960 | bytes 163840 | tf_op jit(solution)/shard_map/pallas_call | solution.py:347
  40.2 0.5 %collective-permute-done.18.came_ref = bf16[32,1024]{1,0:T(8,128)(2,1)S(1)} collective-permute-done((bf16[32,1024]{1,0:T(8,128)(2,1)S(1)}, bf16[32,1024]{1,0:T(8,128)(2,1)S(1)}, u32[]{:S(2)}, u32[]{:S(2)}) %collective-permute-start.18) | collective-permute-done | bytes 65568 | tf_op jit(solution)/shard_map/ppermute | solution.py:363
  40.7 0.7 %shard_map.67 = f32[32,4096]{1,0:T(8,128)} custom-call(f32[32,1024]{1,0:T(8,128)S(1)} %get-tuple-element.55.kept_ref, bf16[32,1024]{1,0:T(8,128)(2,1)S(1)} %collective-permute-done.18.came_ref, f32[32,4096]{1,0:T(8,128)} %shard_map.66.refs_0_), custom_call_target="tpu_custom_call", output_to_operand_aliasing={{}: (2, {})} | custom-call | flops 32768 | bytes 131072 | tf_op jit(solution)/shard_map/pallas_call | solution.py:347
  (32 shorter events, 2.1 us)
Async XLA Ops:
  1.4 4.7 %collective-permute-start = (bf16[2,4096]{1,0:T(2,128)(2,1)S(1)}, bf16[2,4096]{1,0:T(2,128)(2,1)S(1)}, u32[]{:S(2)}, u32[]{:S(2)}) collective-permute-start(bf16[2,4096]{1,0:T(2,128)(2,1)S(1)} %dynamic-slice_bitcast_fusion), channel_id=1, source_target_pairs={{0,16},{16,0},{1,17},{17,1},{2,18},{18,2},{3,19},{19,3},{4,20},{20... | collective-permute-start | bytes 49160 | tf_op jit(solution)/shard_map/ppermute | solution.py:363
  6.2 5.9 %collective-permute-start.2 = (bf16[2,128]{1,0:T(2,128)(2,1)S(1)}, bf16[2,128]{1,0:T(2,128)(2,1)S(1)}, u32[]{:S(2)}, u32[]{:S(2)}) collective-permute-start(bf16[2,128]{1,0:T(2,128)(2,1)S(1)} %get-tuple-element.61), channel_id=1, source_target_pairs={{1,2},{3,4},{5,6},{7,8},{9,10},{11,12},{13,14},{2,1},{4,3},{6,5},{... | collective-permute-start | bytes 1544 | tf_op jit(solution)/shard_map/ppermute | solution.py:372
  6.8 5.3 %collective-permute-start.1 = (bf16[2,128]{1,0:T(2,128)(2,1)S(1)}, bf16[2,128]{1,0:T(2,128)(2,1)S(1)}, u32[]{:S(2)}, u32[]{:S(2)}) collective-permute-start(bf16[2,128]{1,0:T(2,128)(2,1)S(1)} %get-tuple-element.62), channel_id=1, source_target_pairs={{0,1},{1,0},{2,3},{3,2},{4,5},{5,4},{6,7},{7,6},{8,9},{9,8},{10,11... | collective-permute-start | bytes 1544 | tf_op jit(solution)/shard_map/ppermute | solution.py:363
  12.8 6.0 %collective-permute-start.4 = (bf16[4,7168]{1,0:T(4,128)(2,1)S(1)}, bf16[4,7168]{1,0:T(4,128)(2,1)S(1)}, u32[]{:S(2)}, u32[]{:S(2)}) collective-permute-start(bf16[4,7168]{1,0:T(4,128)(2,1)S(1)} %shard_map.56.refs_0_), channel_id=1, source_target_pairs={{0,4},{1,5},{2,6},{3,7},{4,0},{5,1},{6,2},{7,3},{8,12},{9,13},{10,... | collective-permute-start | bytes 172040 | tf_op jit(solution)/shard_map/ppermute | solution.py:363
  14.7 7.5 %collective-permute-start.3 = (bf16[4,7168]{1,0:T(4,128)(2,1)S(1)}, bf16[4,7168]{1,0:T(4,128)(2,1)S(1)}, u32[]{:S(2)}, u32[]{:S(2)}) collective-permute-start(bf16[4,7168]{1,0:T(4,128)(2,1)S(1)} %shard_map.56.refs_0_), channel_id=1, source_target_pairs={{0,8},{1,9},{2,10},{3,11},{4,12},{5,13},{6,14},{7,15},{8,0},{9,1},... | collective-permute-start | bytes 172040 | tf_op jit(solution)/shard_map/ppermute | solution.py:363
  17.3 4.9 %collective-permute-start.5 = (bf16[4,7168]{1,0:T(4,128)(2,1)S(1)}, bf16[4,7168]{1,0:T(4,128)(2,1)S(1)}, u32[]{:S(2)}, u32[]{:S(2)}) collective-permute-start(bf16[4,7168]{1,0:T(4,128)(2,1)S(1)} %shard_map.56.refs_0_), channel_id=1, source_target_pairs={{0,1},{1,0},{2,3},{3,2},{4,5},{5,4},{6,7},{7,6},{8,9},{9,8},{10,11... | collective-permute-start | bytes 172040 | tf_op jit(solution)/shard_map/ppermute | solution.py:363
  17.3 6.4 %collective-permute-start.8 = (bf16[4,7168]{1,0:T(4,128)(2,1)S(1)}, bf16[4,7168]{1,0:T(4,128)(2,1)S(1)}, u32[]{:S(2)}, u32[]{:S(2)}) collective-permute-start(bf16[4,7168]{1,0:T(4,128)(2,1)S(1)} %shard_map.56.refs_0_), channel_id=1, source_target_pairs={{0,12},{1,13},{2,14},{3,15},{4,8},{5,9},{6,10},{7,11},{8,4},{9,5},... | collective-permute-start | bytes 172040 | tf_op jit(solution)/shard_map/ppermute | solution.py:363
  17.3 6.4 %collective-permute-start.6 = (bf16[4,7168]{1,0:T(4,128)(2,1)S(1)}, bf16[4,7168]{1,0:T(4,128)(2,1)S(1)}, u32[]{:S(2)}, u32[]{:S(2)}) collective-permute-start(bf16[4,7168]{1,0:T(4,128)(2,1)S(1)} %shard_map.56.refs_0_), channel_id=1, source_target_pairs={{0,2},{1,3},{2,0},{3,1},{4,6},{5,7},{6,4},{7,5},{8,10},{9,11},{10,... | collective-permute-start | bytes 172040 | tf_op jit(solution)/shard_map/ppermute | solution.py:363
  18.7 5.0 %collective-permute-start.7 = (bf16[4,7168]{1,0:T(4,128)(2,1)S(1)}, bf16[4,7168]{1,0:T(4,128)(2,1)S(1)}, u32[]{:S(2)}, u32[]{:S(2)}) collective-permute-start(bf16[4,7168]{1,0:T(4,128)(2,1)S(1)} %collective-permute-done.4.refs_1_), channel_id=1, source_target_pairs={{0,2},{1,3},{2,0},{3,1},{4,6},{5,7},{6,4},{7,5},{8,10},{9,11},{10,... | collective-permute-start | bytes 172040 | tf_op jit(solution)/shard_map/ppermute | solution.py:363
  19.4 1.2 %copy-start = (s32[56,4096]{1,0:T(8,128)S(1)}, s32[56,4096]{1,0:T(8,128)}, u32[]{:S(2)}) copy-start(s32[56,4096]{1,0:T(8,128)} %delay_ref) | copy-start | bytes 2752516
  20.5 0.7 %copy-start.1 = (s32[56]{0:T(128)S(1)}, s32[56]{0:T(128)}, u32[]{:S(2)}) copy-start(s32[56]{0:T(128)} %offset_ref.1) | copy-start | bytes 676
  22.2 4.2 %collective-permute-start.12 = (bf16[4,7168]{1,0:T(4,128)(2,1)S(1)}, bf16[4,7168]{1,0:T(4,128)(2,1)S(1)}, u32[]{:S(2)}, u32[]{:S(2)}) collective-permute-start(bf16[4,7168]{1,0:T(4,128)(2,1)S(1)} %collective-permute-done.3.refs_2_), channel_id=1, source_target_pairs={{0,2},{1,3},{2,0},{3,1},{4,6},{5,7},{6,4},{7,5},{8,10},{9,11},{10,... | collective-permute-start | bytes 172040 | tf_op jit(solution)/shard_map/ppermute | solution.py:363
  23.7 3.1 %collective-permute-start.9 = (bf16[4,7168]{1,0:T(4,128)(2,1)S(1)}, bf16[4,7168]{1,0:T(4,128)(2,1)S(1)}, u32[]{:S(2)}, u32[]{:S(2)}) collective-permute-start(bf16[4,7168]{1,0:T(4,128)(2,1)S(1)} %collective-permute-done.4.refs_1_), channel_id=1, source_target_pairs={{0,1},{1,0},{2,3},{3,2},{4,5},{5,4},{6,7},{7,6},{8,9},{9,8},{10,11... | collective-permute-start | bytes 172040 | tf_op jit(solution)/shard_map/ppermute | solution.py:363
  23.8 4.3 %collective-permute-start.13 = (bf16[4,7168]{1,0:T(4,128)(2,1)S(1)}, bf16[4,7168]{1,0:T(4,128)(2,1)S(1)}, u32[]{:S(2)}, u32[]{:S(2)}) collective-permute-start(bf16[4,7168]{1,0:T(4,128)(2,1)S(1)} %collective-permute-done.8.refs_3_), channel_id=1, source_target_pairs={{0,2},{1,3},{2,0},{3,1},{4,6},{5,7},{6,4},{7,5},{8,10},{9,11},{10,... | collective-permute-start | bytes 172040 | tf_op jit(solution)/shard_map/ppermute | solution.py:363
  26.5 1.7 %collective-permute-start.14 = (bf16[4,7168]{1,0:T(4,128)(2,1)S(1)}, bf16[4,7168]{1,0:T(4,128)(2,1)S(1)}, u32[]{:S(2)}, u32[]{:S(2)}) collective-permute-start(bf16[4,7168]{1,0:T(4,128)(2,1)S(1)} %collective-permute-done.12.refs_2_), channel_id=1, source_target_pairs={{0,1},{1,0},{2,3},{3,2},{4,5},{5,4},{6,7},{7,6},{8,9},{9,8},{10,11... | collective-permute-start | bytes 172040 | tf_op jit(solution)/shard_map/ppermute | solution.py:363
  26.8 1.5 %collective-permute-start.11 = (bf16[4,7168]{1,0:T(4,128)(2,1)S(1)}, bf16[4,7168]{1,0:T(4,128)(2,1)S(1)}, u32[]{:S(2)}, u32[]{:S(2)}) collective-permute-start(bf16[4,7168]{1,0:T(4,128)(2,1)S(1)} %collective-permute-done.8.refs_3_), channel_id=1, source_target_pairs={{0,1},{1,0},{2,3},{3,2},{4,5},{5,4},{6,7},{7,6},{8,9},{9,8},{10,11... | collective-permute-start | bytes 172040 | tf_op jit(solution)/shard_map/ppermute | solution.py:363
  27.4 1.9 %collective-permute-start.15 = (bf16[4,7168]{1,0:T(4,128)(2,1)S(1)}, bf16[4,7168]{1,0:T(4,128)(2,1)S(1)}, u32[]{:S(2)}, u32[]{:S(2)}) collective-permute-start(bf16[4,7168]{1,0:T(4,128)(2,1)S(1)} %collective-permute-done.6.refs_0_), channel_id=1, source_target_pairs={{0,1},{1,0},{2,3},{3,2},{4,5},{5,4},{6,7},{7,6},{8,9},{9,8},{10,11... | collective-permute-start | bytes 172040 | tf_op jit(solution)/shard_map/ppermute | solution.py:363
  27.4 1.5 %collective-permute-start.10 = (bf16[4,7168]{1,0:T(4,128)(2,1)S(1)}, bf16[4,7168]{1,0:T(4,128)(2,1)S(1)}, u32[]{:S(2)}, u32[]{:S(2)}) collective-permute-start(bf16[4,7168]{1,0:T(4,128)(2,1)S(1)} %collective-permute-done.3.refs_2_), channel_id=1, source_target_pairs={{0,1},{1,0},{2,3},{3,2},{4,5},{5,4},{6,7},{7,6},{8,9},{9,8},{10,11... | collective-permute-start | bytes 172040 | tf_op jit(solution)/shard_map/ppermute | solution.py:363
  28.1 1.2 %collective-permute-start.16 = (bf16[4,7168]{1,0:T(4,128)(2,1)S(1)}, bf16[4,7168]{1,0:T(4,128)(2,1)S(1)}, u32[]{:S(2)}, u32[]{:S(2)}) collective-permute-start(bf16[4,7168]{1,0:T(4,128)(2,1)S(1)} %collective-permute-done.7.refs_1_), channel_id=1, source_target_pairs={{0,1},{1,0},{2,3},{3,2},{4,5},{5,4},{6,7},{7,6},{8,9},{9,8},{10,11... | collective-permute-start | bytes 172040 | tf_op jit(solution)/shard_map/ppermute | solution.py:363
  28.3 1.3 %collective-permute-start.17 = (bf16[4,7168]{1,0:T(4,128)(2,1)S(1)}, bf16[4,7168]{1,0:T(4,128)(2,1)S(1)}, u32[]{:S(2)}, u32[]{:S(2)}) collective-permute-start(bf16[4,7168]{1,0:T(4,128)(2,1)S(1)} %collective-permute-done.13.refs_3_), channel_id=1, source_target_pairs={{0,1},{1,0},{2,3},{3,2},{4,5},{5,4},{6,7},{7,6},{8,9},{9,8},{10,11... | collective-permute-start | bytes 172040 | tf_op jit(solution)/shard_map/ppermute | solution.py:363
  31.7 6.2 %collective-permute-start.20 = (bf16[32,1792]{1,0:T(8,128)(2,1)S(1)}, bf16[32,1792]{1,0:T(8,128)(2,1)S(1)}, u32[]{:S(2)}, u32[]{:S(2)}) collective-permute-start(bf16[32,1792]{1,0:T(8,128)(2,1)S(1)} %get-tuple-element.60), channel_id=1, source_target_pairs={{0,16},{16,0},{1,17},{17,1},{2,18},{18,2},{3,19},{19,3},{4,20},{20... | collective-permute-start | bytes 344072 | tf_op jit(solution)/shard_map/ppermute | solution.py:363
  34.6 4.9 %collective-permute-start.19 = (bf16[32,1280]{1,0:T(8,128)(2,1)S(1)}, bf16[32,1280]{1,0:T(8,128)(2,1)S(1)}, u32[]{:S(2)}, u32[]{:S(2)}) collective-permute-start(bf16[32,1280]{1,0:T(8,128)(2,1)S(1)} %get-tuple-element.58), channel_id=1, source_target_pairs={{0,16},{16,0},{1,17},{17,1},{2,18},{18,2},{3,19},{19,3},{4,20},{20... | collective-permute-start | bytes 245768 | tf_op jit(solution)/shard_map/ppermute | solution.py:363
  36.4 4.3 %collective-permute-start.18 = (bf16[32,1024]{1,0:T(8,128)(2,1)S(1)}, bf16[32,1024]{1,0:T(8,128)(2,1)S(1)}, u32[]{:S(2)}, u32[]{:S(2)}) collective-permute-start(bf16[32,1024]{1,0:T(8,128)(2,1)S(1)} %get-tuple-element.56), channel_id=1, source_target_pairs={{0,16},{16,0},{1,17},{17,1},{2,18},{18,2},{3,19},{19,3},{4,20},{20... | collective-permute-start | bytes 196616 | tf_op jit(solution)/shard_map/ppermute | solution.py:363

commit v7 on v6

--- a/solution.py
+++ b/solution.py
@@ -395,12 +395,13 @@
     for d in (2, 4, 6):
         blocks[d | 1] = flip(blocks[d], "vox", 1)
     early = split([blocks[d] for d in ORDER[0]])
-    gate = lax.optimization_barrier((blocks[8], blocks[12], early, blocks[5]))
+    gate = lax.optimization_barrier((blocks[8], blocks[12], early))
     blocks[8], blocks[12], early = gate[:3]
     for d in (8, 12):
         blocks[d | 1] = flip(blocks[d], "vox", 1)
+    blocks[10] = after(blocks[10], blocks[5], blocks[3])
     blocks[11] = flip(blocks[10], "vox", 1)
-    blocks[14] = after(blocks[14], blocks[11], blocks[13])
+    blocks[14] = after(blocks[14], blocks[13])
     blocks[15] = flip(blocks[14], "vox", 1)
     middle = split([blocks[d] for d in ORDER[1]])
     return [early, middle] + [split([blocks[d] for d in order]) for order in ORDER[2:]], target

time: 41.6 us -> 41.4 us (level)
  transfers between devices with their start and end apart: 21 -> 21, of which waited for: 8 -> 7; matrix products, arithmetic and copies ran while one was open for 3% -> 3% of each run, Pallas kernels for 18% -> 19%
where the time goes in v7:
time: 41.4 us; the launch traced here: 41.1 us
  starting transfers between devices  21.2 us (51%)
  Pallas kernels  11.1 us (27%)
  waiting for transfers between devices  4.09 us (10%)
  local copies, waits for them, and re-layouts  2.57 us (6%)
  other arithmetic  1.33 us (3%)
  between operations  0.86 us (2%)
    ppermute x20, starting transfers between devices, flip(): return lax.ppermute(block, axis, [(i, i ^ mask) for i in range(count)])  20.5 us
    pallas_call x3, Pallas kernels, image(): pl.pallas_call(functools.partial(image_kernel, swap, len(pieces), start),...  4.38 us
    ppermute x20, waiting for transfers between devices, flip(): return lax.ppermute(block, axis, [(i, i ^ mask) for i in range(count)])  4.09 us
    pallas_call x3, Pallas kernels, add_part(): pl.pallas_call(functools.partial(add_kernel, start), out_shape=jax.ShapeD...  2.08 us
    unnamed x4, local copies, waits for them, and re-layouts  1.83 us
    pallas_call x1, Pallas kernels, correlate(): pl.pallas_call(corr_kernel, out_shape=jax.ShapeDtypeStruct((pitch * slice...  1.78 us
    transpose x1, other arithmetic, shards(): windowed = jnp.transpose(windowed, (1, 0, 2))  1.29 us
    pallas_call x4, Pallas kernels, split(): pl.pallas_call(split_kernel, out_shape=[jax.ShapeDtypeStruct((rows, colum...  1.25 us
  transfers between devices with their start and end apart: 21, of which 7 were waited for; matrix products, arithmetic and copies ran while one was open for 3% of the time, Pallas kernels for 19%

profile of v7, /device:TPU:0, one launch (start us, length us, event | category | flops | bytes accessed | tf_op | source)
XLA Modules:
  0.0 41.1 jit_solution(634650929270067924)
XLA Ops:
  0.7 0.7 %dynamic-slice_bitcast_fusion = bf16[2,4096]{1,0:T(2,128)(2,1)S(1)} fusion(bf16[28,2,4096]{2,1,0:T(2,128)(2,1)} %param.5, s32[]{:T(128)S(6)} %select_n.50), kind=kLoop, calls=%fused_computation.3 | loop fusion | bytes 32772 | tf_op jit(solution)/shard_map/jit(dynamic_index_in_dim)/squeeze | solution.py:421
  1.4 3.0 %collective-permute-start = (bf16[2,4096]{1,0:T(2,128)(2,1)S(1)}, bf16[2,4096]{1,0:T(2,128)(2,1)S(1)}, u32[]{:S(2)}, u32[]{:S(2)}) collective-permute-start(bf16[2,4096]{1,0:T(2,128)(2,1)S(1)} %dynamic-slice_bitcast_fusion), channel_id=1, source_target_pairs={{0,16},{16,0},{1,17},{17,1},{2,18},{18,2},{3,19},{19,3},{4,20},{20... | collective-permute-start | bytes 49160 | tf_op jit(solution)/shard_map/ppermute | solution.py:363
  4.4 1.3 %fusion.win_ref = bf16[2,28,4096]{2,1,0:T(8,128)(2,1)S(1)} fusion(bf16[28,2,4096]{2,1,0:T(2,128)(2,1)} %param.5, f32[4096]{0:T(1024)} %constant.48.clone), kind=kLoop, calls=%fused_computation.1 | loop fusion | flops 688128 | bytes 933888 | tf_op jit(solution)/shard_map/transpose | solution.py:438
  5.7 0.4 collective-permute-done
  6.2 0.7 %collective-permute-start.2 = (bf16[2,128]{1,0:T(2,128)(2,1)S(1)}, bf16[2,128]{1,0:T(2,128)(2,1)S(1)}, u32[]{:S(2)}, u32[]{:S(2)}) collective-permute-start(bf16[2,128]{1,0:T(2,128)(2,1)S(1)} %get-tuple-element.63), channel_id=1, source_target_pairs={{1,2},{3,4},{5,6},{7,8},{9,10},{11,12},{13,14},{2,1},{4,3},{6,5},{... | collective-permute-start | bytes 1544 | tf_op jit(solution)/shard_map/ppermute | solution.py:372
  6.8 3.5 %collective-permute-start.1 = (bf16[2,128]{1,0:T(2,128)(2,1)S(1)}, bf16[2,128]{1,0:T(2,128)(2,1)S(1)}, u32[]{:S(2)}, u32[]{:S(2)}) collective-permute-start(bf16[2,128]{1,0:T(2,128)(2,1)S(1)} %get-tuple-element.64), channel_id=1, source_target_pairs={{0,1},{1,0},{2,3},{3,2},{4,5},{5,4},{6,7},{7,6},{8,9},{9,8},{10,11... | collective-permute-start | bytes 1544 | tf_op jit(solution)/shard_map/ppermute | solution.py:363
  10.3 1.8 %shard_map.55.part_ref = f32[128,256]{1,0:T(8,128)S(1)} custom-call(bf16[2,28,4096]{2,1,0:T(8,128)(2,1)S(1)} %fusion.win_ref, bf16[2,4096]{1,0:T(2,128)(2,1)S(1)} %broadcast_select_fusion.ref_ref.body_ref), custom_call_target="tpu_custom_call" | custom-call | flops 117440512 | bytes 458752 | tf_op jit(solution)/shard_map/pallas_call | solution.py:150
  12.1 0.6 %shard_map.56.refs_0_ = bf16[4,7168]{1,0:T(4,128)(2,1)S(1)} custom-call(s32[1]{0:T(128)S(6)} %copy.12.ref_ref, bf16[2,28,4096]{2,1,0:T(8,128)(2,1)S(1)} %fusion.win_ref, bf16[2,4096]{1,0:T(2,128)(2,1)S(1)} %broadcast_select_fusion.ref_ref.body_ref, bf16[2,128]{1,0:T(2,128)(2,1)S(1)} %get-tuple-element.66.low_ref, ...), custom_call_target="tpu_custom_call" | custom-call | flops 14680064 | bytes 28672 | tf_op jit(solution)/shard_map/pallas_call | solution.py:166
  12.8 2.0 %collective-permute-start.4 = (bf16[4,7168]{1,0:T(4,128)(2,1)S(1)}, bf16[4,7168]{1,0:T(4,128)(2,1)S(1)}, u32[]{:S(2)}, u32[]{:S(2)}) collective-permute-start(bf16[4,7168]{1,0:T(4,128)(2,1)S(1)} %shard_map.56.refs_0_), channel_id=1, source_target_pairs={{0,4},{1,5},{2,6},{3,7},{4,0},{5,1},{6,2},{7,3},{8,12},{9,13},{10,... | collective-permute-start | bytes 172040 | tf_op jit(solution)/shard_map/ppermute | solution.py:363
  14.7 2.6 %collective-permute-start.3 = (bf16[4,7168]{1,0:T(4,128)(2,1)S(1)}, bf16[4,7168]{1,0:T(4,128)(2,1)S(1)}, u32[]{:S(2)}, u32[]{:S(2)}) collective-permute-start(bf16[4,7168]{1,0:T(4,128)(2,1)S(1)} %shard_map.56.refs_0_), channel_id=1, source_target_pairs={{0,8},{1,9},{2,10},{3,11},{4,12},{5,13},{6,14},{7,15},{8,0},{9,1},... | collective-permute-start | bytes 172040 | tf_op jit(solution)/shard_map/ppermute | solution.py:363
  17.3 1.4 %collective-permute-start.6 = (bf16[4,7168]{1,0:T(4,128)(2,1)S(1)}, bf16[4,7168]{1,0:T(4,128)(2,1)S(1)}, u32[]{:S(2)}, u32[]{:S(2)}) collective-permute-start(bf16[4,7168]{1,0:T(4,128)(2,1)S(1)} %shard_map.56.refs_0_), channel_id=1, source_target_pairs={{0,2},{1,3},{2,0},{3,1},{4,6},{5,7},{6,4},{7,5},{8,10},{9,11},{10,... | collective-permute-start | bytes 172040 | tf_op jit(solution)/shard_map/ppermute | solution.py:363
  18.7 0.6 %collective-permute-start.7 = (bf16[4,7168]{1,0:T(4,128)(2,1)S(1)}, bf16[4,7168]{1,0:T(4,128)(2,1)S(1)}, u32[]{:S(2)}, u32[]{:S(2)}) collective-permute-start(bf16[4,7168]{1,0:T(4,128)(2,1)S(1)} %collective-permute-done.4.refs_1_), channel_id=1, source_target_pairs={{0,2},{1,3},{2,0},{3,1},{4,6},{5,7},{6,4},{7,5},{8,10},{9,11},{10,... | collective-permute-start | bytes 172040 | tf_op jit(solution)/shard_map/ppermute | solution.py:363
  19.4 1.2 %copy-done = s32[56,4096]{1,0:T(8,128)S(1)} copy-done((s32[56,4096]{1,0:T(8,128)S(1)}, s32[56,4096]{1,0:T(8,128)}, u32[]{:S(2)}) %copy-start) | copy-done | bytes 917528
  20.5 0.7 %copy-done.1 = s32[56]{0:T(128)S(1)} copy-done((s32[56]{0:T(128)S(1)}, s32[56]{0:T(128)}, u32[]{:S(2)}) %copy-start.1) | copy-done | bytes 248
  21.2 1.0 %shard_map.57.target_ref = s8[28,32,4096]{2,1,0:T(32,128)(4,1)S(1)} custom-call(s32[56]{0:T(128)S(1)} %copy-done.1, s32[56,4096]{1,0:T(8,128)S(1)} %copy-done), custom_call_target="tpu_custom_call" | custom-call | flops 3670016 | bytes 4128768 | tf_op jit(solution)/shard_map/pallas_call | solution.py:240
  22.2 1.5 %collective-permute-start.12 = (bf16[4,7168]{1,0:T(4,128)(2,1)S(1)}, bf16[4,7168]{1,0:T(4,128)(2,1)S(1)}, u32[]{:S(2)}, u32[]{:S(2)}) collective-permute-start(bf16[4,7168]{1,0:T(4,128)(2,1)S(1)} %collective-permute-done.3.refs_2_), channel_id=1, source_target_pairs={{0,2},{1,3},{2,0},{3,1},{4,6},{5,7},{6,4},{7,5},{8,10},{9,11},{10,... | collective-permute-start | bytes 172040 | tf_op jit(solution)/shard_map/ppermute | solution.py:363
  23.7 0.6 %collective-permute-start.14 = (bf16[4,7168]{1,0:T(4,128)(2,1)S(1)}, bf16[4,7168]{1,0:T(4,128)(2,1)S(1)}, u32[]{:S(2)}, u32[]{:S(2)}) collective-permute-start(bf16[4,7168]{1,0:T(4,128)(2,1)S(1)} %collective-permute-done.8.refs_3_), channel_id=1, source_target_pairs={{0,2},{1,3},{2,0},{3,1},{4,6},{5,7},{6,4},{7,5},{8,10},{9,11},{10,... | collective-permute-start | bytes 172040 | tf_op jit(solution)/shard_map/ppermute | solution.py:363
  24.3 0.5 %collective-permute-start.13 = (bf16[4,7168]{1,0:T(4,128)(2,1)S(1)}, bf16[4,7168]{1,0:T(4,128)(2,1)S(1)}, u32[]{:S(2)}, u32[]{:S(2)}) collective-permute-start(bf16[4,7168]{1,0:T(4,128)(2,1)S(1)} %collective-permute-done.6.refs_0_), channel_id=1, source_target_pairs={{0,1},{1,0},{2,3},{3,2},{4,5},{5,4},{6,7},{7,6},{8,9},{9,8},{10,11... | collective-permute-start | bytes 172040 | tf_op jit(solution)/shard_map/ppermute | solution.py:363
  25.3 1.7 %collective-permute-done.12.refs_2_ = bf16[4,7168]{1,0:T(4,128)(2,1)S(1)} collective-permute-done((bf16[4,7168]{1,0:T(4,128)(2,1)S(1)}, bf16[4,7168]{1,0:T(4,128)(2,1)S(1)}, u32[]{:S(2)}, u32[]{:S(2)}) %collective-permute-start.12) | collective-permute-done | bytes 57376 | tf_op jit(solution)/shard_map/ppermute | solution.py:363
  27.0 0.5 %collective-permute-start.15 = (bf16[4,7168]{1,0:T(4,128)(2,1)S(1)}, bf16[4,7168]{1,0:T(4,128)(2,1)S(1)}, u32[]{:S(2)}, u32[]{:S(2)}) collective-permute-start(bf16[4,7168]{1,0:T(4,128)(2,1)S(1)} %collective-permute-done.7.refs_1_), channel_id=1, source_target_pairs={{0,1},{1,0},{2,3},{3,2},{4,5},{5,4},{6,7},{7,6},{8,9},{9,8},{10,11... | collective-permute-start | bytes 172040 | tf_op jit(solution)/shard_map/ppermute | solution.py:363
  27.9 0.5 %collective-permute-start.17 = (bf16[4,7168]{1,0:T(4,128)(2,1)S(1)}, bf16[4,7168]{1,0:T(4,128)(2,1)S(1)}, u32[]{:S(2)}, u32[]{:S(2)}) collective-permute-start(bf16[4,7168]{1,0:T(4,128)(2,1)S(1)} %collective-permute-done.14.refs_3_), channel_id=1, source_target_pairs={{0,1},{1,0},{2,3},{3,2},{4,5},{5,4},{6,7},{7,6},{8,9},{9,8},{10,11... | collective-permute-start | bytes 172040 | tf_op jit(solution)/shard_map/ppermute | solution.py:363
  29.6 1.9 %shard_map.64 = (f32[32,1792]{1,0:T(8,128)S(1)}, bf16[32,1792]{1,0:T(8,128)(2,1)S(1)}) custom-call(s8[28,32,4096]{2,1,0:T(32,128)(4,1)S(1)} %shard_map.57.target_ref, f8e4m3fn[32,7168]{1,0:T(32,128)(4,1)S(1)} %get-tuple-element.43.refs_0_, f8e4m3fn[32,7168]{1,0:T(32,128)(4,1)S(1)} %get-tuple-element.46.refs_1_, ...), custom_call_target="tpu_custom_call" | custom-call | flops 458752 | bytes 64 | tf_op jit(solution)/shard_map/pallas_call | solution.py:319
  31.5 1.6 %collective-permute-start.20 = (bf16[32,1792]{1,0:T(8,128)(2,1)S(1)}, bf16[32,1792]{1,0:T(8,128)(2,1)S(1)}, u32[]{:S(2)}, u32[]{:S(2)}) collective-permute-start(bf16[32,1792]{1,0:T(8,128)(2,1)S(1)} %get-tuple-element.62), channel_id=1, source_target_pairs={{0,16},{16,0},{1,17},{17,1},{2,18},{18,2},{3,19},{19,3},{4,20},{20... | collective-permute-start | bytes 344072 | tf_op jit(solution)/shard_map/ppermute | solution.py:363
  33.0 1.4 %shard_map.63 = (f32[32,1280]{1,0:T(8,128)S(1)}, bf16[32,1280]{1,0:T(8,128)(2,1)S(1)}) custom-call(s8[28,32,4096]{2,1,0:T(32,128)(4,1)S(1)} %shard_map.57.target_ref, f8e4m3fn[32,7168]{1,0:T(32,128)(4,1)S(1)} %get-tuple-element.43.refs_0_, f8e4m3fn[32,7168]{1,0:T(32,128)(4,1)S(1)} %get-tuple-element.46.refs_1_, ...), custom_call_target="tpu_custom_call" | custom-call | flops 327680 | bytes 64 | tf_op jit(solution)/shard_map/pallas_call | solution.py:319
  34.4 0.6 %collective-permute-start.19 = (bf16[32,1280]{1,0:T(8,128)(2,1)S(1)}, bf16[32,1280]{1,0:T(8,128)(2,1)S(1)}, u32[]{:S(2)}, u32[]{:S(2)}) collective-permute-start(bf16[32,1280]{1,0:T(8,128)(2,1)S(1)} %get-tuple-element.60), channel_id=1, source_target_pairs={{0,16},{16,0},{1,17},{17,1},{2,18},{18,2},{3,19},{19,3},{4,20},{20... | collective-permute-start | bytes 245768 | tf_op jit(solution)/shard_map/ppermute | solution.py:363
  35.0 1.1 %shard_map.62 = (f32[32,1024]{1,0:T(8,128)S(1)}, bf16[32,1024]{1,0:T(8,128)(2,1)S(1)}) custom-call(s8[28,32,4096]{2,1,0:T(32,128)(4,1)S(1)} %shard_map.57.target_ref, f8e4m3fn[32,7168]{1,0:T(32,128)(4,1)S(1)} %get-tuple-element.43.refs_0_, f8e4m3fn[32,7168]{1,0:T(32,128)(4,1)S(1)} %get-tuple-element.46.refs_1_, ...), custom_call_target="tpu_custom_call" | custom-call | flops 262144 | bytes 64 | tf_op jit(solution)/shard_map/pallas_call | solution.py:319
  36.1 1.6 %collective-permute-start.18 = (bf16[32,1024]{1,0:T(8,128)(2,1)S(1)}, bf16[32,1024]{1,0:T(8,128)(2,1)S(1)}, u32[]{:S(2)}, u32[]{:S(2)}) collective-permute-start(bf16[32,1024]{1,0:T(8,128)(2,1)S(1)} %get-tuple-element.58), channel_id=1, source_target_pairs={{0,16},{16,0},{1,17},{17,1},{2,18},{18,2},{3,19},{19,3},{4,20},{20... | collective-permute-start | bytes 196616 | tf_op jit(solution)/shard_map/ppermute | solution.py:363
  37.7 0.7 %shard_map.65.refs_0_ = f32[32,4096]{1,0:T(8,128)} custom-call(f32[32,1792]{1,0:T(8,128)S(1)} %get-tuple-element.61.kept_ref, bf16[32,1792]{1,0:T(8,128)(2,1)S(1)} %collective-permute-done.20.came_ref), custom_call_target="tpu_custom_call" | custom-call | flops 57344 | bytes 229376 | tf_op jit(solution)/shard_map/pallas_call | solution.py:347
  38.4 0.9 %collective-permute-done.19.came_ref = bf16[32,1280]{1,0:T(8,128)(2,1)S(1)} collective-permute-done((bf16[32,1280]{1,0:T(8,128)(2,1)S(1)}, bf16[32,1280]{1,0:T(8,128)(2,1)S(1)}, u32[]{:S(2)}, u32[]{:S(2)}) %collective-permute-start.19) | collective-permute-done | bytes 81952 | tf_op jit(solution)/shard_map/ppermute | solution.py:363
  39.3 0.7 %shard_map.66.refs_0_ = f32[32,4096]{1,0:T(8,128)} custom-call(f32[32,1280]{1,0:T(8,128)S(1)} %get-tuple-element.59.kept_ref, bf16[32,1280]{1,0:T(8,128)(2,1)S(1)} %collective-permute-done.19.came_ref, f32[32,4096]{1,0:T(8,128)} %shard_map.65.refs_0_), custom_call_target="tpu_custom_call", output_to_operand_aliasing={{}: (2, {})} | custom-call | flops 40960 | bytes 163840 | tf_op jit(solution)/shard_map/pallas_call | solution.py:347
  40.0 0.5 %collective-permute-done.18.came_ref = bf16[32,1024]{1,0:T(8,128)(2,1)S(1)} collective-permute-done((bf16[32,1024]{1,0:T(8,128)(2,1)S(1)}, bf16[32,1024]{1,0:T(8,128)(2,1)S(1)}, u32[]{:S(2)}, u32[]{:S(2)}) %collective-permute-start.18) | collective-permute-done | bytes 65568 | tf_op jit(solution)/shard_map/ppermute | solution.py:363
  40.5 0.7 %shard_map.67 = f32[32,4096]{1,0:T(8,128)} custom-call(f32[32,1024]{1,0:T(8,128)S(1)} %get-tuple-element.57.kept_ref, bf16[32,1024]{1,0:T(8,128)(2,1)S(1)} %collective-permute-done.18.came_ref, f32[32,4096]{1,0:T(8,128)} %shard_map.66.refs_0_), custom_call_target="tpu_custom_call", output_to_operand_aliasing={{}: (2, {})} | custom-call | flops 32768 | bytes 131072 | tf_op jit(solution)/shard_map/pallas_call | solution.py:347
  (32 shorter events, 2.1 us)
Async XLA Ops:
  1.4 4.7 %collective-permute-start = (bf16[2,4096]{1,0:T(2,128)(2,1)S(1)}, bf16[2,4096]{1,0:T(2,128)(2,1)S(1)}, u32[]{:S(2)}, u32[]{:S(2)}) collective-permute-start(bf16[2,4096]{1,0:T(2,128)(2,1)S(1)} %dynamic-slice_bitcast_fusion), channel_id=1, source_target_pairs={{0,16},{16,0},{1,17},{17,1},{2,18},{18,2},{3,19},{19,3},{4,20},{20... | collective-permute-start | bytes 49160 | tf_op jit(solution)/shard_map/ppermute | solution.py:363
  6.2 5.9 %collective-permute-start.2 = (bf16[2,128]{1,0:T(2,128)(2,1)S(1)}, bf16[2,128]{1,0:T(2,128)(2,1)S(1)}, u32[]{:S(2)}, u32[]{:S(2)}) collective-permute-start(bf16[2,128]{1,0:T(2,128)(2,1)S(1)} %get-tuple-element.63), channel_id=1, source_target_pairs={{1,2},{3,4},{5,6},{7,8},{9,10},{11,12},{13,14},{2,1},{4,3},{6,5},{... | collective-permute-start | bytes 1544 | tf_op jit(solution)/shard_map/ppermute | solution.py:372
  6.8 5.3 %collective-permute-start.1 = (bf16[2,128]{1,0:T(2,128)(2,1)S(1)}, bf16[2,128]{1,0:T(2,128)(2,1)S(1)}, u32[]{:S(2)}, u32[]{:S(2)}) collective-permute-start(bf16[2,128]{1,0:T(2,128)(2,1)S(1)} %get-tuple-element.64), channel_id=1, source_target_pairs={{0,1},{1,0},{2,3},{3,2},{4,5},{5,4},{6,7},{7,6},{8,9},{9,8},{10,11... | collective-permute-start | bytes 1544 | tf_op jit(solution)/shard_map/ppermute | solution.py:363
  12.8 6.0 %collective-permute-start.4 = (bf16[4,7168]{1,0:T(4,128)(2,1)S(1)}, bf16[4,7168]{1,0:T(4,128)(2,1)S(1)}, u32[]{:S(2)}, u32[]{:S(2)}) collective-permute-start(bf16[4,7168]{1,0:T(4,128)(2,1)S(1)} %shard_map.56.refs_0_), channel_id=1, source_target_pairs={{0,4},{1,5},{2,6},{3,7},{4,0},{5,1},{6,2},{7,3},{8,12},{9,13},{10,... | collective-permute-start | bytes 172040 | tf_op jit(solution)/shard_map/ppermute | solution.py:363
  14.7 7.5 %collective-permute-start.3 = (bf16[4,7168]{1,0:T(4,128)(2,1)S(1)}, bf16[4,7168]{1,0:T(4,128)(2,1)S(1)}, u32[]{:S(2)}, u32[]{:S(2)}) collective-permute-start(bf16[4,7168]{1,0:T(4,128)(2,1)S(1)} %shard_map.56.refs_0_), channel_id=1, source_target_pairs={{0,8},{1,9},{2,10},{3,11},{4,12},{5,13},{6,14},{7,15},{8,0},{9,1},... | collective-permute-start | bytes 172040 | tf_op jit(solution)/shard_map/ppermute | solution.py:363
  17.3 4.9 %collective-permute-start.5 = (bf16[4,7168]{1,0:T(4,128)(2,1)S(1)}, bf16[4,7168]{1,0:T(4,128)(2,1)S(1)}, u32[]{:S(2)}, u32[]{:S(2)}) collective-permute-start(bf16[4,7168]{1,0:T(4,128)(2,1)S(1)} %shard_map.56.refs_0_), channel_id=1, source_target_pairs={{0,1},{1,0},{2,3},{3,2},{4,5},{5,4},{6,7},{7,6},{8,9},{9,8},{10,11... | collective-permute-start | bytes 172040 | tf_op jit(solution)/shard_map/ppermute | solution.py:363
  17.3 6.4 %collective-permute-start.8 = (bf16[4,7168]{1,0:T(4,128)(2,1)S(1)}, bf16[4,7168]{1,0:T(4,128)(2,1)S(1)}, u32[]{:S(2)}, u32[]{:S(2)}) collective-permute-start(bf16[4,7168]{1,0:T(4,128)(2,1)S(1)} %shard_map.56.refs_0_), channel_id=1, source_target_pairs={{0,12},{1,13},{2,14},{3,15},{4,8},{5,9},{6,10},{7,11},{8,4},{9,5},... | collective-permute-start | bytes 172040 | tf_op jit(solution)/shard_map/ppermute | solution.py:363
  17.3 7.0 %collective-permute-start.6 = (bf16[4,7168]{1,0:T(4,128)(2,1)S(1)}, bf16[4,7168]{1,0:T(4,128)(2,1)S(1)}, u32[]{:S(2)}, u32[]{:S(2)}) collective-permute-start(bf16[4,7168]{1,0:T(4,128)(2,1)S(1)} %shard_map.56.refs_0_), channel_id=1, source_target_pairs={{0,2},{1,3},{2,0},{3,1},{4,6},{5,7},{6,4},{7,5},{8,10},{9,11},{10,... | collective-permute-start | bytes 172040 | tf_op jit(solution)/shard_map/ppermute | solution.py:363
  18.7 5.6 %collective-permute-start.7 = (bf16[4,7168]{1,0:T(4,128)(2,1)S(1)}, bf16[4,7168]{1,0:T(4,128)(2,1)S(1)}, u32[]{:S(2)}, u32[]{:S(2)}) collective-permute-start(bf16[4,7168]{1,0:T(4,128)(2,1)S(1)} %collective-permute-done.4.refs_1_), channel_id=1, source_target_pairs={{0,2},{1,3},{2,0},{3,1},{4,6},{5,7},{6,4},{7,5},{8,10},{9,11},{10,... | collective-permute-start | bytes 172040 | tf_op jit(solution)/shard_map/ppermute | solution.py:363
  19.4 1.2 %copy-start = (s32[56,4096]{1,0:T(8,128)S(1)}, s32[56,4096]{1,0:T(8,128)}, u32[]{:S(2)}) copy-start(s32[56,4096]{1,0:T(8,128)} %delay_ref) | copy-start | bytes 2752516
  20.5 0.7 %copy-start.1 = (s32[56]{0:T(128)S(1)}, s32[56]{0:T(128)}, u32[]{:S(2)}) copy-start(s32[56]{0:T(128)} %offset_ref.1) | copy-start | bytes 676
  22.2 4.8 %collective-permute-start.12 = (bf16[4,7168]{1,0:T(4,128)(2,1)S(1)}, bf16[4,7168]{1,0:T(4,128)(2,1)S(1)}, u32[]{:S(2)}, u32[]{:S(2)}) collective-permute-start(bf16[4,7168]{1,0:T(4,128)(2,1)S(1)} %collective-permute-done.3.refs_2_), channel_id=1, source_target_pairs={{0,2},{1,3},{2,0},{3,1},{4,6},{5,7},{6,4},{7,5},{8,10},{9,11},{10,... | collective-permute-start | bytes 172040 | tf_op jit(solution)/shard_map/ppermute | solution.py:363
  23.7 4.2 %collective-permute-start.14 = (bf16[4,7168]{1,0:T(4,128)(2,1)S(1)}, bf16[4,7168]{1,0:T(4,128)(2,1)S(1)}, u32[]{:S(2)}, u32[]{:S(2)}) collective-permute-start(bf16[4,7168]{1,0:T(4,128)(2,1)S(1)} %collective-permute-done.8.refs_3_), channel_id=1, source_target_pairs={{0,2},{1,3},{2,0},{3,1},{4,6},{5,7},{6,4},{7,5},{8,10},{9,11},{10,... | collective-permute-start | bytes 172040 | tf_op jit(solution)/shard_map/ppermute | solution.py:363
  24.3 2.7 %collective-permute-start.9 = (bf16[4,7168]{1,0:T(4,128)(2,1)S(1)}, bf16[4,7168]{1,0:T(4,128)(2,1)S(1)}, u32[]{:S(2)}, u32[]{:S(2)}) collective-permute-start(bf16[4,7168]{1,0:T(4,128)(2,1)S(1)} %collective-permute-done.4.refs_1_), channel_id=1, source_target_pairs={{0,1},{1,0},{2,3},{3,2},{4,5},{5,4},{6,7},{7,6},{8,9},{9,8},{10,11... | collective-permute-start | bytes 172040 | tf_op jit(solution)/shard_map/ppermute | solution.py:363
  24.3 3.2 %collective-permute-start.13 = (bf16[4,7168]{1,0:T(4,128)(2,1)S(1)}, bf16[4,7168]{1,0:T(4,128)(2,1)S(1)}, u32[]{:S(2)}, u32[]{:S(2)}) collective-permute-start(bf16[4,7168]{1,0:T(4,128)(2,1)S(1)} %collective-permute-done.6.refs_0_), channel_id=1, source_target_pairs={{0,1},{1,0},{2,3},{3,2},{4,5},{5,4},{6,7},{7,6},{8,9},{9,8},{10,11... | collective-permute-start | bytes 172040 | tf_op jit(solution)/shard_map/ppermute | solution.py:363
  25.1 2.7 %collective-permute-start.11 = (bf16[4,7168]{1,0:T(4,128)(2,1)S(1)}, bf16[4,7168]{1,0:T(4,128)(2,1)S(1)}, u32[]{:S(2)}, u32[]{:S(2)}) collective-permute-start(bf16[4,7168]{1,0:T(4,128)(2,1)S(1)} %collective-permute-done.8.refs_3_), channel_id=1, source_target_pairs={{0,1},{1,0},{2,3},{3,2},{4,5},{5,4},{6,7},{7,6},{8,9},{9,8},{10,11... | collective-permute-start | bytes 172040 | tf_op jit(solution)/shard_map/ppermute | solution.py:363
  27.0 1.7 %collective-permute-start.10 = (bf16[4,7168]{1,0:T(4,128)(2,1)S(1)}, bf16[4,7168]{1,0:T(4,128)(2,1)S(1)}, u32[]{:S(2)}, u32[]{:S(2)}) collective-permute-start(bf16[4,7168]{1,0:T(4,128)(2,1)S(1)} %collective-permute-done.3.refs_2_), channel_id=1, source_target_pairs={{0,1},{1,0},{2,3},{3,2},{4,5},{5,4},{6,7},{7,6},{8,9},{9,8},{10,11... | collective-permute-start | bytes 172040 | tf_op jit(solution)/shard_map/ppermute | solution.py:363
  27.0 2.0 %collective-permute-start.15 = (bf16[4,7168]{1,0:T(4,128)(2,1)S(1)}, bf16[4,7168]{1,0:T(4,128)(2,1)S(1)}, u32[]{:S(2)}, u32[]{:S(2)}) collective-permute-start(bf16[4,7168]{1,0:T(4,128)(2,1)S(1)} %collective-permute-done.7.refs_1_), channel_id=1, source_target_pairs={{0,1},{1,0},{2,3},{3,2},{4,5},{5,4},{6,7},{7,6},{8,9},{9,8},{10,11... | collective-permute-start | bytes 172040 | tf_op jit(solution)/shard_map/ppermute | solution.py:363
  27.9 1.2 %collective-permute-start.16 = (bf16[4,7168]{1,0:T(4,128)(2,1)S(1)}, bf16[4,7168]{1,0:T(4,128)(2,1)S(1)}, u32[]{:S(2)}, u32[]{:S(2)}) collective-permute-start(bf16[4,7168]{1,0:T(4,128)(2,1)S(1)} %collective-permute-done.12.refs_2_), channel_id=1, source_target_pairs={{0,1},{1,0},{2,3},{3,2},{4,5},{5,4},{6,7},{7,6},{8,9},{9,8},{10,11... | collective-permute-start | bytes 172040 | tf_op jit(solution)/shard_map/ppermute | solution.py:363
  27.9 1.4 %collective-permute-start.17 = (bf16[4,7168]{1,0:T(4,128)(2,1)S(1)}, bf16[4,7168]{1,0:T(4,128)(2,1)S(1)}, u32[]{:S(2)}, u32[]{:S(2)}) collective-permute-start(bf16[4,7168]{1,0:T(4,128)(2,1)S(1)} %collective-permute-done.14.refs_3_), channel_id=1, source_target_pairs={{0,1},{1,0},{2,3},{3,2},{4,5},{5,4},{6,7},{7,6},{8,9},{9,8},{10,11... | collective-permute-start | bytes 172040 | tf_op jit(solution)/shard_map/ppermute | solution.py:363
  31.5 6.2 %collective-permute-start.20 = (bf16[32,1792]{1,0:T(8,128)(2,1)S(1)}, bf16[32,1792]{1,0:T(8,128)(2,1)S(1)}, u32[]{:S(2)}, u32[]{:S(2)}) collective-permute-start(bf16[32,1792]{1,0:T(8,128)(2,1)S(1)} %get-tuple-element.62), channel_id=1, source_target_pairs={{0,16},{16,0},{1,17},{17,1},{2,18},{18,2},{3,19},{19,3},{4,20},{20... | collective-permute-start | bytes 344072 | tf_op jit(solution)/shard_map/ppermute | solution.py:363
  34.4 4.9 %collective-permute-start.19 = (bf16[32,1280]{1,0:T(8,128)(2,1)S(1)}, bf16[32,1280]{1,0:T(8,128)(2,1)S(1)}, u32[]{:S(2)}, u32[]{:S(2)}) collective-permute-start(bf16[32,1280]{1,0:T(8,128)(2,1)S(1)} %get-tuple-element.60), channel_id=1, source_target_pairs={{0,16},{16,0},{1,17},{17,1},{2,18},{18,2},{3,19},{19,3},{4,20},{20... | collective-permute-start | bytes 245768 | tf_op jit(solution)/shard_map/ppermute | solution.py:363
  36.1 4.3 %collective-permute-start.18 = (bf16[32,1024]{1,0:T(8,128)(2,1)S(1)}, bf16[32,1024]{1,0:T(8,128)(2,1)S(1)}, u32[]{:S(2)}, u32[]{:S(2)}) collective-permute-start(bf16[32,1024]{1,0:T(8,128)(2,1)S(1)} %get-tuple-element.58), channel_id=1, source_target_pairs={{0,16},{16,0},{1,17},{17,1},{2,18},{18,2},{3,19},{19,3},{4,20},{20... | collective-permute-start | bytes 196616 | tf_op jit(solution)/shard_map/ppermute | solution.py:363

commit v8 on v7

--- a/solution.py
+++ b/solution.py
@@ -399,7 +399,7 @@
     blocks[8], blocks[12], early = gate[:3]
     for d in (8, 12):
         blocks[d | 1] = flip(blocks[d], "vox", 1)
-    blocks[10] = after(blocks[10], blocks[5], blocks[3])
+    blocks[10] = after(blocks[10], blocks[7])
     blocks[11] = flip(blocks[10], "vox", 1)
     blocks[14] = after(blocks[14], blocks[13])
     blocks[15] = flip(blocks[14], "vox", 1)

time: 41.4 us -> 41.4 us (level)
  no operation moved by 1% of the time
where the time goes in v8:
time: 41.4 us; the launch traced here: 41.1 us
  starting transfers between devices  21.2 us (51%)
  Pallas kernels  11.1 us (27%)
  waiting for transfers between devices  4.08 us (10%)
  local copies, waits for them, and re-layouts  2.57 us (6%)
  other arithmetic  1.33 us (3%)
  between operations  0.87 us (2%)
    ppermute x20, starting transfers between devices, flip(): return lax.ppermute(block, axis, [(i, i ^ mask) for i in range(count)])  20.6 us
    pallas_call x3, Pallas kernels, image(): pl.pallas_call(functools.partial(image_kernel, swap, len(pieces), start),...  4.38 us
    ppermute x20, waiting for transfers between devices, flip(): return lax.ppermute(block, axis, [(i, i ^ mask) for i in range(count)])  4.07 us
    pallas_call x3, Pallas kernels, add_part(): pl.pallas_call(functools.partial(add_kernel, start), out_shape=jax.ShapeD...  2.08 us
    unnamed x4, local copies, waits for them, and re-layouts  1.83 us
    pallas_call x1, Pallas kernels, correlate(): pl.pallas_call(corr_kernel, out_shape=jax.ShapeDtypeStruct((pitch * slice...  1.78 us
    transpose x1, other arithmetic, shards(): windowed = jnp.transpose(windowed, (1, 0, 2))  1.29 us
    pallas_call x4, Pallas kernels, split(): pl.pallas_call(split_kernel, out_shape=[jax.ShapeDtypeStruct((rows, colum...  1.25 us
  transfers between devices with their start and end apart: 21, of which 7 were waited for; matrix products, arithmetic and copies ran while one was open for 3% of the time, Pallas kernels for 19%

profile of v8, /device:TPU:0, one launch (start us, length us, event | category | flops | bytes accessed | tf_op | source)
XLA Modules:
  0.0 41.1 jit_solution(14215420436185449675)
XLA Ops:
  0.7 0.7 %dynamic-slice_bitcast_fusion = bf16[2,4096]{1,0:T(2,128)(2,1)S(1)} fusion(bf16[28,2,4096]{2,1,0:T(2,128)(2,1)} %param.5, s32[]{:T(128)S(6)} %select_n.50), kind=kLoop, calls=%fused_computation.3 | loop fusion | bytes 32772 | tf_op jit(solution)/shard_map/jit(dynamic_index_in_dim)/squeeze | solution.py:421
  1.4 3.0 %collective-permute-start = (bf16[2,4096]{1,0:T(2,128)(2,1)S(1)}, bf16[2,4096]{1,0:T(2,128)(2,1)S(1)}, u32[]{:S(2)}, u32[]{:S(2)}) collective-permute-start(bf16[2,4096]{1,0:T(2,128)(2,1)S(1)} %dynamic-slice_bitcast_fusion), channel_id=1, source_target_pairs={{0,16},{16,0},{1,17},{17,1},{2,18},{18,2},{3,19},{19,3},{4,20},{20... | collective-permute-start | bytes 49160 | tf_op jit(solution)/shard_map/ppermute | solution.py:363
  4.4 1.3 %fusion.win_ref = bf16[2,28,4096]{2,1,0:T(8,128)(2,1)S(1)} fusion(bf16[28,2,4096]{2,1,0:T(2,128)(2,1)} %param.5, f32[4096]{0:T(1024)} %constant.48.clone), kind=kLoop, calls=%fused_computation.1 | loop fusion | flops 688128 | bytes 933888 | tf_op jit(solution)/shard_map/transpose | solution.py:438
  5.7 0.4 collective-permute-done
  6.2 0.7 %collective-permute-start.2 = (bf16[2,128]{1,0:T(2,128)(2,1)S(1)}, bf16[2,128]{1,0:T(2,128)(2,1)S(1)}, u32[]{:S(2)}, u32[]{:S(2)}) collective-permute-start(bf16[2,128]{1,0:T(2,128)(2,1)S(1)} %get-tuple-element.63), channel_id=1, source_target_pairs={{1,2},{3,4},{5,6},{7,8},{9,10},{11,12},{13,14},{2,1},{4,3},{6,5},{... | collective-permute-start | bytes 1544 | tf_op jit(solution)/shard_map/ppermute | solution.py:372
  6.8 3.5 %collective-permute-start.1 = (bf16[2,128]{1,0:T(2,128)(2,1)S(1)}, bf16[2,128]{1,0:T(2,128)(2,1)S(1)}, u32[]{:S(2)}, u32[]{:S(2)}) collective-permute-start(bf16[2,128]{1,0:T(2,128)(2,1)S(1)} %get-tuple-element.64), channel_id=1, source_target_pairs={{0,1},{1,0},{2,3},{3,2},{4,5},{5,4},{6,7},{7,6},{8,9},{9,8},{10,11... | collective-permute-start | bytes 1544 | tf_op jit(solution)/shard_map/ppermute | solution.py:363
  10.3 1.8 %shard_map.55.part_ref = f32[128,256]{1,0:T(8,128)S(1)} custom-call(bf16[2,28,4096]{2,1,0:T(8,128)(2,1)S(1)} %fusion.win_ref, bf16[2,4096]{1,0:T(2,128)(2,1)S(1)} %broadcast_select_fusion.ref_ref.body_ref), custom_call_target="tpu_custom_call" | custom-call | flops 117440512 | bytes 458752 | tf_op jit(solution)/shard_map/pallas_call | solution.py:150
  12.1 0.6 %shard_map.56.refs_0_ = bf16[4,7168]{1,0:T(4,128)(2,1)S(1)} custom-call(s32[1]{0:T(128)S(6)} %copy.12.ref_ref, bf16[2,28,4096]{2,1,0:T(8,128)(2,1)S(1)} %fusion.win_ref, bf16[2,4096]{1,0:T(2,128)(2,1)S(1)} %broadcast_select_fusion.ref_ref.body_ref, bf16[2,128]{1,0:T(2,128)(2,1)S(1)} %get-tuple-element.66.low_ref, ...), custom_call_target="tpu_custom_call" | custom-call | flops 14680064 | bytes 28672 | tf_op jit(solution)/shard_map/pallas_call | solution.py:166
  12.8 2.0 %collective-permute-start.4 = (bf16[4,7168]{1,0:T(4,128)(2,1)S(1)}, bf16[4,7168]{1,0:T(4,128)(2,1)S(1)}, u32[]{:S(2)}, u32[]{:S(2)}) collective-permute-start(bf16[4,7168]{1,0:T(4,128)(2,1)S(1)} %shard_map.56.refs_0_), channel_id=1, source_target_pairs={{0,4},{1,5},{2,6},{3,7},{4,0},{5,1},{6,2},{7,3},{8,12},{9,13},{10,... | collective-permute-start | bytes 172040 | tf_op jit(solution)/shard_map/ppermute | solution.py:363
  14.7 2.6 %collective-permute-start.3 = (bf16[4,7168]{1,0:T(4,128)(2,1)S(1)}, bf16[4,7168]{1,0:T(4,128)(2,1)S(1)}, u32[]{:S(2)}, u32[]{:S(2)}) collective-permute-start(bf16[4,7168]{1,0:T(4,128)(2,1)S(1)} %shard_map.56.refs_0_), channel_id=1, source_target_pairs={{0,8},{1,9},{2,10},{3,11},{4,12},{5,13},{6,14},{7,15},{8,0},{9,1},... | collective-permute-start | bytes 172040 | tf_op jit(solution)/shard_map/ppermute | solution.py:363
  17.3 1.4 %collective-permute-start.6 = (bf16[4,7168]{1,0:T(4,128)(2,1)S(1)}, bf16[4,7168]{1,0:T(4,128)(2,1)S(1)}, u32[]{:S(2)}, u32[]{:S(2)}) collective-permute-start(bf16[4,7168]{1,0:T(4,128)(2,1)S(1)} %shard_map.56.refs_0_), channel_id=1, source_target_pairs={{0,2},{1,3},{2,0},{3,1},{4,6},{5,7},{6,4},{7,5},{8,10},{9,11},{10,... | collective-permute-start | bytes 172040 | tf_op jit(solution)/shard_map/ppermute | solution.py:363
  18.7 0.6 %collective-permute-start.7 = (bf16[4,7168]{1,0:T(4,128)(2,1)S(1)}, bf16[4,7168]{1,0:T(4,128)(2,1)S(1)}, u32[]{:S(2)}, u32[]{:S(2)}) collective-permute-start(bf16[4,7168]{1,0:T(4,128)(2,1)S(1)} %collective-permute-done.4.refs_1_), channel_id=1, source_target_pairs={{0,2},{1,3},{2,0},{3,1},{4,6},{5,7},{6,4},{7,5},{8,10},{9,11},{10,... | collective-permute-start | bytes 172040 | tf_op jit(solution)/shard_map/ppermute | solution.py:363
  19.4 1.2 %copy-done = s32[56,4096]{1,0:T(8,128)S(1)} copy-done((s32[56,4096]{1,0:T(8,128)S(1)}, s32[56,4096]{1,0:T(8,128)}, u32[]{:S(2)}) %copy-start) | copy-done | bytes 917528
  20.5 0.7 %copy-done.1 = s32[56]{0:T(128)S(1)} copy-done((s32[56]{0:T(128)S(1)}, s32[56]{0:T(128)}, u32[]{:S(2)}) %copy-start.1) | copy-done | bytes 248
  21.2 1.0 %shard_map.57.target_ref = s8[28,32,4096]{2,1,0:T(32,128)(4,1)S(1)} custom-call(s32[56]{0:T(128)S(1)} %copy-done.1, s32[56,4096]{1,0:T(8,128)S(1)} %copy-done), custom_call_target="tpu_custom_call" | custom-call | flops 3670016 | bytes 4128768 | tf_op jit(solution)/shard_map/pallas_call | solution.py:240
  22.2 1.5 %collective-permute-start.12 = (bf16[4,7168]{1,0:T(4,128)(2,1)S(1)}, bf16[4,7168]{1,0:T(4,128)(2,1)S(1)}, u32[]{:S(2)}, u32[]{:S(2)}) collective-permute-start(bf16[4,7168]{1,0:T(4,128)(2,1)S(1)} %collective-permute-done.3.refs_2_), channel_id=1, source_target_pairs={{0,2},{1,3},{2,0},{3,1},{4,6},{5,7},{6,4},{7,5},{8,10},{9,11},{10,... | collective-permute-start | bytes 172040 | tf_op jit(solution)/shard_map/ppermute | solution.py:363
  23.7 0.6 %collective-permute-start.14 = (bf16[4,7168]{1,0:T(4,128)(2,1)S(1)}, bf16[4,7168]{1,0:T(4,128)(2,1)S(1)}, u32[]{:S(2)}, u32[]{:S(2)}) collective-permute-start(bf16[4,7168]{1,0:T(4,128)(2,1)S(1)} %collective-permute-done.8.refs_3_), channel_id=1, source_target_pairs={{0,2},{1,3},{2,0},{3,1},{4,6},{5,7},{6,4},{7,5},{8,10},{9,11},{10,... | collective-permute-start | bytes 172040 | tf_op jit(solution)/shard_map/ppermute | solution.py:363
  24.6 0.6 %collective-permute-start.11 = (bf16[4,7168]{1,0:T(4,128)(2,1)S(1)}, bf16[4,7168]{1,0:T(4,128)(2,1)S(1)}, u32[]{:S(2)}, u32[]{:S(2)}) collective-permute-start(bf16[4,7168]{1,0:T(4,128)(2,1)S(1)} %collective-permute-done.8.refs_3_), channel_id=1, source_target_pairs={{0,1},{1,0},{2,3},{3,2},{4,5},{5,4},{6,7},{7,6},{8,9},{9,8},{10,11... | collective-permute-start | bytes 172040 | tf_op jit(solution)/shard_map/ppermute | solution.py:363
  25.3 1.7 %collective-permute-done.12.refs_2_ = bf16[4,7168]{1,0:T(4,128)(2,1)S(1)} collective-permute-done((bf16[4,7168]{1,0:T(4,128)(2,1)S(1)}, bf16[4,7168]{1,0:T(4,128)(2,1)S(1)}, u32[]{:S(2)}, u32[]{:S(2)}) %collective-permute-start.12) | collective-permute-done | bytes 57376 | tf_op jit(solution)/shard_map/ppermute | solution.py:363
  27.0 0.5 %collective-permute-start.15 = (bf16[4,7168]{1,0:T(4,128)(2,1)S(1)}, bf16[4,7168]{1,0:T(4,128)(2,1)S(1)}, u32[]{:S(2)}, u32[]{:S(2)}) collective-permute-start(bf16[4,7168]{1,0:T(4,128)(2,1)S(1)} %collective-permute-done.6.refs_0_), channel_id=1, source_target_pairs={{0,1},{1,0},{2,3},{3,2},{4,5},{5,4},{6,7},{7,6},{8,9},{9,8},{10,11... | collective-permute-start | bytes 172040 | tf_op jit(solution)/shard_map/ppermute | solution.py:363
  27.9 0.5 %collective-permute-start.17 = (bf16[4,7168]{1,0:T(4,128)(2,1)S(1)}, bf16[4,7168]{1,0:T(4,128)(2,1)S(1)}, u32[]{:S(2)}, u32[]{:S(2)}) collective-permute-start(bf16[4,7168]{1,0:T(4,128)(2,1)S(1)} %collective-permute-done.14.refs_3_), channel_id=1, source_target_pairs={{0,1},{1,0},{2,3},{3,2},{4,5},{5,4},{6,7},{7,6},{8,9},{9,8},{10,11... | collective-permute-start | bytes 172040 | tf_op jit(solution)/shard_map/ppermute | solution.py:363
  29.6 1.9 %shard_map.64 = (f32[32,1792]{1,0:T(8,128)S(1)}, bf16[32,1792]{1,0:T(8,128)(2,1)S(1)}) custom-call(s8[28,32,4096]{2,1,0:T(32,128)(4,1)S(1)} %shard_map.57.target_ref, f8e4m3fn[32,7168]{1,0:T(32,128)(4,1)S(1)} %get-tuple-element.43.refs_0_, f8e4m3fn[32,7168]{1,0:T(32,128)(4,1)S(1)} %get-tuple-element.46.refs_1_, ...), custom_call_target="tpu_custom_call" | custom-call | flops 458752 | bytes 64 | tf_op jit(solution)/shard_map/pallas_call | solution.py:319
  31.5 1.6 %collective-permute-start.20 = (bf16[32,1792]{1,0:T(8,128)(2,1)S(1)}, bf16[32,1792]{1,0:T(8,128)(2,1)S(1)}, u32[]{:S(2)}, u32[]{:S(2)}) collective-permute-start(bf16[32,1792]{1,0:T(8,128)(2,1)S(1)} %get-tuple-element.62), channel_id=1, source_target_pairs={{0,16},{16,0},{1,17},{17,1},{2,18},{18,2},{3,19},{19,3},{4,20},{20... | collective-permute-start | bytes 344072 | tf_op jit(solution)/shard_map/ppermute | solution.py:363
  33.0 1.4 %shard_map.63 = (f32[32,1280]{1,0:T(8,128)S(1)}, bf16[32,1280]{1,0:T(8,128)(2,1)S(1)}) custom-call(s8[28,32,4096]{2,1,0:T(32,128)(4,1)S(1)} %shard_map.57.target_ref, f8e4m3fn[32,7168]{1,0:T(32,128)(4,1)S(1)} %get-tuple-element.43.refs_0_, f8e4m3fn[32,7168]{1,0:T(32,128)(4,1)S(1)} %get-tuple-element.46.refs_1_, ...), custom_call_target="tpu_custom_call" | custom-call | flops 327680 | bytes 64 | tf_op jit(solution)/shard_map/pallas_call | solution.py:319
  34.4 0.6 %collective-permute-start.19 = (bf16[32,1280]{1,0:T(8,128)(2,1)S(1)}, bf16[32,1280]{1,0:T(8,128)(2,1)S(1)}, u32[]{:S(2)}, u32[]{:S(2)}) collective-permute-start(bf16[32,1280]{1,0:T(8,128)(2,1)S(1)} %get-tuple-element.60), channel_id=1, source_target_pairs={{0,16},{16,0},{1,17},{17,1},{2,18},{18,2},{3,19},{19,3},{4,20},{20... | collective-permute-start | bytes 245768 | tf_op jit(solution)/shard_map/ppermute | solution.py:363
  35.0 1.1 %shard_map.62 = (f32[32,1024]{1,0:T(8,128)S(1)}, bf16[32,1024]{1,0:T(8,128)(2,1)S(1)}) custom-call(s8[28,32,4096]{2,1,0:T(32,128)(4,1)S(1)} %shard_map.57.target_ref, f8e4m3fn[32,7168]{1,0:T(32,128)(4,1)S(1)} %get-tuple-element.43.refs_0_, f8e4m3fn[32,7168]{1,0:T(32,128)(4,1)S(1)} %get-tuple-element.46.refs_1_, ...), custom_call_target="tpu_custom_call" | custom-call | flops 262144 | bytes 64 | tf_op jit(solution)/shard_map/pallas_call | solution.py:319
  36.1 1.6 %collective-permute-start.18 = (bf16[32,1024]{1,0:T(8,128)(2,1)S(1)}, bf16[32,1024]{1,0:T(8,128)(2,1)S(1)}, u32[]{:S(2)}, u32[]{:S(2)}) collective-permute-start(bf16[32,1024]{1,0:T(8,128)(2,1)S(1)} %get-tuple-element.58), channel_id=1, source_target_pairs={{0,16},{16,0},{1,17},{17,1},{2,18},{18,2},{3,19},{19,3},{4,20},{20... | collective-permute-start | bytes 196616 | tf_op jit(solution)/shard_map/ppermute | solution.py:363
  37.7 0.7 %shard_map.65.refs_0_ = f32[32,4096]{1,0:T(8,128)} custom-call(f32[32,1792]{1,0:T(8,128)S(1)} %get-tuple-element.61.kept_ref, bf16[32,1792]{1,0:T(8,128)(2,1)S(1)} %collective-permute-done.20.came_ref), custom_call_target="tpu_custom_call" | custom-call | flops 57344 | bytes 229376 | tf_op jit(solution)/shard_map/pallas_call | solution.py:347
  38.4 0.9 %collective-permute-done.19.came_ref = bf16[32,1280]{1,0:T(8,128)(2,1)S(1)} collective-permute-done((bf16[32,1280]{1,0:T(8,128)(2,1)S(1)}, bf16[32,1280]{1,0:T(8,128)(2,1)S(1)}, u32[]{:S(2)}, u32[]{:S(2)}) %collective-permute-start.19) | collective-permute-done | bytes 81952 | tf_op jit(solution)/shard_map/ppermute | solution.py:363
  39.3 0.7 %shard_map.66.refs_0_ = f32[32,4096]{1,0:T(8,128)} custom-call(f32[32,1280]{1,0:T(8,128)S(1)} %get-tuple-element.59.kept_ref, bf16[32,1280]{1,0:T(8,128)(2,1)S(1)} %collective-permute-done.19.came_ref, f32[32,4096]{1,0:T(8,128)} %shard_map.65.refs_0_), custom_call_target="tpu_custom_call", output_to_operand_aliasing={{}: (2, {})} | custom-call | flops 40960 | bytes 163840 | tf_op jit(solution)/shard_map/pallas_call | solution.py:347
  40.0 0.5 %collective-permute-done.18.came_ref = bf16[32,1024]{1,0:T(8,128)(2,1)S(1)} collective-permute-done((bf16[32,1024]{1,0:T(8,128)(2,1)S(1)}, bf16[32,1024]{1,0:T(8,128)(2,1)S(1)}, u32[]{:S(2)}, u32[]{:S(2)}) %collective-permute-start.18) | collective-permute-done | bytes 65568 | tf_op jit(solution)/shard_map/ppermute | solution.py:363
  40.5 0.7 %shard_map.67 = f32[32,4096]{1,0:T(8,128)} custom-call(f32[32,1024]{1,0:T(8,128)S(1)} %get-tuple-element.57.kept_ref, bf16[32,1024]{1,0:T(8,128)(2,1)S(1)} %collective-permute-done.18.came_ref, f32[32,4096]{1,0:T(8,128)} %shard_map.66.refs_0_), custom_call_target="tpu_custom_call", output_to_operand_aliasing={{}: (2, {})} | custom-call | flops 32768 | bytes 131072 | tf_op jit(solution)/shard_map/pallas_call | solution.py:347
  (32 shorter events, 2.0 us)
Async XLA Ops:
  1.4 4.7 %collective-permute-start = (bf16[2,4096]{1,0:T(2,128)(2,1)S(1)}, bf16[2,4096]{1,0:T(2,128)(2,1)S(1)}, u32[]{:S(2)}, u32[]{:S(2)}) collective-permute-start(bf16[2,4096]{1,0:T(2,128)(2,1)S(1)} %dynamic-slice_bitcast_fusion), channel_id=1, source_target_pairs={{0,16},{16,0},{1,17},{17,1},{2,18},{18,2},{3,19},{19,3},{4,20},{20... | collective-permute-start | bytes 49160 | tf_op jit(solution)/shard_map/ppermute | solution.py:363
  6.2 5.9 %collective-permute-start.2 = (bf16[2,128]{1,0:T(2,128)(2,1)S(1)}, bf16[2,128]{1,0:T(2,128)(2,1)S(1)}, u32[]{:S(2)}, u32[]{:S(2)}) collective-permute-start(bf16[2,128]{1,0:T(2,128)(2,1)S(1)} %get-tuple-element.63), channel_id=1, source_target_pairs={{1,2},{3,4},{5,6},{7,8},{9,10},{11,12},{13,14},{2,1},{4,3},{6,5},{... | collective-permute-start | bytes 1544 | tf_op jit(solution)/shard_map/ppermute | solution.py:372
  6.8 5.3 %collective-permute-start.1 = (bf16[2,128]{1,0:T(2,128)(2,1)S(1)}, bf16[2,128]{1,0:T(2,128)(2,1)S(1)}, u32[]{:S(2)}, u32[]{:S(2)}) collective-permute-start(bf16[2,128]{1,0:T(2,128)(2,1)S(1)} %get-tuple-element.64), channel_id=1, source_target_pairs={{0,1},{1,0},{2,3},{3,2},{4,5},{5,4},{6,7},{7,6},{8,9},{9,8},{10,11... | collective-permute-start | bytes 1544 | tf_op jit(solution)/shard_map/ppermute | solution.py:363
  12.8 6.0 %collective-permute-start.4 = (bf16[4,7168]{1,0:T(4,128)(2,1)S(1)}, bf16[4,7168]{1,0:T(4,128)(2,1)S(1)}, u32[]{:S(2)}, u32[]{:S(2)}) collective-permute-start(bf16[4,7168]{1,0:T(4,128)(2,1)S(1)} %shard_map.56.refs_0_), channel_id=1, source_target_pairs={{0,4},{1,5},{2,6},{3,7},{4,0},{5,1},{6,2},{7,3},{8,12},{9,13},{10,... | collective-permute-start | bytes 172040 | tf_op jit(solution)/shard_map/ppermute | solution.py:363
  14.7 7.5 %collective-permute-start.3 = (bf16[4,7168]{1,0:T(4,128)(2,1)S(1)}, bf16[4,7168]{1,0:T(4,128)(2,1)S(1)}, u32[]{:S(2)}, u32[]{:S(2)}) collective-permute-start(bf16[4,7168]{1,0:T(4,128)(2,1)S(1)} %shard_map.56.refs_0_), channel_id=1, source_target_pairs={{0,8},{1,9},{2,10},{3,11},{4,12},{5,13},{6,14},{7,15},{8,0},{9,1},... | collective-permute-start | bytes 172040 | tf_op jit(solution)/shard_map/ppermute | solution.py:363
  17.3 4.9 %collective-permute-start.5 = (bf16[4,7168]{1,0:T(4,128)(2,1)S(1)}, bf16[4,7168]{1,0:T(4,128)(2,1)S(1)}, u32[]{:S(2)}, u32[]{:S(2)}) collective-permute-start(bf16[4,7168]{1,0:T(4,128)(2,1)S(1)} %shard_map.56.refs_0_), channel_id=1, source_target_pairs={{0,1},{1,0},{2,3},{3,2},{4,5},{5,4},{6,7},{7,6},{8,9},{9,8},{10,11... | collective-permute-start | bytes 172040 | tf_op jit(solution)/shard_map/ppermute | solution.py:363
  17.3 6.4 %collective-permute-start.8 = (bf16[4,7168]{1,0:T(4,128)(2,1)S(1)}, bf16[4,7168]{1,0:T(4,128)(2,1)S(1)}, u32[]{:S(2)}, u32[]{:S(2)}) collective-permute-start(bf16[4,7168]{1,0:T(4,128)(2,1)S(1)} %shard_map.56.refs_0_), channel_id=1, source_target_pairs={{0,12},{1,13},{2,14},{3,15},{4,8},{5,9},{6,10},{7,11},{8,4},{9,5},... | collective-permute-start | bytes 172040 | tf_op jit(solution)/shard_map/ppermute | solution.py:363
  17.3 7.0 %collective-permute-start.6 = (bf16[4,7168]{1,0:T(4,128)(2,1)S(1)}, bf16[4,7168]{1,0:T(4,128)(2,1)S(1)}, u32[]{:S(2)}, u32[]{:S(2)}) collective-permute-start(bf16[4,7168]{1,0:T(4,128)(2,1)S(1)} %shard_map.56.refs_0_), channel_id=1, source_target_pairs={{0,2},{1,3},{2,0},{3,1},{4,6},{5,7},{6,4},{7,5},{8,10},{9,11},{10,... | collective-permute-start | bytes 172040 | tf_op jit(solution)/shard_map/ppermute | solution.py:363
  18.7 5.6 %collective-permute-start.7 = (bf16[4,7168]{1,0:T(4,128)(2,1)S(1)}, bf16[4,7168]{1,0:T(4,128)(2,1)S(1)}, u32[]{:S(2)}, u32[]{:S(2)}) collective-permute-start(bf16[4,7168]{1,0:T(4,128)(2,1)S(1)} %collective-permute-done.4.refs_1_), channel_id=1, source_target_pairs={{0,2},{1,3},{2,0},{3,1},{4,6},{5,7},{6,4},{7,5},{8,10},{9,11},{10,... | collective-permute-start | bytes 172040 | tf_op jit(solution)/shard_map/ppermute | solution.py:363
  19.4 1.2 %copy-start = (s32[56,4096]{1,0:T(8,128)S(1)}, s32[56,4096]{1,0:T(8,128)}, u32[]{:S(2)}) copy-start(s32[56,4096]{1,0:T(8,128)} %delay_ref) | copy-start | bytes 2752516
  20.5 0.7 %copy-start.1 = (s32[56]{0:T(128)S(1)}, s32[56]{0:T(128)}, u32[]{:S(2)}) copy-start(s32[56]{0:T(128)} %offset_ref.1) | copy-start | bytes 676
  22.2 4.8 %collective-permute-start.12 = (bf16[4,7168]{1,0:T(4,128)(2,1)S(1)}, bf16[4,7168]{1,0:T(4,128)(2,1)S(1)}, u32[]{:S(2)}, u32[]{:S(2)}) collective-permute-start(bf16[4,7168]{1,0:T(4,128)(2,1)S(1)} %collective-permute-done.3.refs_2_), channel_id=1, source_target_pairs={{0,2},{1,3},{2,0},{3,1},{4,6},{5,7},{6,4},{7,5},{8,10},{9,11},{10,... | collective-permute-start | bytes 172040 | tf_op jit(solution)/shard_map/ppermute | solution.py:363
  23.7 4.2 %collective-permute-start.14 = (bf16[4,7168]{1,0:T(4,128)(2,1)S(1)}, bf16[4,7168]{1,0:T(4,128)(2,1)S(1)}, u32[]{:S(2)}, u32[]{:S(2)}) collective-permute-start(bf16[4,7168]{1,0:T(4,128)(2,1)S(1)} %collective-permute-done.8.refs_3_), channel_id=1, source_target_pairs={{0,2},{1,3},{2,0},{3,1},{4,6},{5,7},{6,4},{7,5},{8,10},{9,11},{10,... | collective-permute-start | bytes 172040 | tf_op jit(solution)/shard_map/ppermute | solution.py:363
  24.3 2.7 %collective-permute-start.13 = (bf16[4,7168]{1,0:T(4,128)(2,1)S(1)}, bf16[4,7168]{1,0:T(4,128)(2,1)S(1)}, u32[]{:S(2)}, u32[]{:S(2)}) collective-permute-start(bf16[4,7168]{1,0:T(4,128)(2,1)S(1)} %collective-permute-done.7.refs_1_), channel_id=1, source_target_pairs={{0,1},{1,0},{2,3},{3,2},{4,5},{5,4},{6,7},{7,6},{8,9},{9,8},{10,11... | collective-permute-start | bytes 172040 | tf_op jit(solution)/shard_map/ppermute | solution.py:363
  24.6 3.2 %collective-permute-start.11 = (bf16[4,7168]{1,0:T(4,128)(2,1)S(1)}, bf16[4,7168]{1,0:T(4,128)(2,1)S(1)}, u32[]{:S(2)}, u32[]{:S(2)}) collective-permute-start(bf16[4,7168]{1,0:T(4,128)(2,1)S(1)} %collective-permute-done.8.refs_3_), channel_id=1, source_target_pairs={{0,1},{1,0},{2,3},{3,2},{4,5},{5,4},{6,7},{7,6},{8,9},{9,8},{10,11... | collective-permute-start | bytes 172040 | tf_op jit(solution)/shard_map/ppermute | solution.py:363
  25.2 3.5 %collective-permute-start.9 = (bf16[4,7168]{1,0:T(4,128)(2,1)S(1)}, bf16[4,7168]{1,0:T(4,128)(2,1)S(1)}, u32[]{:S(2)}, u32[]{:S(2)}) collective-permute-start(bf16[4,7168]{1,0:T(4,128)(2,1)S(1)} %collective-permute-done.4.refs_1_), channel_id=1, source_target_pairs={{0,1},{1,0},{2,3},{3,2},{4,5},{5,4},{6,7},{7,6},{8,9},{9,8},{10,11... | collective-permute-start | bytes 172040 | tf_op jit(solution)/shard_map/ppermute | solution.py:363
  27.0 1.7 %collective-permute-start.10 = (bf16[4,7168]{1,0:T(4,128)(2,1)S(1)}, bf16[4,7168]{1,0:T(4,128)(2,1)S(1)}, u32[]{:S(2)}, u32[]{:S(2)}) collective-permute-start(bf16[4,7168]{1,0:T(4,128)(2,1)S(1)} %collective-permute-done.3.refs_2_), channel_id=1, source_target_pairs={{0,1},{1,0},{2,3},{3,2},{4,5},{5,4},{6,7},{7,6},{8,9},{9,8},{10,11... | collective-permute-start | bytes 172040 | tf_op jit(solution)/shard_map/ppermute | solution.py:363
  27.0 2.0 %collective-permute-start.15 = (bf16[4,7168]{1,0:T(4,128)(2,1)S(1)}, bf16[4,7168]{1,0:T(4,128)(2,1)S(1)}, u32[]{:S(2)}, u32[]{:S(2)}) collective-permute-start(bf16[4,7168]{1,0:T(4,128)(2,1)S(1)} %collective-permute-done.6.refs_0_), channel_id=1, source_target_pairs={{0,1},{1,0},{2,3},{3,2},{4,5},{5,4},{6,7},{7,6},{8,9},{9,8},{10,11... | collective-permute-start | bytes 172040 | tf_op jit(solution)/shard_map/ppermute | solution.py:363
  27.9 1.2 %collective-permute-start.16 = (bf16[4,7168]{1,0:T(4,128)(2,1)S(1)}, bf16[4,7168]{1,0:T(4,128)(2,1)S(1)}, u32[]{:S(2)}, u32[]{:S(2)}) collective-permute-start(bf16[4,7168]{1,0:T(4,128)(2,1)S(1)} %collective-permute-done.12.refs_2_), channel_id=1, source_target_pairs={{0,1},{1,0},{2,3},{3,2},{4,5},{5,4},{6,7},{7,6},{8,9},{9,8},{10,11... | collective-permute-start | bytes 172040 | tf_op jit(solution)/shard_map/ppermute | solution.py:363
  27.9 1.4 %collective-permute-start.17 = (bf16[4,7168]{1,0:T(4,128)(2,1)S(1)}, bf16[4,7168]{1,0:T(4,128)(2,1)S(1)}, u32[]{:S(2)}, u32[]{:S(2)}) collective-permute-start(bf16[4,7168]{1,0:T(4,128)(2,1)S(1)} %collective-permute-done.14.refs_3_), channel_id=1, source_target_pairs={{0,1},{1,0},{2,3},{3,2},{4,5},{5,4},{6,7},{7,6},{8,9},{9,8},{10,11... | collective-permute-start | bytes 172040 | tf_op jit(solution)/shard_map/ppermute | solution.py:363
  31.5 6.2 %collective-permute-start.20 = (bf16[32,1792]{1,0:T(8,128)(2,1)S(1)}, bf16[32,1792]{1,0:T(8,128)(2,1)S(1)}, u32[]{:S(2)}, u32[]{:S(2)}) collective-permute-start(bf16[32,1792]{1,0:T(8,128)(2,1)S(1)} %get-tuple-element.62), channel_id=1, source_target_pairs={{0,16},{16,0},{1,17},{17,1},{2,18},{18,2},{3,19},{19,3},{4,20},{20... | collective-permute-start | bytes 344072 | tf_op jit(solution)/shard_map/ppermute | solution.py:363
  34.4 4.9 %collective-permute-start.19 = (bf16[32,1280]{1,0:T(8,128)(2,1)S(1)}, bf16[32,1280]{1,0:T(8,128)(2,1)S(1)}, u32[]{:S(2)}, u32[]{:S(2)}) collective-permute-start(bf16[32,1280]{1,0:T(8,128)(2,1)S(1)} %get-tuple-element.60), channel_id=1, source_target_pairs={{0,16},{16,0},{1,17},{17,1},{2,18},{18,2},{3,19},{19,3},{4,20},{20... | collective-permute-start | bytes 245768 | tf_op jit(solution)/shard_map/ppermute | solution.py:363
  36.1 4.3 %collective-permute-start.18 = (bf16[32,1024]{1,0:T(8,128)(2,1)S(1)}, bf16[32,1024]{1,0:T(8,128)(2,1)S(1)}, u32[]{:S(2)}, u32[]{:S(2)}) collective-permute-start(bf16[32,1024]{1,0:T(8,128)(2,1)S(1)} %get-tuple-element.58), channel_id=1, source_target_pairs={{0,16},{16,0},{1,17},{17,1},{2,18},{18,2},{3,19},{19,3},{4,20},{20... | collective-permute-start | bytes 196616 | tf_op jit(solution)/shard_map/ppermute | solution.py:363
